TPU v7x, 128 devices: a whole 4x4x4 slice. The times are simulated.
128 devices in a mesh: req: 16 (over z, x), head: 8 (over y, core).
Axes of the slice: x: 4, y: 4, z: 4, core: 2. Of those that a mesh axis runs over, the one named last changes fastest.
Arguments:
- residual: bfloat16 [256, 4096], P(None, 'req'), may hold values from -80 to 80
- lengths: int32 [256], P('req'), may hold values from 0 to 32768, as said below
- ssm_state: float32 [256, 128, 64, 128], P('req', 'head'), may hold values from -6 to 6
- tail_mix: float32 [256, 3, 8192], P('req', None, 'head'), may hold values from -6 to 6
- tail_group: float32 [256, 3, 2, 1024], P('req', None, None, 'head'), may hold values from -6 to 6
- norm_first: float32 [4096], P('req'), may hold values from 0.1 to 1.9
- mix_weight: bfloat16 [4096, 2, 8192], P('req', None, 'head'), may hold values from -0.09375 to 0.09375
- group_weight: bfloat16 [4096, 2, 1024], P('req', None, 'head'), may hold values from -0.09375 to 0.09375
- step_weight: bfloat16 [4096, 128], P('req', 'head'), may hold values from -0.09375 to 0.09375
- conv_mix: float32 [4, 8192], P(None, 'head'), may hold values from -3 to 3
- conv_group: float32 [4, 2, 1024], P(None, None, 'head'), may hold values from -3 to 3
- bias_mix: float32 [8192], P('head'), may hold values from -3 to 3
- bias_group: float32 [2, 1024], P(None, 'head'), may hold values from -3 to 3
- step_bias: float32 [128], P('head'), may hold values from -2 to 1
- decay_log: float32 [128], P('head'), may hold values from -1 to 2
- skip_gain: float32 [128], P('head'), may hold values from 0.5 to 2
- gate_gain: float32 [8192], P('head'), may hold values from 0.1 to 1.9
- out_weight: bfloat16 [8192, 4096], P('head', 'req'), may hold values from -0.0625 to 0.0625
- norm_second: float32 [4096], P('req'), may hold values from 0.1 to 1.9
- up_weight: bfloat16 [4096, 21504], P('req', 'head'), may hold values from -0.09375 to 0.09375
- down_weight: bfloat16 [21504, 4096], P('head', 'req'), may hold values from -0.0390625 to 0.0390625
Outputs:
- residual_out: bfloat16 [256, 4096], P(None, 'req')
- state_out: float32 [256, 128, 64, 128], P('req', 'head')
- tail_mix_out: float32 [256, 3, 8192], P('req', None, 'head')
- tail_group_out: float32 [256, 3, 2, 1024], P('req', None, None, 'head')
Inputs may be any that keep to these rules, and one draw needn't show every extreme that they name: `lengths`: 0 marks a fresh request.
All inputs are finite; a program needn't handle non-finite values.
Results may differ from a plain program's by a relative error of at most 0.0056.
Values may be sent and summed in bfloat16 or wider, within the bound.
No kernel may reach another device: no remote copies, remote signals or barrier semaphores. Data moves between devices by JAX's collectives and lax.ppermute only.
A program may use at most 128 MiB of HBM per device.

v0:
```python
import jax
import jax.numpy as jnp
from jax import lax
from jax.sharding import Mesh
from jax.sharding import PartitionSpec as P

REQ = ("req_0", "req_1")


eps = 1e-05


def over_axes(value, axes):
    for axis in axes:
        value = lax.psum(value, axis)
    return value


def total_of_pieces(value, axis):
    return lax.all_gather(value, axis).sum(0)


def split_up(value, dim, peers):
    shape = value.shape
    pieces = value.reshape(*shape[:dim], peers, shape[dim] // peers, *shape[dim + 1 :])
    return jnp.moveaxis(pieces, dim, 0)


def sent_and_summed(value, axis, dim):
    pieces = split_up(value, dim, lax.axis_size(axis))
    arrived = lax.all_to_all(pieces, axis, split_axis=0, concat_axis=0, tiled=True)
    return arrived.sum(axis=0)


def in_order(pieces, dim):
    shape = list(pieces.shape[1:])
    shape[dim] *= pieces.shape[0]
    return jnp.moveaxis(pieces, 0, dim).reshape(shape)


def from_everyone(value, axis):
    peers = lax.axis_size(axis)
    return lax.all_to_all(
        jnp.broadcast_to(value[None], (peers, *value.shape)), axis, 0, 0, tiled=True
    )


def gathered_copies(value, axis, dim):
    return in_order(from_everyone(value, axis), dim)


def square_sums(values):
    wide = values.astype(jnp.float32)
    return jnp.sum(wide * wide, axis=1)


def norm_total(partial_sum):
    return over_axes(partial_sum, REQ)


def inverse_of(total, count):
    return lax.rsqrt(total / count + eps)


def head_total(partial_sum):
    return total_of_pieces(partial_sum, "head")


def on_device(
    residual,
    lengths,
    ssm_state,
    tail_mix,
    tail_group,
    norm_first,
    mix_weight,
    group_weight,
    step_weight,
    conv_mix,
    conv_group,
    bias_mix,
    bias_group,
    step_bias,
    decay_log,
    skip_gain,
    gate_gain,
    out_weight,
    norm_second,
    up_weight,
    down_weight,
):
    rows_dev = ssm_state.shape[0]
    heads_dev = ssm_state.shape[1]
    head_dim = ssm_state.shape[2]
    state_size = ssm_state.shape[3]
    mix_dev = mix_weight.shape[2]
    group_dev = group_weight.shape[2]
    groups_dev = group_dev // state_size
    per_group = heads_dev // groups_dev
    width_dev = residual.shape[1]
    width_all = width_dev * lax.axis_size(REQ)
    taps_all = conv_mix.shape[0]
    first_row = lax.axis_index(REQ) * rows_dev
    partial_one = square_sums(residual)
    scaled = (residual.astype(jnp.float32) * norm_first).astype(jnp.bfloat16)
    mix_flat = mix_weight.reshape(width_dev, 2 * mix_dev)
    group_flat = group_weight.reshape(width_dev, 2 * group_dev)
    pieces = [
        jnp.dot(scaled, mix_flat, preferred_element_type=jnp.float32),
        jnp.dot(scaled, group_flat, preferred_element_type=jnp.float32),
        jnp.dot(scaled, step_weight, preferred_element_type=jnp.float32),
    ]
    sums = sent_and_summed(jnp.concatenate(pieces, axis=1), REQ, 0)
    total_one = lax.dynamic_slice_in_dim(norm_total(partial_one), first_row, rows_dev, 0)
    sums = sums * inverse_of(total_one, width_all)[:, None]
    gate_z = sums[:, :mix_dev]
    mix_in = sums[:, mix_dev : 2 * mix_dev]
    group_in = sums[:, 2 * mix_dev : 2 * mix_dev + 2 * group_dev].reshape(rows_dev, 2, group_dev)
    step_raw = sums[:, 2 * mix_dev + 2 * group_dev :]
    valid = jnp.minimum(lengths, taps_all - 1)
    slots = jnp.arange(taps_all - 1)
    keep = (slots[None, :] >= (taps_all - 1 - valid)[:, None]).astype(jnp.float32)
    window_mix = jnp.concatenate([tail_mix * keep[:, :, None], mix_in[:, None, :]], axis=1)
    window_group = jnp.concatenate([tail_group * keep[:, :, None, None], group_in[:, None]], axis=1)
    conv_x = jax.nn.silu(jnp.sum(window_mix * conv_mix[None], axis=1) + bias_mix)
    conv_bc = jax.nn.silu(jnp.sum(window_group * conv_group[None], axis=1) + bias_group)
    step_size = jax.nn.softplus(step_raw + step_bias)
    alive = (lengths > 0).astype(jnp.float32)
    decay = jnp.exp(-step_size * jnp.exp(decay_log)) * alive[:, None]
    inputs = conv_x.reshape(rows_dev, groups_dev, per_group, head_dim)
    b_vector = conv_bc[:, 0].reshape(rows_dev, groups_dev, 1, 1, state_size)
    c_vector = conv_bc[:, 1].reshape(rows_dev, groups_dev, state_size)
    prior = ssm_state.reshape(rows_dev, groups_dev, per_group, head_dim, state_size)
    rate = decay.reshape(rows_dev, groups_dev, per_group, 1, 1)
    stride = step_size.reshape(rows_dev, groups_dev, per_group, 1)
    updated = rate * prior + (stride * inputs)[..., None] * b_vector
    readout = jnp.einsum("rgepn,rgn->rgep", updated, c_vector, precision=lax.Precision.HIGHEST)
    readout = readout + skip_gain.reshape(1, groups_dev, per_group, 1) * inputs
    mixed = readout.reshape(rows_dev, mix_dev)
    state_out = updated.reshape(ssm_state.shape)
    gated = mixed * jax.nn.silu(gate_z)
    grouped = gated.reshape(rows_dev, groups_dev, -1)
    inverse = lax.rsqrt(jnp.mean(grouped * grouped, axis=2, keepdims=True) + eps)
    normed_y = ((grouped * inverse).reshape(rows_dev, mix_dev) * gate_gain).astype(jnp.bfloat16)
    mixer = head_total(
        jnp.dot(gathered_copies(normed_y, REQ, 0), out_weight, preferred_element_type=jnp.float32)
    )
    middle = (residual.astype(jnp.float32) + mixer).astype(jnp.bfloat16)
    partial_two = square_sums(middle)
    scaled_two = (middle.astype(jnp.float32) * norm_second).astype(jnp.bfloat16)
    activation = jnp.dot(scaled_two, up_weight, preferred_element_type=jnp.float32)
    total_two = norm_total(partial_two)
    share = sent_and_summed(activation, REQ, 1)
    share = share * inverse_of(total_two, width_all)[:, None]
    hidden_share = jnp.square(jax.nn.relu(share)).astype(jnp.bfloat16)
    projected = jnp.dot(
        gathered_copies(hidden_share, REQ, 1), down_weight, preferred_element_type=jnp.float32
    )
    projected = head_total(projected)
    residual_out = (middle.astype(jnp.float32) + projected).astype(jnp.bfloat16)
    return (residual_out, state_out, window_mix[:, 1:], window_group[:, 1:])


def solution(mesh):
    finer = Mesh(mesh.devices.reshape(4, 4, mesh.shape["head"]), ("req_0", "req_1", "head"))
    placed = (
        P(None, REQ),
        P(REQ),
        P(REQ, "head", None, None),
        P(REQ, None, "head"),
        P(REQ, None, None, "head"),
        P(REQ),
        P(REQ, None, "head"),
        P(REQ, None, "head"),
        P(REQ, "head"),
        P(None, "head"),
        P(None, None, "head"),
        P("head"),
        P(None, "head"),
        P("head"),
        P("head"),
        P("head"),
        P("head"),
        P("head", REQ),
        P(REQ),
        P(REQ, "head"),
        P("head", REQ),
    )
    return jax.shard_map(
        on_device,
        mesh=finer,
        in_specs=placed,
        out_specs=(
            P(None, REQ),
            P(REQ, "head", None, None),
            P(REQ, None, "head"),
            P(REQ, None, None, "head"),
        ),
        check_vma=False,
    )
```

profile of v0, /device:TPU:1, one launch (start us, length us, event | category | flops | bytes accessed | tf_op | source)
XLA Modules:
  0.0 244.6 jit_solution(6302322050598618049)
XLA Ops:
  7.2 1.2 fusion.15
  8.4 1.2 fusion.11
  9.6 1.5 copy.45
  11.1 0.4 fusion.18
  11.5 1.6 pad_maximum_fusion
  13.2 8.6 %all-to-all-start = ((f32[16,16,2320]{2,1,0:T(8,128)}), f32[16,16,2320]{2,1,0:T(8,128)}, u32[]{:S(2)}, u32[]{:S(2)}) async-start(f32[16,16,2320]{2,1,0:T(8,128)} %bitcast.37), calls=%async_computation | async-start | bytes 4980736 | tf_op jit(solution)/shard_map/all_to_all | solution.py:31
  22.1 0.1 fusion.3
  22.2 23.1 %psum.28 = f32[256]{0:T(256)S(1)} all-reduce(f32[256]{0:T(256)S(1)} %fusion.3), channel_id=1, replica_groups=mesh['req_0'=4,'req_1'=4,'head'=8] {'req_0'}, use_global_device_ids=true, to_apply=%region_2.0 | all-reduce | flops 256 | bytes 2048 | tf_op jit(solution)/shard_map/psum | solution.py:15
  45.3 15.8 %psum.29 = f32[256]{0:T(256)S(1)} all-reduce(f32[256]{0:T(256)S(1)} %psum.28), channel_id=1, replica_groups=mesh['req_0'=4,'req_1'=4,'head'=8] {'req_1'}, use_global_device_ids=true, to_apply=%region_3.0 | all-reduce | flops 256 | bytes 2048 | tf_op jit(solution)/shard_map/psum | solution.py:15
  61.1 0.1 broadcast_multiply_fusion.3
  61.4 1.8 reduce_sum.83
  63.7 0.1 broadcast_multiply_fusion.2
  63.8 5.7 %multiply_add_fusion = f32[16,16,64,128]{3,2,1,0:T(8,128)S(1)} fusion(f32[16,16,64,128]{3,2,1,0:T(8,128)} %param.23, f32[16,128]{1,0:T(8,128)S(1)} %bitcast.46, f32[16,16,64]{2,1,0:T(8,128)S(1)} %broadcast_multiply_fusion.2, f32[16,16]{1,0:T(8,128)S(1)} %get-tuple-element.8), kind=kLoop, calls=%fused_computation | loop fusion | flops 6291456 | bytes 16851968 | tf_op jit(solution)/shard_map/add | solution.py:136
  69.6 19.5 %fusion.23 = f32[16,1,16,64]{3,1,2,0:T(1,128)S(1)} fusion(f32[16,16,64,128]{3,2,1,0:T(8,128)S(1)} %multiply_add_fusion, f32[16,2,128]{2,1,0:T(2,128)S(1)} %divide_multiply_fusion.1), kind=kOutput, calls=%fused_computation.47 | convolution fusion | flops 25165824 | bytes 8462336 | tf_op jit(solution)/shard_map/rgepn,rgn->rgep/dot_general | solution.py:137
  89.3 0.1 multiply_reduce_fusion
  89.6 12.2 %all_to_all.20 = bf16[16,16,1024]{2,1,0:T(8,128)(2,1)S(1)} all-to-all(bf16[16,16,1024]{2,1,0:T(8,128)(2,1)S(1)} %broadcast_in_dim.7), channel_id=1, replica_groups=mesh['req_0'=4,'req_1'=4,'head'=8] {'req_0','req_1'}, dimensions={0} | all-to-all | bytes 1048576 | tf_op jit(solution)/shard_map/all_to_all | solution.py:43
  101.8 1.0 fusion.26
  102.8 28.6 %all-gather.5.cloned.1.call-done = f32[2048,256]{1,0:T(8,128)} async-done(((f32[256,256]{1,0:T(8,128)}), f32[2048,256]{1,0:T(8,128)}) %all-gather.5.cloned.1.call-update) | async-done | bytes 2097168 | tf_op jit(solution)/shard_map/all_gather | solution.py:20
  131.4 1.8 reduce_sum.89
  133.2 0.1 fusion.6
  133.3 2.2 fusion.9
  135.5 6.7 %all-to-all-start.2 = ((f32[16,256,168]{1,2,0:T(8,128)}), f32[16,256,168]{1,2,0:T(8,128)}, u32[]{:S(2)}, u32[]{:S(2)}) async-start(f32[16,256,168]{1,2,0:T(8,128)} %bitcast.36), calls=%async_computation.2 | async-start | bytes 5505024 | tf_op jit(solution)/shard_map/all_to_all | solution.py:31
  142.3 24.1 %psum.30 = f32[256]{0:T(256)S(1)} all-reduce(f32[256]{0:T(256)S(1)} %get-tuple-element.4), channel_id=1, replica_groups=mesh['req_0'=4,'req_1'=4,'head'=8] {'req_0'}, use_global_device_ids=true, to_apply=%region_10.11 | all-reduce | flops 256 | bytes 2048 | tf_op jit(solution)/shard_map/psum | solution.py:15
  166.4 18.6 %psum.31 = f32[256]{0:T(256)S(1)} all-reduce(f32[256]{0:T(256)S(1)} %psum.30), channel_id=1, replica_groups=mesh['req_0'=4,'req_1'=4,'head'=8] {'req_1'}, use_global_device_ids=true, to_apply=%region_11.12 | all-reduce | flops 256 | bytes 2048 | tf_op jit(solution)/shard_map/psum | solution.py:15
  185.0 2.0 reduce_sum.90
  187.1 21.0 %all_to_all.21 = bf16[16,256,168]{1,2,0:T(8,128)(2,1)S(1)} all-to-all(bf16[16,256,168]{1,2,0:T(8,128)(2,1)S(1)} %broadcast_in_dim.8), channel_id=1, replica_groups=mesh['req_0'=4,'req_1'=4,'head'=8] {'req_0','req_1'}, dimensions={0} | all-to-all | bytes 2752512 | tf_op jit(solution)/shard_map/all_to_all | solution.py:43
  208.0 1.3 fusion.27
  209.4 0.6 fusion.22
  210.0 0.7 fusion.8
  210.7 24.6 %all-gather.7.cloned.1.call-done = f32[2048,256]{1,0:T(8,128)} async-done(((f32[256,256]{1,0:T(8,128)}), f32[2048,256]{1,0:T(8,128)}) %all-gather.7.cloned.1.call-update) | async-done | bytes 2097168 | tf_op jit(solution)/shard_map/all_gather | solution.py:20
  235.3 1.8 reduce_sum.92
  237.0 0.7 fusion.7
  (68 shorter events, 1.4 us)
Async XLA Ops:
  7.2 126.1 %copy-start = (bf16[256,2688]{1,0:T(8,128)(2,1)S(1)}, bf16[256,2688]{1,0:T(8,128)(2,1)}, u32[]{:S(2)}) copy-start(bf16[256,2688]{1,0:T(8,128)(2,1)} %param.40) | copy-start | bytes 4128772
  7.2 3.9 %copy-start.2 = (bf16[256,256]{1,0:T(8,128)(2,1)S(1)}, bf16[256,256]{1,0:T(8,128)(2,1)}, u32[]{:S(2)}) copy-start(bf16[256,256]{1,0:T(8,128)(2,1)} %param.21) | copy-start | bytes 393220
  7.2 3.9 %copy-start.8 = (f32[256]{0:T(256)S(1)}, f32[256]{0:T(256)}, u32[]{:S(2)}) copy-start(f32[256]{0:T(256)} %param.26) | copy-start | bytes 3076
  13.2 8.7 %copy-start.16 = (f32[16]{0:T(128)S(1)}, f32[16]{0:T(128)}, u32[]{:S(2)}) copy-start(f32[16]{0:T(128)} %param.35) | copy-start | bytes 196
  13.2 8.8 %copy-start.10 = (f32[1024]{0:T(1024)S(1)}, f32[1024]{0:T(1024)}, u32[]{:S(2)}) copy-start(f32[1024]{0:T(1024)} %param.32) | copy-start | bytes 12292
  13.2 8.8 %copy-start.17 = (s32[16]{0:T(128)S(1)}, s32[16]{0:T(128)}, u32[]{:S(2)}) copy-start(s32[16]{0:T(128)} %param.22) | copy-start | bytes 196
  13.2 48.0 %copy-start.6 = (f32[16,3,2,128]{3,2,1,0:T(2,128)S(1)}, f32[16,3,2,128]{3,2,1,0:T(2,128)}, u32[]{:S(2)}) copy-start(f32[16,3,2,128]{3,2,1,0:T(2,128)} %param.25) | copy-start | bytes 147460
  13.2 48.1 %copy-start.5 = (f32[16,3,1024]{2,0,1:T(8,128)S(1)}, f32[16,3,1024]{2,0,1:T(8,128)}, u32[]{:S(2)}) copy-start(f32[16,3,1024]{2,0,1:T(8,128)} %param.24) | copy-start | bytes 589828
  13.2 48.2 %all-to-all-start = ((f32[16,16,2320]{2,1,0:T(8,128)}), f32[16,16,2320]{2,1,0:T(8,128)}, u32[]{:S(2)}, u32[]{:S(2)}) async-start(f32[16,16,2320]{2,1,0:T(8,128)} %bitcast.37), calls=%async_computation | async-start | bytes 4980736 | tf_op jit(solution)/shard_map/all_to_all | solution.py:31
  21.8 41.5 %copy-start.12 = (f32[4,2,128]{2,1,0:T(2,128)S(1)}, f32[4,2,128]{2,1,0:T(2,128)}, u32[]{:S(2)}) copy-start(f32[4,2,128]{2,1,0:T(2,128)} %param.31) | copy-start | bytes 12292
  21.8 41.6 %copy-start.13 = (f32[2,128]{1,0:T(2,128)S(1)}, f32[2,128]{1,0:T(2,128)}, u32[]{:S(2)}) copy-start(f32[2,128]{1,0:T(2,128)} %param.33) | copy-start | bytes 3076
  21.8 41.6 %copy-start.7 = (f32[4,1024]{1,0:T(4,128)S(1)}, f32[4,1024]{1,0:T(4,128)}, u32[]{:S(2)}) copy-start(f32[4,1024]{1,0:T(4,128)} %param.30) | copy-start | bytes 49156
  21.8 41.8 %copy-start.15 = (f32[16]{0:T(128)S(1)}, f32[16]{0:T(128)}, u32[]{:S(2)}) copy-start(f32[16]{0:T(128)} %param.34) | copy-start | bytes 196
  21.9 109.6 %all-gather.5.cloned.1.call-start = ((), (), s32[]{:S(2)}) async-start(), calls=%async_computation.4 | async-start | bytes 2359296 | tf_op jit(solution)/shard_map/all_gather | solution.py:20
  69.5 19.6 %copy-start.1 = (f32[16,16,64,128]{3,2,1,0:T(8,128)}, f32[16,16,64,128]{3,2,1,0:T(8,128)S(1)}, u32[]{:S(2)}) copy-start(f32[16,16,64,128]{3,2,1,0:T(8,128)S(1)} %multiply_add_fusion) | copy-start | bytes 25165828
  69.5 19.6 %copy-start.14 = (f32[16]{0:T(128)S(1)}, f32[16]{0:T(128)}, u32[]{:S(2)}) copy-start(f32[16]{0:T(128)} %param.36) | copy-start | bytes 196
  69.6 19.9 %copy-start.11 = (f32[1024]{0:T(1024)S(1)}, f32[1024]{0:T(1024)}, u32[]{:S(2)}) copy-start(f32[1024]{0:T(1024)} %param.37) | copy-start | bytes 12292
  89.1 12.7 %copy-start.4 = (bf16[1024,256]{1,0:T(8,128)(2,1)S(1)}, bf16[1024,256]{1,0:T(8,128)(2,1)}, u32[]{:S(2)}) copy-start(bf16[1024,256]{1,0:T(8,128)(2,1)} %param.38) | copy-start | bytes 1572868
  101.8 31.5 %copy-start.9 = (f32[256]{0:T(256)S(1)}, f32[256]{0:T(256)}, u32[]{:S(2)}) copy-start(f32[256]{0:T(256)} %param.39) | copy-start | bytes 3076
  135.5 49.4 %all-to-all-start.2 = ((f32[16,256,168]{1,2,0:T(8,128)}), f32[16,256,168]{1,2,0:T(8,128)}, u32[]{:S(2)}, u32[]{:S(2)}) async-start(f32[16,256,168]{1,2,0:T(8,128)} %bitcast.36), calls=%async_computation.2 | async-start | bytes 5505024 | tf_op jit(solution)/shard_map/all_to_all | solution.py:31
  142.2 93.0 %all-gather.7.cloned.1.call-start = ((), (), s32[]{:S(2)}) async-start(), calls=%async_computation.5 | async-start | bytes 2359296 | tf_op jit(solution)/shard_map/all_gather | solution.py:20
  186.9 21.1 %copy-start.3 = (bf16[2688,256]{1,0:T(8,128)(2,1)S(1)}, bf16[2688,256]{1,0:T(8,128)(2,1)}, u32[]{:S(2)}) copy-start(bf16[2688,256]{1,0:T(8,128)(2,1)} %param.41) | copy-start | bytes 4128772
Sparse Core Ops, SparseCore 0:
  102.9 28.4 all-gather.4
  209.5 25.7 all-gather.6
where the time goes:
time: 245 us
  blocking collectives  115 us (47%)
  waiting for transfers between devices  53.2 us (22%)
  matrix products  26.9 us (11%)
  other arithmetic  17.9 us (7%)
  starting transfers between devices  15.4 us (6%)
  between operations  14.4 us (6%)
    psum x4, blocking collectives, over_axes(): value = lax.psum(value, axis)  81.5 us
    all_gather x2, waiting for transfers between devices, total_of_pieces(): return lax.all_gather(value, axis).sum(0)  53.2 us
    all_to_all x2, blocking collectives, from_everyone(): lax.all_to_all(jnp.broadcast_to(value[None], (peers, *value.shape)), axis...  33.1 us
    dot_general x1, matrix products, on_device(): jnp.einsum('rgepn,rgn->rgep', updated, c_vector, precision=lax.Precision....  19.5 us
    all_to_all x2, starting transfers between devices, sent_and_summed(): lax.all_to_all(pieces, axis, split_axis=0, concat_axis=0, tiled=True)  15.3 us
    add x1, other arithmetic, on_device(): updated = rate * prior + (stride * inputs)[..., None] * b_vector  5.74 us
  transfers between devices with their start and end apart: 4, of which 2 were waited for; matrix products, arithmetic and copies ran while one was open for 1% of the time, Pallas kernels for 0%

commit v1 on v0

v1 whole, which is shorter than its diff:
```python
import jax
import jax.numpy as jnp
from jax import lax
from jax.experimental import pallas as pl
from jax.experimental.pallas import tpu as pltpu
from jax.sharding import Mesh
from jax.sharding import PartitionSpec as P

REQ = ("z", "x")
HEAD = ("y", "c")
LANES = 128
f32 = jnp.float32
bf16 = jnp.bfloat16

eps = 1e-05


def three_parts(total):
    high = total.astype(bf16)
    rest = total - high.astype(f32)
    middle = rest.astype(bf16)
    low = (rest - middle.astype(f32)).astype(bf16)
    return high, middle, low


def silu(v):
    return v / (1.0 + jnp.exp(-v))


def norm_columns(wide, width):
    total = jnp.sum(wide * wide, axis=1, keepdims=True)
    high, middle, low = three_parts(total)
    lane = lax.broadcasted_iota(jnp.int32, (wide.shape[0], LANES), 1)
    zero = jnp.zeros((wide.shape[0], LANES), f32)
    out = jnp.where(lane == width, high.astype(f32), zero)
    out = jnp.where(lane == width + 1, middle.astype(f32), out)
    return jnp.where(lane == width + 2, low.astype(f32), out)


def input_kernel(residual_ref, norm_ref, mix_ref, group_ref, step_ref, out_ref):
    wide = residual_ref[...].astype(f32)
    scaled = (wide * norm_ref[...]).astype(bf16)
    mix = mix_ref.shape[1]
    group = group_ref.shape[1]
    steps = step_ref.shape[0]
    out_ref[:, :mix] = jnp.dot(scaled, mix_ref[...], preferred_element_type=f32).astype(bf16)
    out_ref[:, mix : mix + group] = jnp.dot(scaled, group_ref[...], preferred_element_type=f32).astype(bf16)
    step = lax.dot_general(scaled, step_ref[...], (((1,), (1,)), ((), ())), preferred_element_type=f32)
    tail = norm_columns(wide, steps)
    out_ref[:, mix + group :] = tail.astype(bf16)
    out_ref[:, mix + group : mix + group + steps] = step.astype(bf16)


def input_projection(residual, norm, mix, group, step_t):
    rows = residual.shape[0]
    width = mix.shape[1] + group.shape[1] + LANES
    return pl.pallas_call(
        input_kernel,
        out_shape=jax.ShapeDtypeStruct((rows, width), bf16),
        name="input_projection",
    )(residual, norm, mix, group, step_t)


def make_state_kernel(per_step, width_all, dims):
    pieces, rows, heads, head_dim, state, mix, taps = dims
    steps = rows // per_step

    def kernel(
        arrived_ref, lengths_ref, tail_mix_ref, tail_group_ref, conv_mix_ref, conv_group_ref,
        bias_mix_ref, bias_group_ref, step_bias_ref, decay_log_ref, skip_ref, gain_ref, state_ref,
        y_ref, tail_mix_out_ref, tail_group_out_ref, state_out_ref,
        u_ref, decay_ref, decay_wide_ref, b_ref, c_ref, x_ref, gate_ref, out_acc,
    ):
        i = pl.program_id(0)

        def expand(v):
            row = lax.broadcasted_iota(jnp.int32, (heads, mix), 0)
            col = lax.broadcasted_iota(jnp.int32, (heads, mix), 1)
            spread = (col // head_dim == row).astype(f32)
            return jnp.dot(v, spread, precision=lax.Precision.HIGHEST, preferred_element_type=f32)

        @pl.when(i == 0)
        def _():
            def total(lo, hi):
                acc = arrived_ref[0, :, lo:hi].astype(f32)
                for j in range(1, pieces):
                    acc = acc + arrived_ref[j, :, lo:hi].astype(f32)
                return acc

            base = 2 * mix
            last = total(base + 2 * state, base + 2 * state + LANES)
            squares = last[:, heads : heads + 1] + last[:, heads + 1 : heads + 2] + last[:, heads + 2 : heads + 3]
            inverse = lax.rsqrt(squares / width_all + eps)
            gate_ref[...] = total(0, mix) * inverse
            mix_in = total(mix, base) * inverse
            group_in = [total(base + g * state, base + (g + 1) * state) * inverse for g in range(2)]
            step_raw = last[:, :heads] * inverse
            lengths = lengths_ref[...]
            valid = jnp.minimum(lengths, taps - 1)
            conv = mix_in * conv_mix_ref[taps - 1 : taps, :]
            for j in range(taps - 1):
                keep = (valid >= taps - 1 - j).astype(f32)
                w = tail_mix_ref[j] * keep
                if j > 0:
                    tail_mix_out_ref[j - 1] = w
                conv = conv + w * conv_mix_ref[j : j + 1, :]
            tail_mix_out_ref[taps - 2] = mix_in
            x = silu(conv + bias_mix_ref[...])
            x_ref[...] = x
            for g, dest in ((0, b_ref), (1, c_ref)):
                conv = group_in[g] * conv_group_ref[taps - 1, g : g + 1, :]
                for j in range(taps - 1):
                    keep = (valid >= taps - 1 - j).astype(f32)
                    w = tail_group_ref[:, j, g, :] * keep
                    if j > 0:
                        tail_group_out_ref[:, j - 1, g, :] = w
                    conv = conv + w * conv_group_ref[j, g : g + 1, :]
                tail_group_out_ref[:, taps - 2, g, :] = group_in[g]
                dest[...] = silu(conv + bias_group_ref[g : g + 1, :])
            v = step_raw + step_bias_ref[...]
            step_size = jnp.maximum(v, 0.0) + jnp.log1p(jnp.exp(-jnp.abs(v)))
            alive = (lengths > 0).astype(f32)
            decay = jnp.exp(-step_size * jnp.exp(decay_log_ref[...])) * alive
            decay_wide = expand(decay)
            decay_wide_ref[...] = decay_wide
            decay_ref[...] = jnp.concatenate([decay, jnp.zeros((rows, LANES - heads), f32)], axis=1)
            u = expand(step_size) * x
            for t in range(mix // LANES):
                u_ref[t] = u[:, t * LANES : (t + 1) * LANES]
            out_acc[...] = jnp.zeros_like(out_acc)

        lane = lax.broadcasted_iota(jnp.int32, (state, LANES), 1)
        for k in range(per_step):
            r = i * per_step + k
            b_row = b_ref[pl.ds(r, 1), :]
            c_row = c_ref[pl.ds(r, 1), :]
            c_col = jnp.transpose(jnp.broadcast_to(c_row, (LANES, state)))
            c_high = c_col.astype(bf16)
            c_low = (c_col - c_high.astype(f32)).astype(bf16)
            rhs = jnp.where(lane == r, c_high.astype(f32), 0.0) + jnp.where(lane == r + rows, c_low.astype(f32), 0.0)
            rhs = rhs.astype(bf16)
            d_row = jnp.transpose(jnp.broadcast_to(decay_ref[pl.ds(r, 1), :], (LANES, LANES)))
            for h in range(heads):
                at = h * head_dim
                if at % LANES == 0:
                    u_row = u_ref[at // LANES, pl.ds(r, 1), :]
                    u_col = jnp.transpose(jnp.broadcast_to(u_row, (LANES, LANES)))
                u_h = u_col[at % LANES : at % LANES + head_dim, :]
                s = state_ref[k, h]
                state_out_ref[k, h] = s * d_row[h : h + 1, :] + u_h * b_row
                s_high = s.astype(bf16)
                s_low = (s - s_high.astype(f32)).astype(bf16)
                rows_h = pl.ds(h * head_dim, head_dim)
                out_acc[rows_h, :] += jnp.dot(s_high, rhs, preferred_element_type=f32) + jnp.dot(
                    s_low, rhs, preferred_element_type=f32
                )

        @pl.when(i == steps - 1)
        def _():
            acc = jnp.transpose(out_acc[...])
            read = acc[:rows, :] + acc[rows : 2 * rows, :]
            bc = jnp.sum(b_ref[...] * c_ref[...], axis=1, keepdims=True)
            x = x_ref[...]
            u = jnp.concatenate([u_ref[t] for t in range(mix // LANES)], axis=1)
            mixed = decay_wide_ref[...] * read + u * bc + expand(jnp.broadcast_to(skip_ref[...], (rows, heads))) * x
            gated = mixed * silu(gate_ref[...])
            inverse = lax.rsqrt(jnp.mean(gated * gated, axis=1, keepdims=True) + eps)
            y_ref[...] = (gated * inverse * gain_ref[...]).astype(bf16)

    return kernel


def state_step(arrived, lengths, tail_mix, tail_group, conv_mix, conv_group, bias_mix, bias_group,
               step_bias, decay_log, skip_gain, gate_gain, ssm_state, width_all, per_step=2):
    pieces, rows, width = arrived.shape
    _, heads, head_dim, state = ssm_state.shape
    mix = heads * head_dim
    taps = conv_mix.shape[0]
    args = (
        arrived, lengths[:, None], jnp.transpose(tail_mix, (1, 0, 2)), tail_group, conv_mix, conv_group,
        bias_mix[None], bias_group, step_bias[None], decay_log[None], skip_gain[None], gate_gain[None],
    )

    def whole(shape):
        return pl.BlockSpec(shape, lambda i, n=len(shape): (0,) * n)

    block = pl.BlockSpec((per_step, heads, head_dim, state), lambda i: (i, 0, 0, 0))
    outs = (
        jax.ShapeDtypeStruct((rows, mix), bf16),
        jax.ShapeDtypeStruct((taps - 1, rows, mix), f32),
        jax.ShapeDtypeStruct((rows, taps - 1, 2, state), f32),
        jax.ShapeDtypeStruct(ssm_state.shape, f32),
    )
    y, tail_mix_out, tail_group_out, state_out = pl.pallas_call(
        make_state_kernel(per_step, width_all, (pieces, rows, heads, head_dim, state, mix, taps)),
        grid=(rows // per_step,),
        in_specs=[whole(a.shape) for a in args] + [block],
        out_specs=[whole(o.shape) for o in outs[:3]] + [block],
        out_shape=outs,
        scratch_shapes=[
            pltpu.VMEM((mix // LANES, rows, LANES), f32),
            pltpu.VMEM((rows, LANES), f32),
            pltpu.VMEM((rows, mix), f32),
            pltpu.VMEM((rows, state), f32),
            pltpu.VMEM((rows, state), f32),
            pltpu.VMEM((rows, mix), f32),
            pltpu.VMEM((rows, mix), f32),
            pltpu.VMEM((mix, LANES), f32),
        ],
        name="state_step",
    )(*args, ssm_state)
    return y, jnp.transpose(tail_mix_out, (1, 0, 2)), tail_group_out, state_out


def swap_core(value):
    return lax.ppermute(value, "c", [(0, 1), (1, 0)])


def ring_pairs(value, first):
    n = lax.axis_size("y")
    pairs = []
    for a in range(first, n + first, 2):
        p, q = a % n, (a + 1) % n
        pairs += [(p, q), (q, p)]
    return lax.ppermute(value, "y", pairs)


def head_sum_half(partial):
    half = partial.shape[0] // 2
    core = lax.axis_index("c")
    mine = lax.dynamic_slice_in_dim(partial, core * half, half, 0)
    theirs = lax.dynamic_slice_in_dim(partial, (1 - core) * half, half, 0).astype(bf16)
    total = mine + swap_core(theirs).astype(f32)
    for first in (0, 1):
        sent = total.astype(bf16)
        total = sent.astype(f32) + ring_pairs(sent, first).astype(f32)
    return total, core


def both_halves(half, core):
    other = swap_core(half)
    first = jnp.where(core == 0, half, other)
    second = jnp.where(core == 0, other, half)
    return jnp.concatenate([first, second], axis=0)


def add_over_heads(base, partial):
    total, core = head_sum_half(partial)
    half = total.shape[0]
    mine = lax.dynamic_slice_in_dim(base, core * half, half, 0).astype(f32)
    return both_halves((mine + total).astype(bf16), core)


def exchange(value, axis):
    return lax.all_to_all(value, axis, 0, 0, tiled=True)


def to_everyone(value, axis):
    peers = lax.axis_size(axis)
    copies = jnp.broadcast_to(value[None], (peers, *value.shape))
    return exchange(copies, axis).reshape(peers * value.shape[0], *value.shape[1:])


def on_device(
    residual, lengths, ssm_state, tail_mix, tail_group, norm_first, mix_weight, group_weight, step_weight,
    conv_mix, conv_group, bias_mix, bias_group, step_bias, decay_log, skip_gain, gate_gain, out_weight,
    norm_second, up_weight, down_weight,
):
    peers = lax.axis_size(REQ)
    rows_dev = ssm_state.shape[0]
    rows, width_dev = residual.shape
    width_all = width_dev * peers
    mix_flat = mix_weight.reshape(width_dev, -1)
    group_flat = group_weight.reshape(width_dev, -1)
    pieces = input_projection(residual, norm_first[None], mix_flat, group_flat, step_weight.T)
    arrived = exchange(pieces.reshape(peers, rows_dev, -1), REQ)
    normed_y, tail_mix_out, tail_group_out, state_out = state_step(
        arrived, lengths, tail_mix, tail_group, conv_mix, conv_group, bias_mix, bias_group, step_bias,
        decay_log, skip_gain, gate_gain, ssm_state, width_all,
    )
    every_y = to_everyone(normed_y, REQ)
    middle = add_over_heads(residual, jnp.dot(every_y, out_weight, preferred_element_type=f32))
    wide = middle.astype(f32)
    scaled_two = (wide * norm_second).astype(bf16)
    activation = jnp.dot(scaled_two, up_weight, preferred_element_type=f32).astype(bf16)
    hidden_dev = up_weight.shape[1]
    total = jnp.sum(wide * wide, axis=1, keepdims=True)
    high = lax.reduce_precision(total, 8, 7)
    mid = lax.reduce_precision(total - high, 8, 7)
    low = total - high - mid
    lane = lax.broadcasted_iota(jnp.int32, (rows, LANES), 1)
    columns = jnp.where(lane == 0, high, jnp.where(lane == 1, mid, jnp.where(lane == 2, low, 0.0))).astype(bf16)
    sent = jnp.concatenate([activation, columns], axis=1).reshape(peers, rows_dev, hidden_dev + LANES)
    sums = exchange(sent, REQ).astype(f32).sum(axis=0)
    squares = sums[:, hidden_dev : hidden_dev + 1] + sums[:, hidden_dev + 1 : hidden_dev + 2] + sums[:, hidden_dev + 2 : hidden_dev + 3]
    inverse = lax.rsqrt(squares / width_all + eps)
    hidden = jnp.square(jax.nn.relu(sums[:, :hidden_dev] * inverse)).astype(bf16)
    every_hidden = to_everyone(hidden, REQ)
    residual_out = add_over_heads(middle, jnp.dot(every_hidden, down_weight, preferred_element_type=f32))
    return residual_out, state_out, tail_mix_out, tail_group_out


def solution(mesh):
    devices = mesh.devices
    finer = Mesh(devices.reshape(4, devices.shape[0] // 4, devices.shape[1] // 2, 2), REQ + HEAD)
    placed = (
        P(None, REQ),
        P(REQ),
        P(REQ, HEAD, None, None),
        P(REQ, None, HEAD),
        P(REQ, None, None, HEAD),
        P(REQ),
        P(REQ, None, HEAD),
        P(REQ, None, HEAD),
        P(REQ, HEAD),
        P(None, HEAD),
        P(None, None, HEAD),
        P(HEAD),
        P(None, HEAD),
        P(HEAD),
        P(HEAD),
        P(HEAD),
        P(HEAD),
        P(HEAD, REQ),
        P(REQ),
        P(REQ, HEAD),
        P(HEAD, REQ),
    )
    return jax.shard_map(
        on_device,
        mesh=finer,
        in_specs=placed,
        out_specs=(P(None, REQ), P(REQ, HEAD, None, None), P(REQ, None, HEAD), P(REQ, None, None, HEAD)),
        check_vma=False,
    )
```

time: 245 us -> 145 us (0.59)
  blocking collectives: 115 us -> 46.3 us
  matrix products: 26.9 us -> 1.4 us
  other arithmetic: 17.9 us -> 1.8 us
  Pallas kernels: 0 us -> 15.6 us
  starting transfers between devices: 15.4 us -> 30.6 us
  between operations: 14.4 us -> 0.83 us
  waiting for transfers between devices: 53.2 us -> 39.7 us
  local copies, waits for them, and re-layouts: 2.13 us -> 7.74 us
    psum x4 -> x0, blocking collectives: 81.5 us -> none  [over_axes(): value = lax.psum(value, axis)]
    all_gather x2 -> x0, waiting for transfers between devices: 53.2 us -> none  [total_of_pieces(): return lax.all_gather(value, axis).sum(0)]
    all_to_all x2, waiting for transfers between devices: 0.01 us -> 28 us  [exchange(): return lax.all_to_all(value, axis, 0, 0, tiled=True)]
    dot_general x7 -> x3, matrix products: 26.9 us -> 1.4 us  [the longest x1 0.55 us: on_device(): jnp.dot(scaled_two, up_weight, preferred_element_type=f32).astype(bf16)]
    ppermute x0 -> x8, starting transfers between devices: none -> 16.7 us  [the longest x4 9.52 us: swap_core(): return lax.ppermute(value, 'c', [(0, 1), (1, 0)])]
    pallas_call x0 -> x2, Pallas kernels: none -> 15.6 us  [the longest x1 12.6 us: state_step(): pl.pallas_call(make_state_kernel(per_step, width_all, (pieces, rows, head...]
    all_to_all x2, blocking collectives: 33.1 us -> 46.3 us  [exchange(): return lax.all_to_all(value, axis, 0, 0, tiled=True)]
    ppermute x0 -> x8, waiting for transfers between devices: none -> 11.8 us  [the longest x4 8.15 us: ring_pairs(): return lax.ppermute(value, 'y', pairs)]
  transfers between devices with their start and end apart: 4 -> 10, of which waited for: 2 -> 10; matrix products, arithmetic and copies ran while one was open for 1% -> 0% of each run, Pallas kernels for 0% -> 0%
where the time goes in v1:
time: 145 us; the launch traced here: 144 us
  blocking collectives  46.3 us (32%)
  waiting for transfers between devices  39.7 us (27%)
  starting transfers between devices  30.6 us (21%)
  Pallas kernels  15.6 us (11%)
  local copies, waits for them, and re-layouts  7.74 us (5%)
  other arithmetic  1.8 us (1%)
    all_to_all x2, blocking collectives, exchange(): return lax.all_to_all(value, axis, 0, 0, tiled=True)  46.3 us
    all_to_all x2, waiting for transfers between devices, exchange(): return lax.all_to_all(value, axis, 0, 0, tiled=True)  28 us
    all_to_all x2, starting transfers between devices, exchange(): return lax.all_to_all(value, axis, 0, 0, tiled=True)  13.9 us
    pallas_call x1, Pallas kernels, state_step(): pl.pallas_call(make_state_kernel(per_step, width_all, (pieces, rows, head...  12.6 us
    ppermute x4, starting transfers between devices, swap_core(): return lax.ppermute(value, 'c', [(0, 1), (1, 0)])  9.52 us
    ppermute x4, waiting for transfers between devices, ring_pairs(): return lax.ppermute(value, 'y', pairs)  8.15 us
    ppermute x4, starting transfers between devices, ring_pairs(): return lax.ppermute(value, 'y', pairs)  7.16 us
    unnamed x16, local copies, waits for them, and re-layouts  5.27 us
  transfers between devices with their start and end apart: 10, of which 10 were waited for; matrix products, arithmetic and copies ran while one was open for 0% of the time, Pallas kernels for 0%

profile of v1, /device:TPU:1, one launch (start us, length us, event | category | flops | bytes accessed | tf_op | source)
XLA Modules:
  0.0 144.0 jit_solution(975215553709772298)
XLA Ops:
  0.6 1.7 %copy.32 = bf16[32,8,2,128]{3,1,2,0:T(8,128)(2,1)} copy(bf16[32,8,2,128]{3,2,1,0:T(2,128)(2,1)} %bitcast.33) | data formatting | bytes 262144
  2.3 2.5 %copy.29 = bf16[32,8,2,1024]{3,1,2,0:T(8,128)(2,1)} copy(bf16[32,8,2,1024]{3,2,1,0:T(2,128)(2,1)} %bitcast.30) | data formatting | bytes 2097152
  4.8 2.9 %input_projection.1 = bf16[256,2432]{1,0:T(8,128)(2,1)} custom-call(bf16[256,256]{1,0:T(8,128)(2,1)} %residual_ref.1, f32[1,256]{1,0:T(1,128)} %bitcast.37, bf16[256,2048]{1,0:T(8,128)(2,1)} %bitcast.28, bf16[256,256]{1,0:T(8,128)(2,1)} %bitcast.31, bf16[16,256]{1,0:T(8,128)(2,1)} %bitcast.34), custom_call_target="tpu_custom_call" | custom-call | tf_op jit(solution)/shard_map/input_projection/pallas_call | solution.py:57
  7.7 8.5 %all-to-all-start = ((bf16[16,16,2432]{2,1,0:T(8,128)(2,1)}), bf16[16,16,2432]{2,1,0:T(8,128)(2,1)S(1)}, u32[]{:S(2)}, u32[]{:S(2)}) async-start(bf16[16,16,2432]{2,1,0:T(8,128)(2,1)} %bitcast.27), calls=%async_computation | async-start | bytes 2490368 | tf_op jit(solution)/shard_map/all_to_all | solution.py:255
  16.3 0.7 copy.28.lengths_ref
  17.0 17.5 %all-to-all-done.arrived_ref = bf16[16,16,2432]{2,1,0:T(8,128)(2,1)S(1)} async-done(((bf16[16,16,2432]{2,1,0:T(8,128)(2,1)}), bf16[16,16,2432]{2,1,0:T(8,128)(2,1)S(1)}, u32[]{:S(2)}, u32[]{:S(2)}) %all-to-all-start) | async-done | bytes 1245216 | tf_op jit(solution)/shard_map/all_to_all | solution.py:255
  34.4 1.1 copy-done.1
  35.5 12.6 %state_step.1 = (bf16[16,1024]{1,0:T(8,128)(2,1)}, f32[3,16,1024]{2,1,0:T(8,128)}, f32[16,3,2,128]{3,2,1,0:T(2,128)}, f32[16,16,64,128]{3,2,1,0:T(8,128)}) custom-call(bf16[16,16,2432]{2,1,0:T(8,128)(2,1)} %copy-done.1, s32[16,1]{1,0:T(8,128)} %copy.28.lengths_ref, f32[3,16,1024]{2,1,0:T(8,128)} %bitcast.32, f32[16,3,2,128]{3,2,1,0:T(2,128)} %tail_group_ref.1, ...), custom_call_target="tpu_custom_call" | custom-call | tf_op jit(solution)/shard_map/state_step/pallas_call | solution.py:194
  48.2 1.7 %broadcast_in_dim.67 = bf16[16,16,1024]{2,1,0:T(8,128)(2,1)} broadcast(bf16[16,1024]{1,0:T(8,128)(2,1)} %get-tuple-element.8), dimensions={1,2} | broadcast | bytes 557056 | tf_op jit(solution)/shard_map/broadcast_in_dim | solution.py:260
  49.8 5.4 %all-to-all-start.1 = ((bf16[16,16,1024]{2,1,0:T(8,128)(2,1)}), bf16[16,16,1024]{2,1,0:T(8,128)(2,1)S(1)}, u32[]{:S(2)}, u32[]{:S(2)}) async-start(bf16[16,16,1024]{2,1,0:T(8,128)(2,1)} %broadcast_in_dim.67), calls=%async_computation.1 | async-start | bytes 1048576 | tf_op jit(solution)/shard_map/all_to_all | solution.py:255
  55.2 10.5 %all-to-all-done.1 = bf16[16,16,1024]{2,1,0:T(8,128)(2,1)S(1)} async-done(((bf16[16,16,1024]{2,1,0:T(8,128)(2,1)}), bf16[16,16,1024]{2,1,0:T(8,128)(2,1)S(1)}, u32[]{:S(2)}, u32[]{:S(2)}) %all-to-all-start.1) | async-done | bytes 524320 | tf_op jit(solution)/shard_map/all_to_all | solution.py:255
  65.7 0.3 fusion.14
  66.1 2.0 %collective-permute-start = (bf16[128,256]{1,0:T(8,128)(2,1)S(1)}, bf16[128,256]{1,0:T(8,128)(2,1)S(1)}, u32[]{:S(2)}, u32[]{:S(2)}) collective-permute-start(bf16[128,256]{1,0:T(8,128)(2,1)S(1)} %dynamic-slice_convert_fusion.1), channel_id=1, source_target_pairs={{0,1},{1,0},{2,3},{3,2},{4,5},{5,4},{6,7},{7,6},{8,9},{9,8},{10,11... | collective-permute-start | bytes 196616 | tf_op jit(solution)/shard_map/ppermute | solution.py:216
  68.1 0.9 collective-permute-done
  69.0 1.4 collective-permute-start.1
  70.4 1.8 %collective-permute-done.1 = bf16[128,256]{1,0:T(8,128)(2,1)S(1)} collective-permute-done((bf16[128,256]{1,0:T(8,128)(2,1)S(1)}, bf16[128,256]{1,0:T(8,128)(2,1)S(1)}, u32[]{:S(2)}, u32[]{:S(2)}) %collective-permute-start.1) | collective-permute-done | bytes 65568 | tf_op jit(solution)/shard_map/ppermute | solution.py:225
  72.3 2.8 %collective-permute-start.2 = (bf16[128,256]{1,0:T(8,128)(2,1)S(1)}, bf16[128,256]{1,0:T(8,128)(2,1)S(1)}, u32[]{:S(2)}, u32[]{:S(2)}) collective-permute-start(bf16[128,256]{1,0:T(8,128)(2,1)S(1)} %add_convert_fusion.4), channel_id=1, source_target_pairs={{2,4},{4,2},{6,0},{0,6},{3,5},{5,3},{7,1},{1,7},{10,12},{12,10},{1... | collective-permute-start | bytes 196616 | tf_op jit(solution)/shard_map/ppermute | solution.py:225
  75.1 1.6 %collective-permute-done.2 = bf16[128,256]{1,0:T(8,128)(2,1)S(1)} collective-permute-done((bf16[128,256]{1,0:T(8,128)(2,1)S(1)}, bf16[128,256]{1,0:T(8,128)(2,1)S(1)}, u32[]{:S(2)}, u32[]{:S(2)}) %collective-permute-start.2) | collective-permute-done | bytes 65568 | tf_op jit(solution)/shard_map/ppermute | solution.py:225
  76.7 2.7 %collective-permute-start.3 = (bf16[128,256]{1,0:T(8,128)(2,1)S(1)}, bf16[128,256]{1,0:T(8,128)(2,1)S(1)}, u32[]{:S(2)}, u32[]{:S(2)}) collective-permute-start(bf16[128,256]{1,0:T(8,128)(2,1)S(1)} %add_convert_fusion.3), channel_id=1, source_target_pairs={{0,1},{1,0},{2,3},{3,2},{4,5},{5,4},{6,7},{7,6},{8,9},{9,8},{10,11... | collective-permute-start | bytes 196616 | tf_op jit(solution)/shard_map/ppermute | solution.py:216
  79.4 0.9 collective-permute-done.3
  80.5 0.6 convolution_convert_fusion
  81.3 23.4 %all_to_all.20 = bf16[16,16,2816]{2,1,0:T(8,128)(2,1)S(1)} all-to-all(bf16[16,16,2816]{2,1,0:T(8,128)(2,1)S(1)} %bitcast.25), channel_id=1, replica_groups=mesh['z'=4,'x'=4,'y'=4,'c'=2] {'z','x'}, dimensions={0} | all-to-all | bytes 2883584 | tf_op jit(solution)/shard_map/all_to_all | solution.py:255
  105.4 22.9 %all_to_all.21 = bf16[16,16,2688]{2,1,0:T(8,128)(2,1)S(1)} all-to-all(bf16[16,16,2688]{2,1,0:T(8,128)(2,1)S(1)} %broadcast_in_dim.72), channel_id=1, replica_groups=mesh['z'=4,'x'=4,'y'=4,'c'=2] {'z','x'}, dimensions={0} | all-to-all | bytes 2752512 | tf_op jit(solution)/shard_map/all_to_all | solution.py:255
  128.2 0.5 fusion.15
  128.8 2.1 %collective-permute-start.4 = (bf16[128,256]{1,0:T(8,128)(2,1)S(1)}, bf16[128,256]{1,0:T(8,128)(2,1)S(1)}, u32[]{:S(2)}, u32[]{:S(2)}) collective-permute-start(bf16[128,256]{1,0:T(8,128)(2,1)S(1)} %dynamic-slice_convert_fusion), channel_id=1, source_target_pairs={{0,1},{1,0},{2,3},{3,2},{4,5},{5,4},{6,7},{7,6},{8,9},{9,8},{10,11... | collective-permute-start | bytes 196616 | tf_op jit(solution)/shard_map/ppermute | solution.py:216
  131.0 0.9 collective-permute-done.4
  132.0 3.0 %collective-permute-done.5 = bf16[128,256]{1,0:T(8,128)(2,1)S(1)} collective-permute-done((bf16[128,256]{1,0:T(8,128)(2,1)S(1)}, bf16[128,256]{1,0:T(8,128)(2,1)S(1)}, u32[]{:S(2)}, u32[]{:S(2)}) %collective-permute-start.5) | collective-permute-done | bytes 65568 | tf_op jit(solution)/shard_map/ppermute | solution.py:225
  135.1 2.8 %collective-permute-start.6 = (bf16[128,256]{1,0:T(8,128)(2,1)S(1)}, bf16[128,256]{1,0:T(8,128)(2,1)S(1)}, u32[]{:S(2)}, u32[]{:S(2)}) collective-permute-start(bf16[128,256]{1,0:T(8,128)(2,1)S(1)} %add_convert_fusion.1), channel_id=1, source_target_pairs={{2,4},{4,2},{6,0},{0,6},{3,5},{5,3},{7,1},{1,7},{10,12},{12,10},{1... | collective-permute-start | bytes 196616 | tf_op jit(solution)/shard_map/ppermute | solution.py:225
  137.9 1.7 %collective-permute-done.6 = bf16[128,256]{1,0:T(8,128)(2,1)S(1)} collective-permute-done((bf16[128,256]{1,0:T(8,128)(2,1)S(1)}, bf16[128,256]{1,0:T(8,128)(2,1)S(1)}, u32[]{:S(2)}, u32[]{:S(2)}) %collective-permute-start.6) | collective-permute-done | bytes 65568 | tf_op jit(solution)/shard_map/ppermute | solution.py:225
  139.7 2.7 %collective-permute-start.7 = (bf16[128,256]{1,0:T(8,128)(2,1)S(1)}, bf16[128,256]{1,0:T(8,128)(2,1)S(1)}, u32[]{:S(2)}, u32[]{:S(2)}) collective-permute-start(bf16[128,256]{1,0:T(8,128)(2,1)S(1)} %add_convert_fusion), channel_id=1, source_target_pairs={{0,1},{1,0},{2,3},{3,2},{4,5},{5,4},{6,7},{7,6},{8,9},{9,8},{10,11... | collective-permute-start | bytes 196616 | tf_op jit(solution)/shard_map/ppermute | solution.py:216
  142.4 0.9 collective-permute-done.7
  143.3 0.7 pad_maximum_fusion.2
  (34 shorter events, 1.5 us)
Async XLA Ops:
  0.6 79.8 %copy-start = (bf16[256,2688]{1,0:T(8,128)(2,1)S(1)}, bf16[256,2688]{1,0:T(8,128)(2,1)}, u32[]{:S(2)}) copy-start(bf16[256,2688]{1,0:T(8,128)(2,1)} %param.40) | copy-start | bytes 4128772
  7.7 8.6 %copy-start.6 = (s32[16]{0:T(128)S(1)}, s32[16]{0:T(128)}, u32[]{:S(2)}) copy-start(s32[16]{0:T(128)} %param.22) | copy-start | bytes 196
  7.7 26.7 %all-to-all-start = ((bf16[16,16,2432]{2,1,0:T(8,128)(2,1)}), bf16[16,16,2432]{2,1,0:T(8,128)(2,1)S(1)}, u32[]{:S(2)}, u32[]{:S(2)}) async-start(bf16[16,16,2432]{2,1,0:T(8,128)(2,1)} %bitcast.27), calls=%async_computation | async-start | bytes 2490368 | tf_op jit(solution)/shard_map/all_to_all | solution.py:255
  34.4 1.1 copy-start.1
  48.2 17.6 %copy-start.3 = (bf16[1024,256]{1,0:T(8,128)(2,1)S(1)}, bf16[1024,256]{1,0:T(8,128)(2,1)}, u32[]{:S(2)}) copy-start(bf16[1024,256]{1,0:T(8,128)(2,1)} %param.38) | copy-start | bytes 1572868
  49.8 26.9 %copy-start.4 = (bf16[256,256]{1,0:T(8,128)(2,1)S(1)}, bf16[256,256]{1,0:T(8,128)(2,1)}, u32[]{:S(2)}) copy-start(bf16[256,256]{1,0:T(8,128)(2,1)} %residual_ref.1) | copy-start | bytes 393220
  49.8 15.9 %all-to-all-start.1 = ((bf16[16,16,1024]{2,1,0:T(8,128)(2,1)}), bf16[16,16,1024]{2,1,0:T(8,128)(2,1)S(1)}, u32[]{:S(2)}, u32[]{:S(2)}) async-start(bf16[16,16,1024]{2,1,0:T(8,128)(2,1)} %broadcast_in_dim.67), calls=%async_computation.1 | async-start | bytes 1048576 | tf_op jit(solution)/shard_map/all_to_all | solution.py:255
  55.2 25.3 %copy-start.5 = (f32[256]{0:T(256)S(1)}, f32[256]{0:T(256)}, u32[]{:S(2)}) copy-start(f32[256]{0:T(256)} %param.39) | copy-start | bytes 3076
  66.1 2.9 %collective-permute-start = (bf16[128,256]{1,0:T(8,128)(2,1)S(1)}, bf16[128,256]{1,0:T(8,128)(2,1)S(1)}, u32[]{:S(2)}, u32[]{:S(2)}) collective-permute-start(bf16[128,256]{1,0:T(8,128)(2,1)S(1)} %dynamic-slice_convert_fusion.1), channel_id=1, source_target_pairs={{0,1},{1,0},{2,3},{3,2},{4,5},{5,4},{6,7},{7,6},{8,9},{9,8},{10,11... | collective-permute-start | bytes 196616 | tf_op jit(solution)/shard_map/ppermute | solution.py:216
  69.0 3.2 %collective-permute-start.1 = (bf16[128,256]{1,0:T(8,128)(2,1)S(1)}, bf16[128,256]{1,0:T(8,128)(2,1)S(1)}, u32[]{:S(2)}, u32[]{:S(2)}) collective-permute-start(bf16[128,256]{1,0:T(8,128)(2,1)S(1)} %add_convert_fusion.5), channel_id=1, source_target_pairs={{0,2},{2,0},{4,6},{6,4},{1,3},{3,1},{5,7},{7,5},{8,10},{10,8},{12,... | collective-permute-start | bytes 196616 | tf_op jit(solution)/shard_map/ppermute | solution.py:225
  72.3 4.5 %collective-permute-start.2 = (bf16[128,256]{1,0:T(8,128)(2,1)S(1)}, bf16[128,256]{1,0:T(8,128)(2,1)S(1)}, u32[]{:S(2)}, u32[]{:S(2)}) collective-permute-start(bf16[128,256]{1,0:T(8,128)(2,1)S(1)} %add_convert_fusion.4), channel_id=1, source_target_pairs={{2,4},{4,2},{6,0},{0,6},{3,5},{5,3},{7,1},{1,7},{10,12},{12,10},{1... | collective-permute-start | bytes 196616 | tf_op jit(solution)/shard_map/ppermute | solution.py:225
  76.7 3.6 %collective-permute-start.3 = (bf16[128,256]{1,0:T(8,128)(2,1)S(1)}, bf16[128,256]{1,0:T(8,128)(2,1)S(1)}, u32[]{:S(2)}, u32[]{:S(2)}) collective-permute-start(bf16[128,256]{1,0:T(8,128)(2,1)S(1)} %add_convert_fusion.3), channel_id=1, source_target_pairs={{0,1},{1,0},{2,3},{3,2},{4,5},{5,4},{6,7},{7,6},{8,9},{9,8},{10,11... | collective-permute-start | bytes 196616 | tf_op jit(solution)/shard_map/ppermute | solution.py:216
  105.3 22.9 %copy-start.2 = (bf16[2688,256]{1,0:T(8,128)(2,1)S(1)}, bf16[2688,256]{1,0:T(8,128)(2,1)}, u32[]{:S(2)}) copy-start(bf16[2688,256]{1,0:T(8,128)(2,1)} %param.41) | copy-start | bytes 4128772
  128.8 3.0 %collective-permute-start.4 = (bf16[128,256]{1,0:T(8,128)(2,1)S(1)}, bf16[128,256]{1,0:T(8,128)(2,1)S(1)}, u32[]{:S(2)}, u32[]{:S(2)}) collective-permute-start(bf16[128,256]{1,0:T(8,128)(2,1)S(1)} %dynamic-slice_convert_fusion), channel_id=1, source_target_pairs={{0,1},{1,0},{2,3},{3,2},{4,5},{5,4},{6,7},{7,6},{8,9},{9,8},{10,11... | collective-permute-start | bytes 196616 | tf_op jit(solution)/shard_map/ppermute | solution.py:216
  131.9 3.2 %collective-permute-start.5 = (bf16[128,256]{1,0:T(8,128)(2,1)S(1)}, bf16[128,256]{1,0:T(8,128)(2,1)S(1)}, u32[]{:S(2)}, u32[]{:S(2)}) collective-permute-start(bf16[128,256]{1,0:T(8,128)(2,1)S(1)} %add_convert_fusion.2), channel_id=1, source_target_pairs={{0,2},{2,0},{4,6},{6,4},{1,3},{3,1},{5,7},{7,5},{8,10},{10,8},{12,... | collective-permute-start | bytes 196616 | tf_op jit(solution)/shard_map/ppermute | solution.py:225
  135.1 4.5 %collective-permute-start.6 = (bf16[128,256]{1,0:T(8,128)(2,1)S(1)}, bf16[128,256]{1,0:T(8,128)(2,1)S(1)}, u32[]{:S(2)}, u32[]{:S(2)}) collective-permute-start(bf16[128,256]{1,0:T(8,128)(2,1)S(1)} %add_convert_fusion.1), channel_id=1, source_target_pairs={{2,4},{4,2},{6,0},{0,6},{3,5},{5,3},{7,1},{1,7},{10,12},{12,10},{1... | collective-permute-start | bytes 196616 | tf_op jit(solution)/shard_map/ppermute | solution.py:225
  139.7 3.6 %collective-permute-start.7 = (bf16[128,256]{1,0:T(8,128)(2,1)S(1)}, bf16[128,256]{1,0:T(8,128)(2,1)S(1)}, u32[]{:S(2)}, u32[]{:S(2)}) collective-permute-start(bf16[128,256]{1,0:T(8,128)(2,1)S(1)} %add_convert_fusion), channel_id=1, source_target_pairs={{0,1},{1,0},{2,3},{3,2},{4,5},{5,4},{6,7},{7,6},{8,9},{9,8},{10,11... | collective-permute-start | bytes 196616 | tf_op jit(solution)/shard_map/ppermute | solution.py:216

commit v2 on v1

v2 whole, which is shorter than its diff:
```python
import jax
import jax.numpy as jnp
from jax import lax
from jax.experimental import pallas as pl
from jax.experimental.pallas import tpu as pltpu
from jax.sharding import Mesh
from jax.sharding import PartitionSpec as P

REQ = ("z", "x")
HEAD = ("y", "c")
LANES = 128
BATCH = 4
IN_VMEM = pl.BlockSpec(memory_space=pltpu.VMEM)
SMALL = pltpu.CompilerParams(vmem_limit_bytes=16 * 2**20)
f32 = jnp.float32
bf16 = jnp.bfloat16

eps = 1e-05


def three_parts(total):
    high = total.astype(bf16)
    rest = total - high.astype(f32)
    middle = rest.astype(bf16)
    low = (rest - middle.astype(f32)).astype(bf16)
    return high, middle, low


def in_hbm(value):
    return pltpu.with_memory_space_constraint(value, pltpu.HBM)


def silu(v):
    return v / (1.0 + jnp.exp(-v))


def norm_columns(wide, width):
    total = jnp.sum(wide * wide, axis=1, keepdims=True)
    high, middle, low = three_parts(total)
    lane = lax.broadcasted_iota(jnp.int32, (wide.shape[0], LANES), 1)
    zero = jnp.zeros((wide.shape[0], LANES), f32)
    out = jnp.where(lane == width, high.astype(f32), zero)
    out = jnp.where(lane == width + 1, middle.astype(f32), out)
    return jnp.where(lane == width + 2, low.astype(f32), out)


def input_kernel(residual_ref, norm_ref, mix_ref, group_ref, step_ref, out_ref):
    wide = residual_ref[...].astype(f32)
    scaled = (wide * norm_ref[...]).astype(bf16)
    mix = mix_ref.shape[1]
    group = group_ref.shape[1]
    steps = step_ref.shape[0]
    out_ref[:, :mix] = jnp.dot(scaled, mix_ref[...], preferred_element_type=f32).astype(bf16)
    out_ref[:, mix : mix + group] = jnp.dot(scaled, group_ref[...], preferred_element_type=f32).astype(bf16)
    step = lax.dot_general(scaled, step_ref[...], (((1,), (1,)), ((), ())), preferred_element_type=f32)
    tail = norm_columns(wide, steps)
    out_ref[:, mix + group :] = tail.astype(bf16)
    out_ref[:, mix + group : mix + group + steps] = step.astype(bf16)


def input_projection(residual, norm, mix, group, step_t):
    rows = residual.shape[0]
    width = mix.shape[1] + group.shape[1] + LANES
    return pl.pallas_call(
        input_kernel,
        out_shape=jax.ShapeDtypeStruct((rows, width), bf16),
        in_specs=[IN_VMEM] * 5,
        out_specs=IN_VMEM,
        compiler_params=SMALL,
        name="input_projection",
    )(residual, norm, mix, group, step_t)


def expander(heads, mix, head_dim):
    row = lax.broadcasted_iota(jnp.int32, (heads, mix), 0)
    col = lax.broadcasted_iota(jnp.int32, (heads, mix), 1)
    return (col // head_dim == row).astype(f32)


def make_mixer_kernel(width_all, dims):
    pieces, rows, heads, head_dim, state, mix, taps = dims

    def kernel(
        arrived_ref, lengths_ref, tail_mix_ref, tail_group_ref, conv_mix_ref, conv_group_ref,
        bias_mix_ref, bias_group_ref, step_bias_ref, decay_log_ref, skip_ref, gain_ref, state_ref,
        y_ref, tail_mix_out_ref, tail_group_out_ref, u_ref, decay_ref, b_ref,
        c_ref, read_ref, buffer_ref, sems,
    ):
        def fetch(r):
            return pltpu.make_async_copy(state_ref.at[r], buffer_ref.at[r], sems.at[r])

        for r in range(rows):
            fetch(r).start()
        spread = expander(heads, mix, head_dim)

        def expand(v):
            return jnp.dot(v, spread, precision=lax.Precision.HIGHEST, preferred_element_type=f32)

        def total(lo, hi):
            acc = arrived_ref[0, :, lo:hi].astype(f32)
            for j in range(1, pieces):
                acc = acc + arrived_ref[j, :, lo:hi].astype(f32)
            return acc

        base = 2 * mix
        last = total(base + 2 * state, base + 2 * state + LANES)
        squares = last[:, heads : heads + 1] + last[:, heads + 1 : heads + 2] + last[:, heads + 2 : heads + 3]
        inverse = lax.rsqrt(squares / width_all + eps)
        across = jnp.broadcast_to(lengths_ref[...].astype(f32), (rows, rows))
        diagonal = lax.broadcasted_iota(jnp.int32, (rows, rows), 0) == lax.broadcasted_iota(jnp.int32, (rows, rows), 1)
        lengths = jnp.sum(jnp.where(diagonal, across, 0.0), axis=1, keepdims=True)
        valid = jnp.minimum(lengths, taps - 1.0)
        keep = [(valid >= taps - 1.0 - j).astype(f32) for j in range(taps - 1)]
        for g, dest in ((0, b_ref), (1, c_ref)):
            group_in = total(base + g * state, base + (g + 1) * state) * inverse
            conv = group_in * conv_group_ref[taps - 1, g : g + 1, :]
            for j in range(taps - 1):
                w = tail_group_ref[:, j, g, :] * keep[j]
                if j > 0:
                    tail_group_out_ref[:, j - 1, g, :] = w
                conv = conv + w * conv_group_ref[j, g : g + 1, :]
            tail_group_out_ref[:, taps - 2, g, :] = group_in
            dest[...] = silu(conv + bias_group_ref[g : g + 1, :])

        mix_in = total(mix, base) * inverse
        conv = mix_in * conv_mix_ref[taps - 1 : taps, :]
        for j in range(taps - 1):
            w = tail_mix_ref[j] * keep[j]
            if j > 0:
                tail_mix_out_ref[j - 1] = w
            conv = conv + w * conv_mix_ref[j : j + 1, :]
        tail_mix_out_ref[taps - 2] = mix_in
        x = silu(conv + bias_mix_ref[...])
        v = last[:, :heads] * inverse + step_bias_ref[...]
        step_size = jnp.maximum(v, 0.0) + jnp.log1p(jnp.exp(-jnp.abs(v)))
        alive = (lengths > 0.0).astype(f32)
        decay = jnp.exp(-step_size * jnp.exp(decay_log_ref[...])) * alive
        decay_ref[...] = jnp.concatenate([decay, jnp.zeros((rows, LANES - heads), f32)], axis=1)
        u = expand(step_size) * x
        for t in range(mix // LANES):
            u_ref[t] = u[:, t * LANES : (t + 1) * LANES]
        lane = lax.broadcasted_iota(jnp.int32, (head_dim, LANES), 1)
        for first in range(0, rows, BATCH):
            for r in range(first, first + BATCH):
                fetch(r).wait()

            def one_head(h, carry, first=first):
                at = pl.ds(pl.multiple_of(h * head_dim, head_dim), head_dim)
                acc = jnp.zeros((head_dim, LANES), f32) if first == 0 else read_ref[at, :]
                for r in range(first, first + BATCH):
                    part = jnp.sum(buffer_ref[r, h] * c_ref[r : r + 1, :], axis=1, keepdims=True)
                    acc = jnp.where(lane == r, part, acc)
                read_ref[at, :] = acc
                return carry

            lax.fori_loop(0, heads, one_head, 0)

        read = jnp.transpose(read_ref[...])[:rows, :]
        bc = jnp.sum(b_ref[...] * c_ref[...], axis=1, keepdims=True)
        skip = expand(jnp.broadcast_to(skip_ref[...], (rows, heads)))
        mixed = expand(decay) * read + u * bc + skip * x
        gated = mixed * silu(total(0, mix) * inverse)
        inverse_gated = lax.rsqrt(jnp.mean(gated * gated, axis=1, keepdims=True) + eps)
        y = (gated * inverse_gated * gain_ref[...]).astype(bf16)
        for j in range(pieces):
            y_ref[j] = y

    return kernel


def mixer_step(arrived, lengths, tail_mix, tail_group, conv_mix, conv_group, bias_mix, bias_group,
               step_bias, decay_log, skip_gain, gate_gain, ssm_state, width_all):
    pieces, rows, width = arrived.shape
    _, heads, head_dim, state = ssm_state.shape
    mix = heads * head_dim
    taps = conv_mix.shape[0]
    args = (
        arrived, lengths[None], jnp.transpose(tail_mix, (1, 0, 2)), tail_group, conv_mix, conv_group,
        bias_mix[None], bias_group, step_bias[None], decay_log[None], skip_gain[None], gate_gain[None], in_hbm(ssm_state),
    )
    outs = (
        jax.ShapeDtypeStruct((pieces, rows, mix), bf16),
        jax.ShapeDtypeStruct((taps - 1, rows, mix), f32),
        jax.ShapeDtypeStruct((rows, taps - 1, 2, state), f32),
        jax.ShapeDtypeStruct((mix // LANES, rows, LANES), f32),
        jax.ShapeDtypeStruct((rows, LANES), f32),
        jax.ShapeDtypeStruct((rows, state), f32),
    )
    return pl.pallas_call(
        make_mixer_kernel(width_all, (pieces, rows, heads, head_dim, state, mix, taps)),
        in_specs=[IN_VMEM] * (len(args) - 1) + [pl.BlockSpec(memory_space=pl.ANY)],
        out_specs=[IN_VMEM] * len(outs),
        out_shape=outs,
        scratch_shapes=[
            pltpu.VMEM((rows, state), f32),
            pltpu.VMEM((mix, LANES), f32),
            pltpu.VMEM((rows, heads, head_dim, state), f32),
            pltpu.SemaphoreType.DMA((rows,)),
        ],
        compiler_params=SMALL,
        name="mixer_step",
    )(*args)


def make_update_kernel(per_step, heads, head_dim):
    def kernel(u_ref, decay_ref, b_ref, state_ref, out_ref):
        i = pl.program_id(0)
        for k in range(per_step):
            r = i * per_step + k
            b_row = b_ref[pl.ds(r, 1), :]
            d_col = jnp.transpose(jnp.broadcast_to(decay_ref[pl.ds(r, 1), :], (LANES, LANES)))
            for h in range(heads):
                at = h * head_dim
                if at % LANES == 0:
                    u_row = u_ref[at // LANES, pl.ds(r, 1), :]
                    u_col = jnp.transpose(jnp.broadcast_to(u_row, (LANES, LANES)))
                u_h = u_col[at % LANES : at % LANES + head_dim, :]
                out_ref[k, h] = state_ref[k, h] * d_col[h : h + 1, :] + u_h * b_row

    return kernel


def state_update(ssm_state, u, decay, b, per_step=2):
    rows, heads, head_dim, state = ssm_state.shape
    block = pl.BlockSpec((per_step, heads, head_dim, state), lambda i: (i, 0, 0, 0))
    return pl.pallas_call(
        make_update_kernel(per_step, heads, head_dim),
        grid=(rows // per_step,),
        in_specs=[IN_VMEM] * 3 + [block],
        out_specs=block,
        out_shape=jax.ShapeDtypeStruct(ssm_state.shape, f32),
        compiler_params=SMALL,
        name="state_update",
    )(u, decay, b, in_hbm(ssm_state))


def swap_core(value):
    return lax.ppermute(value, "c", [(0, 1), (1, 0)])


def ring_pairs(value, first):
    n = lax.axis_size("y")
    pairs = []
    for a in range(first, n + first, 2):
        p, q = a % n, (a + 1) % n
        pairs += [(p, q), (q, p)]
    return lax.ppermute(value, "y", pairs)


def head_sum_half(partial):
    half = partial.shape[0] // 2
    core = lax.axis_index("c")
    mine = lax.dynamic_slice_in_dim(partial, core * half, half, 0)
    theirs = lax.dynamic_slice_in_dim(partial, (1 - core) * half, half, 0).astype(bf16)
    total = mine + swap_core(theirs).astype(f32)
    for first in (0, 1):
        sent = total.astype(bf16)
        total = sent.astype(f32) + ring_pairs(sent, first).astype(f32)
    return total, core


def both_halves(half, core):
    other = swap_core(half)
    first = jnp.where(core == 0, half, other)
    second = jnp.where(core == 0, other, half)
    return jnp.concatenate([first, second], axis=0)


def add_over_heads(base, partial):
    total, core = head_sum_half(partial)
    half = total.shape[0]
    mine = lax.dynamic_slice_in_dim(base, core * half, half, 0).astype(f32)
    return both_halves((mine + total).astype(bf16), core)


def exchange(value, axis):
    return lax.all_to_all(value, axis, 0, 0, tiled=True)


def to_everyone(value, axis):
    peers = lax.axis_size(axis)
    copies = jnp.broadcast_to(value[None], (peers, *value.shape))
    return exchange(copies, axis).reshape(peers * value.shape[0], *value.shape[1:])


def on_device(
    residual, lengths, ssm_state, tail_mix, tail_group, norm_first, mix_weight, group_weight, step_weight,
    conv_mix, conv_group, bias_mix, bias_group, step_bias, decay_log, skip_gain, gate_gain, out_weight,
    norm_second, up_weight, down_weight,
):
    peers = lax.axis_size(REQ)
    rows_dev = ssm_state.shape[0]
    rows, width_dev = residual.shape
    width_all = width_dev * peers
    mix_flat = mix_weight.reshape(width_dev, -1)
    group_flat = group_weight.reshape(width_dev, -1)
    pieces = input_projection(residual, norm_first[None], mix_flat, group_flat, step_weight.T)
    arrived = exchange(pieces.reshape(peers, rows_dev, -1), REQ)
    copies, tail_mix_out, tail_group_out, u, decay, b = mixer_step(
        arrived, lengths, tail_mix, tail_group, conv_mix, conv_group, bias_mix, bias_group, step_bias,
        decay_log, skip_gain, gate_gain, ssm_state, width_all,
    )
    every_y = exchange(copies, REQ).reshape(rows, -1)
    state_out = state_update(ssm_state, u, decay, b)
    every_y, state_out = lax.optimization_barrier((every_y, state_out))
    middle = add_over_heads(residual, jnp.dot(every_y, out_weight, preferred_element_type=f32))
    wide = middle.astype(f32)
    scaled_two = (wide * norm_second).astype(bf16)
    activation = jnp.dot(scaled_two, up_weight, preferred_element_type=f32).astype(bf16)
    hidden_dev = up_weight.shape[1]
    total = jnp.sum(wide * wide, axis=1, keepdims=True)
    high = lax.reduce_precision(total, 8, 7)
    mid = lax.reduce_precision(total - high, 8, 7)
    low = total - high - mid
    lane = lax.broadcasted_iota(jnp.int32, (rows, LANES), 1)
    columns = jnp.where(lane == 0, high, jnp.where(lane == 1, mid, jnp.where(lane == 2, low, 0.0))).astype(bf16)
    sent = jnp.concatenate([activation, columns], axis=1).reshape(peers, rows_dev, hidden_dev + LANES)
    sums = exchange(sent, REQ).astype(f32).sum(axis=0)
    squares = sums[:, hidden_dev : hidden_dev + 1] + sums[:, hidden_dev + 1 : hidden_dev + 2] + sums[:, hidden_dev + 2 : hidden_dev + 3]
    inverse = lax.rsqrt(squares / width_all + eps)
    hidden = jnp.square(jax.nn.relu(sums[:, :hidden_dev] * inverse)).astype(bf16)
    every_hidden = to_everyone(hidden, REQ)
    residual_out = add_over_heads(middle, jnp.dot(every_hidden, down_weight, preferred_element_type=f32))
    return residual_out, state_out, jnp.transpose(tail_mix_out, (1, 0, 2)), tail_group_out


def solution(mesh):
    devices = mesh.devices
    finer = Mesh(devices.reshape(4, devices.shape[0] // 4, devices.shape[1] // 2, 2), REQ + HEAD)
    placed = (
        P(None, REQ),
        P(REQ),
        P(REQ, HEAD, None, None),
        P(REQ, None, HEAD),
        P(REQ, None, None, HEAD),
        P(REQ),
        P(REQ, None, HEAD),
        P(REQ, None, HEAD),
        P(REQ, HEAD),
        P(None, HEAD),
        P(None, None, HEAD),
        P(HEAD),
        P(None, HEAD),
        P(HEAD),
        P(HEAD),
        P(HEAD),
        P(HEAD),
        P(HEAD, REQ),
        P(REQ),
        P(REQ, HEAD),
        P(HEAD, REQ),
    )
    return jax.shard_map(
        on_device,
        mesh=finer,
        in_specs=placed,
        out_specs=(P(None, REQ), P(REQ, HEAD, None, None), P(REQ, None, HEAD), P(REQ, None, None, HEAD)),
        check_vma=False,
    )
```

time: 145 us -> 137 us (0.945)
  blocking collectives: 46.3 us -> 76.5 us
  waiting for transfers between devices: 39.7 us -> 11.7 us
  starting transfers between devices: 30.6 us -> 20.7 us
  Pallas kernels: 15.6 us -> 20.6 us
  local copies, waits for them, and re-layouts: 7.74 us -> 2.76 us
    all_to_all x2 -> x3, blocking collectives: 46.3 us -> 76.5 us  [exchange(): return lax.all_to_all(value, axis, 0, 0, tiled=True)]
    all_to_all x2 -> x1, waiting for transfers between devices: 28 us -> 0.01 us  [exchange(): return lax.all_to_all(value, axis, 0, 0, tiled=True)]
    all_to_all x2 -> x1, starting transfers between devices: 13.9 us -> 3.58 us  [exchange(): return lax.all_to_all(value, axis, 0, 0, tiled=True)]
    pallas_call x1 -> x2, Pallas kernels: 12.6 us -> 20.1 us  [the longest x1 10.1 us: state_update(): pl.pallas_call(make_update_kernel(per_step, heads, head_dim), grid=(rows...]
    unnamed x16 -> x38, local copies, waits for them, and re-layouts: 5.27 us -> 2.63 us
    pallas_call x1, Pallas kernels: 2.93 us -> 0.51 us  [input_projection(): pl.pallas_call(input_kernel, out_shape=jax.ShapeDtypeStruct((rows, width)...]
    broadcast_in_dim x2 -> x1, local copies, waits for them, and re-layouts: 1.76 us -> 0.09 us  [to_everyone(): copies = jnp.broadcast_to(value[None], (peers, *value.shape))]
  transfers between devices with their start and end apart: 10 -> 9, of which waited for: 10 -> 8; matrix products, arithmetic and copies ran while one was open for 0% -> 0% of each run, Pallas kernels for 0% -> 7%
where the time goes in v2:
time: 137 us
  blocking collectives  76.5 us (56%)
  starting transfers between devices  20.7 us (15%)
  Pallas kernels  20.6 us (15%)
  waiting for transfers between devices  11.7 us (9%)
  local copies, waits for them, and re-layouts  2.76 us (2%)
  other arithmetic  1.8 us (1%)
  matrix products  1.4 us (1%)
    all_to_all x3, blocking collectives, exchange(): return lax.all_to_all(value, axis, 0, 0, tiled=True)  76.5 us
    pallas_call x1, Pallas kernels, state_update(): pl.pallas_call(make_update_kernel(per_step, heads, head_dim), grid=(rows...  10.1 us
    pallas_call x1, Pallas kernels, mixer_step(): pl.pallas_call(make_mixer_kernel(width_all, (pieces, rows, heads, head_di...  9.98 us
    ppermute x4, starting transfers between devices, swap_core(): return lax.ppermute(value, 'c', [(0, 1), (1, 0)])  9.86 us
    ppermute x4, waiting for transfers between devices, ring_pairs(): return lax.ppermute(value, 'y', pairs)  8.14 us
    ppermute x4, starting transfers between devices, ring_pairs(): return lax.ppermute(value, 'y', pairs)  7.22 us
    ppermute x4, waiting for transfers between devices, swap_core(): return lax.ppermute(value, 'c', [(0, 1), (1, 0)])  3.6 us
    all_to_all x1, starting transfers between devices, exchange(): return lax.all_to_all(value, axis, 0, 0, tiled=True)  3.58 us
  transfers between devices with their start and end apart: 9, of which 8 were waited for; matrix products, arithmetic and copies ran while one was open for 0% of the time, Pallas kernels for 7%

profile of v2, /device:TPU:1, one launch (start us, length us, event | category | flops | bytes accessed | tf_op | source)
XLA Modules:
  0.0 136.5 jit_solution(17920820301809689353)
XLA Ops:
  0.7 1.0 copy.29
  1.7 1.5 %copy.26 = bf16[32,8,2,1024]{3,1,2,0:T(8,128)(2,1)S(1)} copy(bf16[32,8,2,1024]{3,2,1,0:T(2,128)(2,1)} %bitcast.40) | data formatting | bytes 2097152
  3.2 0.5 input_projection.1
  3.9 26.8 %all_to_all.20.arrived_ref = bf16[16,16,2432]{2,1,0:T(8,128)(2,1)S(1)} all-to-all(bf16[16,16,2432]{2,1,0:T(8,128)(2,1)S(1)} %bitcast.25), channel_id=1, replica_groups=mesh['z'=4,'x'=4,'y'=4,'c'=2] {'z','x'}, dimensions={0} | all-to-all | bytes 2490368 | tf_op jit(solution)/shard_map/all_to_all | solution.py:277
  30.8 10.0 %mixer_step.1 = (bf16[16,16,1024]{2,1,0:T(8,128)(2,1)}, f32[3,16,1024]{2,1,0:T(8,128)}, f32[16,3,2,128]{3,2,1,0:T(2,128)}, f32[8,16,128]{2,1,0:T(8,128)S(1)}, f3...) custom-call(bf16[16,16,2432]{2,1,0:T(8,128)(2,1)S(1)} %all_to_all.20.arrived_ref, s32[1,16]{1,0:T(1,128)S(1)} %bitcast.33, ...), custom_call_target="tpu_custom_call" | custom-call | tf_op jit(solution)/shard_map/mixer_step/pallas_call | solution.py:189
  40.8 3.6 %all-to-all-start.1 = ((bf16[16,16,1024]{2,1,0:T(8,128)(2,1)}), bf16[16,16,1024]{2,1,0:T(8,128)(2,1)S(1)}, u32[]{:S(2)}, u32[]{:S(2)}) async-start(bf16[16,16,1024]{2,1,0:T(8,128)(2,1)} %get-tuple-element.12), calls=%async_computation.1 | async-start | bytes 1048576 | tf_op jit(solution)/shard_map/all_to_all | solution.py:277
  44.4 10.1 %state_update.1 = f32[16,16,64,128]{3,2,1,0:T(8,128)} custom-call(f32[8,16,128]{2,1,0:T(8,128)S(1)} %get-tuple-element.13.u_ref, f32[16,128]{1,0:T(8,128)S(1)} %get-tuple-element.14.decay_ref, f32[16,128]{1,0:T(8,128)S(1)} %get-tuple-element.15.b_ref, f32[16,16,64,128]{3,2,1,0:T(8,128)} %state_ref.3), custom_call_target="tpu_custom_call" | custom-call | tf_op jit(solution)/shard_map/state_update/pallas_call | solution.py:226
  54.5 0.3 fusion.14
  54.8 2.4 %collective-permute-start = (bf16[128,256]{1,0:T(8,128)(2,1)S(1)}, bf16[128,256]{1,0:T(8,128)(2,1)S(1)}, u32[]{:S(2)}, u32[]{:S(2)}) collective-permute-start(bf16[128,256]{1,0:T(8,128)(2,1)S(1)} %dynamic-slice_convert_fusion.1), channel_id=1, source_target_pairs={{0,1},{1,0},{2,3},{3,2},{4,5},{5,4},{6,7},{7,6},{8,9},{9,8},{10,11... | collective-permute-start | bytes 196616 | tf_op jit(solution)/shard_map/ppermute | solution.py:238
  57.3 0.9 collective-permute-done
  58.2 1.4 %collective-permute-start.1 = (bf16[128,256]{1,0:T(8,128)(2,1)S(1)}, bf16[128,256]{1,0:T(8,128)(2,1)S(1)}, u32[]{:S(2)}, u32[]{:S(2)}) collective-permute-start(bf16[128,256]{1,0:T(8,128)(2,1)S(1)} %add_convert_fusion.5), channel_id=1, source_target_pairs={{0,2},{2,0},{4,6},{6,4},{1,3},{3,1},{5,7},{7,5},{8,10},{10,8},{12,... | collective-permute-start | bytes 196616 | tf_op jit(solution)/shard_map/ppermute | solution.py:247
  59.6 1.8 %collective-permute-done.1 = bf16[128,256]{1,0:T(8,128)(2,1)S(1)} collective-permute-done((bf16[128,256]{1,0:T(8,128)(2,1)S(1)}, bf16[128,256]{1,0:T(8,128)(2,1)S(1)}, u32[]{:S(2)}, u32[]{:S(2)}) %collective-permute-start.1) | collective-permute-done | bytes 65568 | tf_op jit(solution)/shard_map/ppermute | solution.py:247
  61.4 2.8 %collective-permute-start.2 = (bf16[128,256]{1,0:T(8,128)(2,1)S(1)}, bf16[128,256]{1,0:T(8,128)(2,1)S(1)}, u32[]{:S(2)}, u32[]{:S(2)}) collective-permute-start(bf16[128,256]{1,0:T(8,128)(2,1)S(1)} %add_convert_fusion.4), channel_id=1, source_target_pairs={{2,4},{4,2},{6,0},{0,6},{3,5},{5,3},{7,1},{1,7},{10,12},{12,10},{1... | collective-permute-start | bytes 196616 | tf_op jit(solution)/shard_map/ppermute | solution.py:247
  64.3 1.6 %collective-permute-done.2 = bf16[128,256]{1,0:T(8,128)(2,1)S(1)} collective-permute-done((bf16[128,256]{1,0:T(8,128)(2,1)S(1)}, bf16[128,256]{1,0:T(8,128)(2,1)S(1)}, u32[]{:S(2)}, u32[]{:S(2)}) %collective-permute-start.2) | collective-permute-done | bytes 65568 | tf_op jit(solution)/shard_map/ppermute | solution.py:247
  65.9 2.6 %collective-permute-start.3 = (bf16[128,256]{1,0:T(8,128)(2,1)S(1)}, bf16[128,256]{1,0:T(8,128)(2,1)S(1)}, u32[]{:S(2)}, u32[]{:S(2)}) collective-permute-start(bf16[128,256]{1,0:T(8,128)(2,1)S(1)} %add_convert_fusion.3), channel_id=1, source_target_pairs={{0,1},{1,0},{2,3},{3,2},{4,5},{5,4},{6,7},{7,6},{8,9},{9,8},{10,11... | collective-permute-start | bytes 196616 | tf_op jit(solution)/shard_map/ppermute | solution.py:238
  68.6 0.9 collective-permute-done.3
  69.6 0.6 convolution_convert_fusion
  70.2 0.2 select_convert_fusion
  70.5 26.8 %all_to_all.21 = bf16[16,16,2816]{2,1,0:T(8,128)(2,1)S(1)} all-to-all(bf16[16,16,2816]{2,1,0:T(8,128)(2,1)S(1)} %bitcast.37), channel_id=1, replica_groups=mesh['z'=4,'x'=4,'y'=4,'c'=2] {'z','x'}, dimensions={0} | all-to-all | bytes 2883584 | tf_op jit(solution)/shard_map/all_to_all | solution.py:277
  97.3 0.2 convert_reduce_fusion
  97.5 0.2 fusion.11
  97.9 22.9 %all_to_all.22 = bf16[16,16,2688]{2,1,0:T(8,128)(2,1)S(1)} all-to-all(bf16[16,16,2688]{2,1,0:T(8,128)(2,1)S(1)} %broadcast_in_dim.65), channel_id=1, replica_groups=mesh['z'=4,'x'=4,'y'=4,'c'=2] {'z','x'}, dimensions={0} | all-to-all | bytes 2752512 | tf_op jit(solution)/shard_map/all_to_all | solution.py:277
  120.8 0.5 fusion.15
  121.4 2.1 %collective-permute-start.4 = (bf16[128,256]{1,0:T(8,128)(2,1)S(1)}, bf16[128,256]{1,0:T(8,128)(2,1)S(1)}, u32[]{:S(2)}, u32[]{:S(2)}) collective-permute-start(bf16[128,256]{1,0:T(8,128)(2,1)S(1)} %dynamic-slice_convert_fusion), channel_id=1, source_target_pairs={{0,1},{1,0},{2,3},{3,2},{4,5},{5,4},{6,7},{7,6},{8,9},{9,8},{10,11... | collective-permute-start | bytes 196616 | tf_op jit(solution)/shard_map/ppermute | solution.py:238
  123.6 0.9 collective-permute-done.4
  124.5 0.2 collective-permute-start.5
  124.6 3.0 %collective-permute-done.5 = bf16[128,256]{1,0:T(8,128)(2,1)S(1)} collective-permute-done((bf16[128,256]{1,0:T(8,128)(2,1)S(1)}, bf16[128,256]{1,0:T(8,128)(2,1)S(1)}, u32[]{:S(2)}, u32[]{:S(2)}) %collective-permute-start.5) | collective-permute-done | bytes 65568 | tf_op jit(solution)/shard_map/ppermute | solution.py:247
  127.7 2.8 %collective-permute-start.6 = (bf16[128,256]{1,0:T(8,128)(2,1)S(1)}, bf16[128,256]{1,0:T(8,128)(2,1)S(1)}, u32[]{:S(2)}, u32[]{:S(2)}) collective-permute-start(bf16[128,256]{1,0:T(8,128)(2,1)S(1)} %add_convert_fusion.1), channel_id=1, source_target_pairs={{2,4},{4,2},{6,0},{0,6},{3,5},{5,3},{7,1},{1,7},{10,12},{12,10},{1... | collective-permute-start | bytes 196616 | tf_op jit(solution)/shard_map/ppermute | solution.py:247
  130.5 1.7 %collective-permute-done.6 = bf16[128,256]{1,0:T(8,128)(2,1)S(1)} collective-permute-done((bf16[128,256]{1,0:T(8,128)(2,1)S(1)}, bf16[128,256]{1,0:T(8,128)(2,1)S(1)}, u32[]{:S(2)}, u32[]{:S(2)}) %collective-permute-start.6) | collective-permute-done | bytes 65568 | tf_op jit(solution)/shard_map/ppermute | solution.py:247
  132.3 2.7 %collective-permute-start.7 = (bf16[128,256]{1,0:T(8,128)(2,1)S(1)}, bf16[128,256]{1,0:T(8,128)(2,1)S(1)}, u32[]{:S(2)}, u32[]{:S(2)}) collective-permute-start(bf16[128,256]{1,0:T(8,128)(2,1)S(1)} %add_convert_fusion), channel_id=1, source_target_pairs={{0,1},{1,0},{2,3},{3,2},{4,5},{5,4},{6,7},{7,6},{8,9},{9,8},{10,11... | collective-permute-start | bytes 196616 | tf_op jit(solution)/shard_map/ppermute | solution.py:238
  135.0 0.9 collective-permute-done.7
  135.9 0.7 pad_maximum_fusion.2
  (54 shorter events, 0.8 us)
Async XLA Ops:
  0.6 69.0 %copy-start = (bf16[256,2688]{1,0:T(8,128)(2,1)S(1)}, bf16[256,2688]{1,0:T(8,128)(2,1)}, u32[]{:S(2)}) copy-start(bf16[256,2688]{1,0:T(8,128)(2,1)} %param.40) | copy-start | bytes 4128772
  0.6 2.6 %copy-start.1 = (bf16[256,256]{1,0:T(8,128)(2,1)S(1)}, bf16[256,256]{1,0:T(8,128)(2,1)}, u32[]{:S(2)}) copy-start(bf16[256,256]{1,0:T(8,128)(2,1)} %residual_ref.1) | copy-start | bytes 393220
  0.7 2.6 %copy-start.5 = (bf16[256,16]{0,1:T(8,128)(2,1)S(1)}, bf16[256,16]{0,1:T(8,128)(2,1)}, u32[]{:S(2)}) copy-start(bf16[256,16]{0,1:T(8,128)(2,1)} %param.29) | copy-start | bytes 24580
  0.7 2.6 %copy-start.9 = (f32[256]{0:T(256)S(1)}, f32[256]{0:T(256)}, u32[]{:S(2)}) copy-start(f32[256]{0:T(256)} %param.26) | copy-start | bytes 3076
  3.8 26.9 %copy-start.2 = (f32[16,3,1024]{2,0,1:T(8,128)S(1)}, f32[16,3,1024]{2,0,1:T(8,128)}, u32[]{:S(2)}) copy-start(f32[16,3,1024]{2,0,1:T(8,128)} %param.24) | copy-start | bytes 589828
  3.8 26.9 %copy-start.3 = (f32[16,3,2,128]{3,2,1,0:T(2,128)S(1)}, f32[16,3,2,128]{3,2,1,0:T(2,128)}, u32[]{:S(2)}) copy-start(f32[16,3,2,128]{3,2,1,0:T(2,128)} %tail_group_ref.1) | copy-start | bytes 147460
  3.8 26.9 %copy-start.4 = (f32[4,1024]{1,0:T(4,128)S(1)}, f32[4,1024]{1,0:T(4,128)}, u32[]{:S(2)}) copy-start(f32[4,1024]{1,0:T(4,128)} %conv_mix_ref.1) | copy-start | bytes 49156
  3.8 26.9 %copy-start.6 = (f32[4,2,128]{2,1,0:T(2,128)S(1)}, f32[4,2,128]{2,1,0:T(2,128)}, u32[]{:S(2)}) copy-start(f32[4,2,128]{2,1,0:T(2,128)} %conv_group_ref.1) | copy-start | bytes 12292
  3.8 26.9 %copy-start.7 = (f32[1024]{0:T(1024)S(1)}, f32[1024]{0:T(1024)}, u32[]{:S(2)}) copy-start(f32[1024]{0:T(1024)} %param.32) | copy-start | bytes 12292
  3.8 26.9 %copy-start.8 = (f32[1024]{0:T(1024)S(1)}, f32[1024]{0:T(1024)}, u32[]{:S(2)}) copy-start(f32[1024]{0:T(1024)} %param.37) | copy-start | bytes 12292
  3.8 26.9 %copy-start.10 = (f32[2,128]{1,0:T(2,128)S(1)}, f32[2,128]{1,0:T(2,128)}, u32[]{:S(2)}) copy-start(f32[2,128]{1,0:T(2,128)} %bias_group_ref.1) | copy-start | bytes 3076
  3.8 26.9 %copy-start.11 = (s32[16]{0:T(128)S(1)}, s32[16]{0:T(128)}, u32[]{:S(2)}) copy-start(s32[16]{0:T(128)} %param.22) | copy-start | bytes 196
  3.9 26.9 %copy-start.12 = (f32[16]{0:T(128)S(1)}, f32[16]{0:T(128)}, u32[]{:S(2)}) copy-start(f32[16]{0:T(128)} %param.34) | copy-start | bytes 196
  3.9 26.9 %copy-start.13 = (f32[16]{0:T(128)S(1)}, f32[16]{0:T(128)}, u32[]{:S(2)}) copy-start(f32[16]{0:T(128)} %param.35) | copy-start | bytes 196
  3.9 26.9 %copy-start.14 = (f32[16]{0:T(128)S(1)}, f32[16]{0:T(128)}, u32[]{:S(2)}) copy-start(f32[16]{0:T(128)} %param.36) | copy-start | bytes 196
  40.8 13.7 %all-to-all-start.1 = ((bf16[16,16,1024]{2,1,0:T(8,128)(2,1)}), bf16[16,16,1024]{2,1,0:T(8,128)(2,1)S(1)}, u32[]{:S(2)}, u32[]{:S(2)}) async-start(bf16[16,16,1024]{2,1,0:T(8,128)(2,1)} %get-tuple-element.12), calls=%async_computation.1 | async-start | bytes 1048576 | tf_op jit(solution)/shard_map/all_to_all | solution.py:277
  44.4 10.1 %copy-start.16 = (bf16[1024,256]{1,0:T(8,128)(2,1)S(1)}, bf16[1024,256]{1,0:T(8,128)(2,1)}, u32[]{:S(2)}) copy-start(bf16[1024,256]{1,0:T(8,128)(2,1)} %param.38) | copy-start | bytes 1572868
  54.5 15.1 %copy-start.17 = (f32[256]{0:T(256)S(1)}, f32[256]{0:T(256)}, u32[]{:S(2)}) copy-start(f32[256]{0:T(256)} %param.39) | copy-start | bytes 3076
  54.8 3.3 %collective-permute-start = (bf16[128,256]{1,0:T(8,128)(2,1)S(1)}, bf16[128,256]{1,0:T(8,128)(2,1)S(1)}, u32[]{:S(2)}, u32[]{:S(2)}) collective-permute-start(bf16[128,256]{1,0:T(8,128)(2,1)S(1)} %dynamic-slice_convert_fusion.1), channel_id=1, source_target_pairs={{0,1},{1,0},{2,3},{3,2},{4,5},{5,4},{6,7},{7,6},{8,9},{9,8},{10,11... | collective-permute-start | bytes 196616 | tf_op jit(solution)/shard_map/ppermute | solution.py:238
  58.2 3.2 %collective-permute-start.1 = (bf16[128,256]{1,0:T(8,128)(2,1)S(1)}, bf16[128,256]{1,0:T(8,128)(2,1)S(1)}, u32[]{:S(2)}, u32[]{:S(2)}) collective-permute-start(bf16[128,256]{1,0:T(8,128)(2,1)S(1)} %add_convert_fusion.5), channel_id=1, source_target_pairs={{0,2},{2,0},{4,6},{6,4},{1,3},{3,1},{5,7},{7,5},{8,10},{10,8},{12,... | collective-permute-start | bytes 196616 | tf_op jit(solution)/shard_map/ppermute | solution.py:247
  61.4 4.5 %collective-permute-start.2 = (bf16[128,256]{1,0:T(8,128)(2,1)S(1)}, bf16[128,256]{1,0:T(8,128)(2,1)S(1)}, u32[]{:S(2)}, u32[]{:S(2)}) collective-permute-start(bf16[128,256]{1,0:T(8,128)(2,1)S(1)} %add_convert_fusion.4), channel_id=1, source_target_pairs={{2,4},{4,2},{6,0},{0,6},{3,5},{5,3},{7,1},{1,7},{10,12},{12,10},{1... | collective-permute-start | bytes 196616 | tf_op jit(solution)/shard_map/ppermute | solution.py:247
  65.9 3.5 %collective-permute-start.3 = (bf16[128,256]{1,0:T(8,128)(2,1)S(1)}, bf16[128,256]{1,0:T(8,128)(2,1)S(1)}, u32[]{:S(2)}, u32[]{:S(2)}) collective-permute-start(bf16[128,256]{1,0:T(8,128)(2,1)S(1)} %add_convert_fusion.3), channel_id=1, source_target_pairs={{0,1},{1,0},{2,3},{3,2},{4,5},{5,4},{6,7},{7,6},{8,9},{9,8},{10,11... | collective-permute-start | bytes 196616 | tf_op jit(solution)/shard_map/ppermute | solution.py:238
  97.9 22.9 %copy-start.15 = (bf16[2688,256]{1,0:T(8,128)(2,1)S(1)}, bf16[2688,256]{1,0:T(8,128)(2,1)}, u32[]{:S(2)}) copy-start(bf16[2688,256]{1,0:T(8,128)(2,1)} %param.41) | copy-start | bytes 4128772
  121.4 3.0 %collective-permute-start.4 = (bf16[128,256]{1,0:T(8,128)(2,1)S(1)}, bf16[128,256]{1,0:T(8,128)(2,1)S(1)}, u32[]{:S(2)}, u32[]{:S(2)}) collective-permute-start(bf16[128,256]{1,0:T(8,128)(2,1)S(1)} %dynamic-slice_convert_fusion), channel_id=1, source_target_pairs={{0,1},{1,0},{2,3},{3,2},{4,5},{5,4},{6,7},{7,6},{8,9},{9,8},{10,11... | collective-permute-start | bytes 196616 | tf_op jit(solution)/shard_map/ppermute | solution.py:238
  124.5 3.2 %collective-permute-start.5 = (bf16[128,256]{1,0:T(8,128)(2,1)S(1)}, bf16[128,256]{1,0:T(8,128)(2,1)S(1)}, u32[]{:S(2)}, u32[]{:S(2)}) collective-permute-start(bf16[128,256]{1,0:T(8,128)(2,1)S(1)} %add_convert_fusion.2), channel_id=1, source_target_pairs={{0,2},{2,0},{4,6},{6,4},{1,3},{3,1},{5,7},{7,5},{8,10},{10,8},{12,... | collective-permute-start | bytes 196616 | tf_op jit(solution)/shard_map/ppermute | solution.py:247
  127.7 4.5 %collective-permute-start.6 = (bf16[128,256]{1,0:T(8,128)(2,1)S(1)}, bf16[128,256]{1,0:T(8,128)(2,1)S(1)}, u32[]{:S(2)}, u32[]{:S(2)}) collective-permute-start(bf16[128,256]{1,0:T(8,128)(2,1)S(1)} %add_convert_fusion.1), channel_id=1, source_target_pairs={{2,4},{4,2},{6,0},{0,6},{3,5},{5,3},{7,1},{1,7},{10,12},{12,10},{1... | collective-permute-start | bytes 196616 | tf_op jit(solution)/shard_map/ppermute | solution.py:247
  132.3 3.6 %collective-permute-start.7 = (bf16[128,256]{1,0:T(8,128)(2,1)S(1)}, bf16[128,256]{1,0:T(8,128)(2,1)S(1)}, u32[]{:S(2)}, u32[]{:S(2)}) collective-permute-start(bf16[128,256]{1,0:T(8,128)(2,1)S(1)} %add_convert_fusion), channel_id=1, source_target_pairs={{0,1},{1,0},{2,3},{3,2},{4,5},{5,4},{6,7},{7,6},{8,9},{9,8},{10,11... | collective-permute-start | bytes 196616 | tf_op jit(solution)/shard_map/ppermute | solution.py:238

commit v3 on v2

--- a/solution.py
+++ b/solution.py
@@ -84,13 +84,16 @@
         arrived_ref, lengths_ref, tail_mix_ref, tail_group_ref, conv_mix_ref, conv_group_ref,
         bias_mix_ref, bias_group_ref, step_bias_ref, decay_log_ref, skip_ref, gain_ref, state_ref,
         y_ref, tail_mix_out_ref, tail_group_out_ref, u_ref, decay_ref, b_ref,
-        c_ref, read_ref, buffer_ref, sems,
+        c_ref, columns_ref, read_ref, buffer_ref, sems,
     ):
         def fetch(r):
             return pltpu.make_async_copy(state_ref.at[r], buffer_ref.at[r], sems.at[r])
 
-        for r in range(rows):
+        def begin(r, carry):
             fetch(r).start()
+            return carry
+
+        lax.fori_loop(0, rows, begin, 0)
         spread = expander(heads, mix, head_dim)
 
         def expand(v):
@@ -139,23 +142,32 @@
         u = expand(step_size) * x
         for t in range(mix // LANES):
             u_ref[t] = u[:, t * LANES : (t + 1) * LANES]
-        lane = lax.broadcasted_iota(jnp.int32, (head_dim, LANES), 1)
-        for first in range(0, rows, BATCH):
-            for r in range(first, first + BATCH):
+        c = c_ref[...]
+        c_high = c.astype(bf16).astype(f32)
+        both = jnp.concatenate([c_high, c - c_high, jnp.zeros((LANES - 2 * rows, state), f32)], axis=0)
+        columns_ref[...] = jnp.transpose(both)
+        read_ref[...] = jnp.zeros_like(read_ref)
+        lane = lax.broadcasted_iota(jnp.int32, (state, LANES), 1)
+
+        def some_rows(i, carry):
+            left = []
+            right = []
+            for k in range(BATCH):
+                r = i * BATCH + k
                 fetch(r).wait()
-
-            def one_head(h, carry, first=first):
-                at = pl.ds(pl.multiple_of(h * head_dim, head_dim), head_dim)
-                acc = jnp.zeros((head_dim, LANES), f32) if first == 0 else read_ref[at, :]
-                for r in range(first, first + BATCH):
-                    part = jnp.sum(buffer_ref[r, h] * c_ref[r : r + 1, :], axis=1, keepdims=True)
-                    acc = jnp.where(lane == r, part, acc)
-                read_ref[at, :] = acc
-                return carry
-
-            lax.fori_loop(0, heads, one_head, 0)
-
-        read = jnp.transpose(read_ref[...])[:rows, :]
+                s = buffer_ref[r].reshape(mix, state)
+                s_high = s.astype(bf16)
+                left += [s_high, (s - s_high.astype(f32)).astype(bf16)]
+                own = jnp.where(lane % rows == r, columns_ref[...], 0.0).astype(bf16)
+                right += [own, own]
+            read_ref[...] += jnp.dot(
+                jnp.concatenate(left, axis=1), jnp.concatenate(right, axis=0), preferred_element_type=f32
+            )
+            return carry
+
+        lax.fori_loop(0, rows // BATCH, some_rows, 0)
+        across_read = jnp.transpose(read_ref[...])
+        read = across_read[:rows, :] + across_read[rows : 2 * rows, :]
         bc = jnp.sum(b_ref[...] * c_ref[...], axis=1, keepdims=True)
         skip = expand(jnp.broadcast_to(skip_ref[...], (rows, heads)))
         mixed = expand(decay) * read + u * bc + skip * x
@@ -193,6 +205,7 @@
         out_shape=outs,
         scratch_shapes=[
             pltpu.VMEM((rows, state), f32),
+            pltpu.VMEM((state, LANES), f32),
             pltpu.VMEM((mix, LANES), f32),
             pltpu.VMEM((rows, heads, head_dim, state), f32),
             pltpu.SemaphoreType.DMA((rows,)),
@@ -202,11 +215,22 @@
     )(*args)
 
 
-def make_update_kernel(per_step, heads, head_dim):
-    def kernel(u_ref, decay_ref, b_ref, state_ref, out_ref):
-        i = pl.program_id(0)
-        for k in range(per_step):
-            r = i * per_step + k
+def make_update_kernel(rows, heads, head_dim, state):
+    def kernel(u_ref, decay_ref, b_ref, state_ref, out_ref, buffer_ref, arrivals, departures):
+        def fetch(r):
+            return pltpu.make_async_copy(state_ref.at[r], buffer_ref.at[r], arrivals.at[r])
+
+        def leave(r):
+            return pltpu.make_async_copy(buffer_ref.at[r], out_ref.at[r], departures.at[r])
+
+        def begin(r, carry):
+            fetch(r).start()
+            return carry
+
+        lax.fori_loop(0, rows, begin, 0)
+
+        def one_row(r, carry):
+            fetch(r).wait()
             b_row = b_ref[pl.ds(r, 1), :]
             d_col = jnp.transpose(jnp.broadcast_to(decay_ref[pl.ds(r, 1), :], (LANES, LANES)))
             for h in range(heads):
@@ -215,20 +239,33 @@
                     u_row = u_ref[at // LANES, pl.ds(r, 1), :]
                     u_col = jnp.transpose(jnp.broadcast_to(u_row, (LANES, LANES)))
                 u_h = u_col[at % LANES : at % LANES + head_dim, :]
-                out_ref[k, h] = state_ref[k, h] * d_col[h : h + 1, :] + u_h * b_row
+                buffer_ref[r, h] = buffer_ref[r, h] * d_col[h : h + 1, :] + u_h * b_row
+            leave(r).start()
+            return carry
+
+        lax.fori_loop(0, rows, one_row, 0)
+
+        def finish(r, carry):
+            leave(r).wait()
+            return carry
+
+        lax.fori_loop(0, rows, finish, 0)
 
     return kernel
 
 
-def state_update(ssm_state, u, decay, b, per_step=2):
+def state_update(ssm_state, u, decay, b):
     rows, heads, head_dim, state = ssm_state.shape
-    block = pl.BlockSpec((per_step, heads, head_dim, state), lambda i: (i, 0, 0, 0))
     return pl.pallas_call(
-        make_update_kernel(per_step, heads, head_dim),
-        grid=(rows // per_step,),
-        in_specs=[IN_VMEM] * 3 + [block],
-        out_specs=block,
+        make_update_kernel(rows, heads, head_dim, state),
+        in_specs=[IN_VMEM] * 3 + [pl.BlockSpec(memory_space=pl.ANY)],
+        out_specs=pl.BlockSpec(memory_space=pl.ANY),
         out_shape=jax.ShapeDtypeStruct(ssm_state.shape, f32),
+        scratch_shapes=[
+            pltpu.VMEM(ssm_state.shape, f32),
+            pltpu.SemaphoreType.DMA((rows,)),
+            pltpu.SemaphoreType.DMA((rows,)),
+        ],
         compiler_params=SMALL,
         name="state_update",
     )(u, decay, b, in_hbm(ssm_state))

time: 137 us -> 130 us (0.949)
  Pallas kernels: 20.6 us -> 13.9 us
  waiting for transfers between devices: 11.7 us -> 14.8 us
  blocking collectives: 76.5 us -> 73.4 us
    pallas_call x1, Pallas kernels: 9.98 us -> 6.4 us  [mixer_step(): pl.pallas_call(make_mixer_kernel(width_all, (pieces, rows, heads, head_di...]
    pallas_call x1, Pallas kernels: 10.1 us -> 6.98 us  [state_update(): pl.pallas_call(make_update_kernel(rows, heads, head_dim, state), in_specs...]
    all_to_all x3, blocking collectives: 76.5 us -> 73.4 us  [exchange(): return lax.all_to_all(value, axis, 0, 0, tiled=True)]
    all_to_all x1, waiting for transfers between devices: 0.01 us -> 2.98 us  [exchange(): return lax.all_to_all(value, axis, 0, 0, tiled=True)]
  transfers between devices with their start and end apart: 9 -> 9, of which waited for: 8 -> 9; matrix products, arithmetic and copies ran while one was open for 0% -> 0% of each run, Pallas kernels for 7% -> 5%
where the time goes in v3:
time: 130 us
  blocking collectives  73.4 us (56%)
  starting transfers between devices  20.8 us (16%)
  waiting for transfers between devices  14.8 us (11%)
  Pallas kernels  13.9 us (11%)
  local copies, waits for them, and re-layouts  2.76 us (2%)
  other arithmetic  1.8 us (1%)
  matrix products  1.39 us (1%)
    all_to_all x3, blocking collectives, exchange(): return lax.all_to_all(value, axis, 0, 0, tiled=True)  73.4 us
    ppermute x4, starting transfers between devices, swap_core(): return lax.ppermute(value, 'c', [(0, 1), (1, 0)])  9.99 us
    ppermute x4, waiting for transfers between devices, ring_pairs(): return lax.ppermute(value, 'y', pairs)  8.18 us
    ppermute x4, starting transfers between devices, ring_pairs(): return lax.ppermute(value, 'y', pairs)  7.21 us
    pallas_call x1, Pallas kernels, state_update(): pl.pallas_call(make_update_kernel(rows, heads, head_dim, state), in_specs...  6.98 us
    pallas_call x1, Pallas kernels, mixer_step(): pl.pallas_call(make_mixer_kernel(width_all, (pieces, rows, heads, head_di...  6.4 us
    ppermute x4, waiting for transfers between devices, swap_core(): return lax.ppermute(value, 'c', [(0, 1), (1, 0)])  3.6 us
    all_to_all x1, starting transfers between devices, exchange(): return lax.all_to_all(value, axis, 0, 0, tiled=True)  3.58 us
  transfers between devices with their start and end apart: 9, of which 9 were waited for; matrix products, arithmetic and copies ran while one was open for 0% of the time, Pallas kernels for 5%

profile of v3, /device:TPU:1, one launch (start us, length us, event | category | flops | bytes accessed | tf_op | source)
XLA Modules:
  0.0 129.9 jit_solution(5720255928739338071)
XLA Ops:
  0.7 1.0 copy.29
  1.7 1.5 %copy.26 = bf16[32,8,2,1024]{3,1,2,0:T(8,128)(2,1)S(1)} copy(bf16[32,8,2,1024]{3,2,1,0:T(2,128)(2,1)} %bitcast.40) | data formatting | bytes 2097152
  3.2 0.5 input_projection.1
  3.9 26.8 %all_to_all.20.arrived_ref = bf16[16,16,2432]{2,1,0:T(8,128)(2,1)S(1)} all-to-all(bf16[16,16,2432]{2,1,0:T(8,128)(2,1)S(1)} %bitcast.25), channel_id=1, replica_groups=mesh['z'=4,'x'=4,'y'=4,'c'=2] {'z','x'}, dimensions={0} | all-to-all | bytes 2490368 | tf_op jit(solution)/shard_map/all_to_all | solution.py:314
  30.8 6.4 %mixer_step.1 = (bf16[16,16,1024]{2,1,0:T(8,128)(2,1)}, f32[3,16,1024]{2,1,0:T(8,128)}, f32[16,3,2,128]{3,2,1,0:T(2,128)}, f32[8,16,128]{2,1,0:T(8,128)S(1)}, f3...) custom-call(bf16[16,16,2432]{2,1,0:T(8,128)(2,1)S(1)} %all_to_all.20.arrived_ref, s32[1,16]{1,0:T(1,128)S(1)} %bitcast.33, ...), custom_call_target="tpu_custom_call" | custom-call | tf_op jit(solution)/shard_map/mixer_step/pallas_call | solution.py:201
  37.2 3.6 %all-to-all-start.1 = ((bf16[16,16,1024]{2,1,0:T(8,128)(2,1)}), bf16[16,16,1024]{2,1,0:T(8,128)(2,1)S(1)}, u32[]{:S(2)}, u32[]{:S(2)}) async-start(bf16[16,16,1024]{2,1,0:T(8,128)(2,1)} %get-tuple-element.12), calls=%async_computation.1 | async-start | bytes 1048576 | tf_op jit(solution)/shard_map/all_to_all | solution.py:314
  40.8 7.0 %state_update.1 = f32[16,16,64,128]{3,2,1,0:T(8,128)} custom-call(f32[8,16,128]{2,1,0:T(8,128)S(1)} %get-tuple-element.13.u_ref, f32[16,128]{1,0:T(8,128)S(1)} %get-tuple-element.14.decay_ref, f32[16,128]{1,0:T(8,128)S(1)} %get-tuple-element.15.b_ref, f32[16,16,64,128]{3,2,1,0:T(8,128)} %state_ref.3), custom_call_target="tpu_custom_call" | custom-call | tf_op jit(solution)/shard_map/state_update/pallas_call | solution.py:259
  47.8 3.0 %all-to-all-done.1 = bf16[16,16,1024]{2,1,0:T(8,128)(2,1)S(1)} async-done(((bf16[16,16,1024]{2,1,0:T(8,128)(2,1)}), bf16[16,16,1024]{2,1,0:T(8,128)(2,1)S(1)}, u32[]{:S(2)}, u32[]{:S(2)}) %all-to-all-start.1) | async-done | bytes 524320 | tf_op jit(solution)/shard_map/all_to_all | solution.py:314
  50.8 0.3 fusion.14
  51.1 2.6 %collective-permute-start = (bf16[128,256]{1,0:T(8,128)(2,1)S(1)}, bf16[128,256]{1,0:T(8,128)(2,1)S(1)}, u32[]{:S(2)}, u32[]{:S(2)}) collective-permute-start(bf16[128,256]{1,0:T(8,128)(2,1)S(1)} %dynamic-slice_convert_fusion.1), channel_id=1, source_target_pairs={{0,1},{1,0},{2,3},{3,2},{4,5},{5,4},{6,7},{7,6},{8,9},{9,8},{10,11... | collective-permute-start | bytes 196616 | tf_op jit(solution)/shard_map/ppermute | solution.py:275
  53.7 0.9 collective-permute-done
  54.6 1.4 %collective-permute-start.1 = (bf16[128,256]{1,0:T(8,128)(2,1)S(1)}, bf16[128,256]{1,0:T(8,128)(2,1)S(1)}, u32[]{:S(2)}, u32[]{:S(2)}) collective-permute-start(bf16[128,256]{1,0:T(8,128)(2,1)S(1)} %add_convert_fusion.5), channel_id=1, source_target_pairs={{0,2},{2,0},{4,6},{6,4},{1,3},{3,1},{5,7},{7,5},{8,10},{10,8},{12,... | collective-permute-start | bytes 196616 | tf_op jit(solution)/shard_map/ppermute | solution.py:284
  56.0 1.8 %collective-permute-done.1 = bf16[128,256]{1,0:T(8,128)(2,1)S(1)} collective-permute-done((bf16[128,256]{1,0:T(8,128)(2,1)S(1)}, bf16[128,256]{1,0:T(8,128)(2,1)S(1)}, u32[]{:S(2)}, u32[]{:S(2)}) %collective-permute-start.1) | collective-permute-done | bytes 65568 | tf_op jit(solution)/shard_map/ppermute | solution.py:284
  57.8 2.9 %collective-permute-start.2 = (bf16[128,256]{1,0:T(8,128)(2,1)S(1)}, bf16[128,256]{1,0:T(8,128)(2,1)S(1)}, u32[]{:S(2)}, u32[]{:S(2)}) collective-permute-start(bf16[128,256]{1,0:T(8,128)(2,1)S(1)} %add_convert_fusion.4), channel_id=1, source_target_pairs={{2,4},{4,2},{6,0},{0,6},{3,5},{5,3},{7,1},{1,7},{10,12},{12,10},{1... | collective-permute-start | bytes 196616 | tf_op jit(solution)/shard_map/ppermute | solution.py:284
  60.7 1.6 %collective-permute-done.2 = bf16[128,256]{1,0:T(8,128)(2,1)S(1)} collective-permute-done((bf16[128,256]{1,0:T(8,128)(2,1)S(1)}, bf16[128,256]{1,0:T(8,128)(2,1)S(1)}, u32[]{:S(2)}, u32[]{:S(2)}) %collective-permute-start.2) | collective-permute-done | bytes 65568 | tf_op jit(solution)/shard_map/ppermute | solution.py:284
  62.4 2.6 %collective-permute-start.3 = (bf16[128,256]{1,0:T(8,128)(2,1)S(1)}, bf16[128,256]{1,0:T(8,128)(2,1)S(1)}, u32[]{:S(2)}, u32[]{:S(2)}) collective-permute-start(bf16[128,256]{1,0:T(8,128)(2,1)S(1)} %add_convert_fusion.3), channel_id=1, source_target_pairs={{0,1},{1,0},{2,3},{3,2},{4,5},{5,4},{6,7},{7,6},{8,9},{9,8},{10,11... | collective-permute-start | bytes 196616 | tf_op jit(solution)/shard_map/ppermute | solution.py:275
  65.0 0.9 collective-permute-done.3
  66.1 0.6 convolution_convert_fusion
  66.6 0.2 select_convert_fusion
  66.9 23.7 %all_to_all.21 = bf16[16,16,2816]{2,1,0:T(8,128)(2,1)S(1)} all-to-all(bf16[16,16,2816]{2,1,0:T(8,128)(2,1)S(1)} %bitcast.37), channel_id=1, replica_groups=mesh['z'=4,'x'=4,'y'=4,'c'=2] {'z','x'}, dimensions={0} | all-to-all | bytes 2883584 | tf_op jit(solution)/shard_map/all_to_all | solution.py:314
  90.7 0.2 convert_reduce_fusion
  90.9 0.2 fusion.11
  91.3 22.9 %all_to_all.22 = bf16[16,16,2688]{2,1,0:T(8,128)(2,1)S(1)} all-to-all(bf16[16,16,2688]{2,1,0:T(8,128)(2,1)S(1)} %broadcast_in_dim.65), channel_id=1, replica_groups=mesh['z'=4,'x'=4,'y'=4,'c'=2] {'z','x'}, dimensions={0} | all-to-all | bytes 2752512 | tf_op jit(solution)/shard_map/all_to_all | solution.py:314
  114.2 0.5 fusion.15
  114.7 2.1 %collective-permute-start.4 = (bf16[128,256]{1,0:T(8,128)(2,1)S(1)}, bf16[128,256]{1,0:T(8,128)(2,1)S(1)}, u32[]{:S(2)}, u32[]{:S(2)}) collective-permute-start(bf16[128,256]{1,0:T(8,128)(2,1)S(1)} %dynamic-slice_convert_fusion), channel_id=1, source_target_pairs={{0,1},{1,0},{2,3},{3,2},{4,5},{5,4},{6,7},{7,6},{8,9},{9,8},{10,11... | collective-permute-start | bytes 196616 | tf_op jit(solution)/shard_map/ppermute | solution.py:275
  116.9 0.9 collective-permute-done.4
  117.9 3.1 %collective-permute-done.5 = bf16[128,256]{1,0:T(8,128)(2,1)S(1)} collective-permute-done((bf16[128,256]{1,0:T(8,128)(2,1)S(1)}, bf16[128,256]{1,0:T(8,128)(2,1)S(1)}, u32[]{:S(2)}, u32[]{:S(2)}) %collective-permute-start.5) | collective-permute-done | bytes 65568 | tf_op jit(solution)/shard_map/ppermute | solution.py:284
  121.0 2.8 %collective-permute-start.6 = (bf16[128,256]{1,0:T(8,128)(2,1)S(1)}, bf16[128,256]{1,0:T(8,128)(2,1)S(1)}, u32[]{:S(2)}, u32[]{:S(2)}) collective-permute-start(bf16[128,256]{1,0:T(8,128)(2,1)S(1)} %add_convert_fusion.1), channel_id=1, source_target_pairs={{2,4},{4,2},{6,0},{0,6},{3,5},{5,3},{7,1},{1,7},{10,12},{12,10},{1... | collective-permute-start | bytes 196616 | tf_op jit(solution)/shard_map/ppermute | solution.py:284
  123.8 1.7 %collective-permute-done.6 = bf16[128,256]{1,0:T(8,128)(2,1)S(1)} collective-permute-done((bf16[128,256]{1,0:T(8,128)(2,1)S(1)}, bf16[128,256]{1,0:T(8,128)(2,1)S(1)}, u32[]{:S(2)}, u32[]{:S(2)}) %collective-permute-start.6) | collective-permute-done | bytes 65568 | tf_op jit(solution)/shard_map/ppermute | solution.py:284
  125.6 2.7 %collective-permute-start.7 = (bf16[128,256]{1,0:T(8,128)(2,1)S(1)}, bf16[128,256]{1,0:T(8,128)(2,1)S(1)}, u32[]{:S(2)}, u32[]{:S(2)}) collective-permute-start(bf16[128,256]{1,0:T(8,128)(2,1)S(1)} %add_convert_fusion), channel_id=1, source_target_pairs={{0,1},{1,0},{2,3},{3,2},{4,5},{5,4},{6,7},{7,6},{8,9},{9,8},{10,11... | collective-permute-start | bytes 196616 | tf_op jit(solution)/shard_map/ppermute | solution.py:275
  128.3 0.9 collective-permute-done.7
  129.2 0.7 pad_maximum_fusion.2
  (54 shorter events, 1.0 us)
Async XLA Ops:
  0.6 65.4 %copy-start = (bf16[256,2688]{1,0:T(8,128)(2,1)S(1)}, bf16[256,2688]{1,0:T(8,128)(2,1)}, u32[]{:S(2)}) copy-start(bf16[256,2688]{1,0:T(8,128)(2,1)} %param.40) | copy-start | bytes 4128772
  0.6 2.6 %copy-start.1 = (bf16[256,256]{1,0:T(8,128)(2,1)S(1)}, bf16[256,256]{1,0:T(8,128)(2,1)}, u32[]{:S(2)}) copy-start(bf16[256,256]{1,0:T(8,128)(2,1)} %residual_ref.1) | copy-start | bytes 393220
  0.7 2.6 %copy-start.5 = (bf16[256,16]{0,1:T(8,128)(2,1)S(1)}, bf16[256,16]{0,1:T(8,128)(2,1)}, u32[]{:S(2)}) copy-start(bf16[256,16]{0,1:T(8,128)(2,1)} %param.29) | copy-start | bytes 24580
  0.7 2.6 %copy-start.9 = (f32[256]{0:T(256)S(1)}, f32[256]{0:T(256)}, u32[]{:S(2)}) copy-start(f32[256]{0:T(256)} %param.26) | copy-start | bytes 3076
  3.8 26.9 %copy-start.2 = (f32[16,3,1024]{2,0,1:T(8,128)S(1)}, f32[16,3,1024]{2,0,1:T(8,128)}, u32[]{:S(2)}) copy-start(f32[16,3,1024]{2,0,1:T(8,128)} %param.24) | copy-start | bytes 589828
  3.8 26.9 %copy-start.3 = (f32[16,3,2,128]{3,2,1,0:T(2,128)S(1)}, f32[16,3,2,128]{3,2,1,0:T(2,128)}, u32[]{:S(2)}) copy-start(f32[16,3,2,128]{3,2,1,0:T(2,128)} %tail_group_ref.1) | copy-start | bytes 147460
  3.8 26.9 %copy-start.4 = (f32[4,1024]{1,0:T(4,128)S(1)}, f32[4,1024]{1,0:T(4,128)}, u32[]{:S(2)}) copy-start(f32[4,1024]{1,0:T(4,128)} %conv_mix_ref.1) | copy-start | bytes 49156
  3.8 26.9 %copy-start.6 = (f32[4,2,128]{2,1,0:T(2,128)S(1)}, f32[4,2,128]{2,1,0:T(2,128)}, u32[]{:S(2)}) copy-start(f32[4,2,128]{2,1,0:T(2,128)} %conv_group_ref.1) | copy-start | bytes 12292
  3.8 26.9 %copy-start.7 = (f32[1024]{0:T(1024)S(1)}, f32[1024]{0:T(1024)}, u32[]{:S(2)}) copy-start(f32[1024]{0:T(1024)} %param.32) | copy-start | bytes 12292
  3.8 26.9 %copy-start.8 = (f32[1024]{0:T(1024)S(1)}, f32[1024]{0:T(1024)}, u32[]{:S(2)}) copy-start(f32[1024]{0:T(1024)} %param.37) | copy-start | bytes 12292
  3.8 26.9 %copy-start.10 = (f32[2,128]{1,0:T(2,128)S(1)}, f32[2,128]{1,0:T(2,128)}, u32[]{:S(2)}) copy-start(f32[2,128]{1,0:T(2,128)} %bias_group_ref.1) | copy-start | bytes 3076
  3.8 26.9 %copy-start.11 = (s32[16]{0:T(128)S(1)}, s32[16]{0:T(128)}, u32[]{:S(2)}) copy-start(s32[16]{0:T(128)} %param.22) | copy-start | bytes 196
  3.9 26.9 %copy-start.12 = (f32[16]{0:T(128)S(1)}, f32[16]{0:T(128)}, u32[]{:S(2)}) copy-start(f32[16]{0:T(128)} %param.34) | copy-start | bytes 196
  3.9 26.9 %copy-start.13 = (f32[16]{0:T(128)S(1)}, f32[16]{0:T(128)}, u32[]{:S(2)}) copy-start(f32[16]{0:T(128)} %param.35) | copy-start | bytes 196
  3.9 26.9 %copy-start.14 = (f32[16]{0:T(128)S(1)}, f32[16]{0:T(128)}, u32[]{:S(2)}) copy-start(f32[16]{0:T(128)} %param.36) | copy-start | bytes 196
  37.2 13.6 %all-to-all-start.1 = ((bf16[16,16,1024]{2,1,0:T(8,128)(2,1)}), bf16[16,16,1024]{2,1,0:T(8,128)(2,1)S(1)}, u32[]{:S(2)}, u32[]{:S(2)}) async-start(bf16[16,16,1024]{2,1,0:T(8,128)(2,1)} %get-tuple-element.12), calls=%async_computation.1 | async-start | bytes 1048576 | tf_op jit(solution)/shard_map/all_to_all | solution.py:314
  40.8 10.0 %copy-start.16 = (bf16[1024,256]{1,0:T(8,128)(2,1)S(1)}, bf16[1024,256]{1,0:T(8,128)(2,1)}, u32[]{:S(2)}) copy-start(bf16[1024,256]{1,0:T(8,128)(2,1)} %param.38) | copy-start | bytes 1572868
  47.8 18.3 %copy-start.17 = (f32[256]{0:T(256)S(1)}, f32[256]{0:T(256)}, u32[]{:S(2)}) copy-start(f32[256]{0:T(256)} %param.39) | copy-start | bytes 3076
  51.1 3.5 %collective-permute-start = (bf16[128,256]{1,0:T(8,128)(2,1)S(1)}, bf16[128,256]{1,0:T(8,128)(2,1)S(1)}, u32[]{:S(2)}, u32[]{:S(2)}) collective-permute-start(bf16[128,256]{1,0:T(8,128)(2,1)S(1)} %dynamic-slice_convert_fusion.1), channel_id=1, source_target_pairs={{0,1},{1,0},{2,3},{3,2},{4,5},{5,4},{6,7},{7,6},{8,9},{9,8},{10,11... | collective-permute-start | bytes 196616 | tf_op jit(solution)/shard_map/ppermute | solution.py:275
  54.6 3.2 %collective-permute-start.1 = (bf16[128,256]{1,0:T(8,128)(2,1)S(1)}, bf16[128,256]{1,0:T(8,128)(2,1)S(1)}, u32[]{:S(2)}, u32[]{:S(2)}) collective-permute-start(bf16[128,256]{1,0:T(8,128)(2,1)S(1)} %add_convert_fusion.5), channel_id=1, source_target_pairs={{0,2},{2,0},{4,6},{6,4},{1,3},{3,1},{5,7},{7,5},{8,10},{10,8},{12,... | collective-permute-start | bytes 196616 | tf_op jit(solution)/shard_map/ppermute | solution.py:284
  57.8 4.5 %collective-permute-start.2 = (bf16[128,256]{1,0:T(8,128)(2,1)S(1)}, bf16[128,256]{1,0:T(8,128)(2,1)S(1)}, u32[]{:S(2)}, u32[]{:S(2)}) collective-permute-start(bf16[128,256]{1,0:T(8,128)(2,1)S(1)} %add_convert_fusion.4), channel_id=1, source_target_pairs={{2,4},{4,2},{6,0},{0,6},{3,5},{5,3},{7,1},{1,7},{10,12},{12,10},{1... | collective-permute-start | bytes 196616 | tf_op jit(solution)/shard_map/ppermute | solution.py:284
  62.4 3.5 %collective-permute-start.3 = (bf16[128,256]{1,0:T(8,128)(2,1)S(1)}, bf16[128,256]{1,0:T(8,128)(2,1)S(1)}, u32[]{:S(2)}, u32[]{:S(2)}) collective-permute-start(bf16[128,256]{1,0:T(8,128)(2,1)S(1)} %add_convert_fusion.3), channel_id=1, source_target_pairs={{0,1},{1,0},{2,3},{3,2},{4,5},{5,4},{6,7},{7,6},{8,9},{9,8},{10,11... | collective-permute-start | bytes 196616 | tf_op jit(solution)/shard_map/ppermute | solution.py:275
  91.3 22.9 %copy-start.15 = (bf16[2688,256]{1,0:T(8,128)(2,1)S(1)}, bf16[2688,256]{1,0:T(8,128)(2,1)}, u32[]{:S(2)}) copy-start(bf16[2688,256]{1,0:T(8,128)(2,1)} %param.41) | copy-start | bytes 4128772
  114.7 3.0 %collective-permute-start.4 = (bf16[128,256]{1,0:T(8,128)(2,1)S(1)}, bf16[128,256]{1,0:T(8,128)(2,1)S(1)}, u32[]{:S(2)}, u32[]{:S(2)}) collective-permute-start(bf16[128,256]{1,0:T(8,128)(2,1)S(1)} %dynamic-slice_convert_fusion), channel_id=1, source_target_pairs={{0,1},{1,0},{2,3},{3,2},{4,5},{5,4},{6,7},{7,6},{8,9},{9,8},{10,11... | collective-permute-start | bytes 196616 | tf_op jit(solution)/shard_map/ppermute | solution.py:275
  117.8 3.2 %collective-permute-start.5 = (bf16[128,256]{1,0:T(8,128)(2,1)S(1)}, bf16[128,256]{1,0:T(8,128)(2,1)S(1)}, u32[]{:S(2)}, u32[]{:S(2)}) collective-permute-start(bf16[128,256]{1,0:T(8,128)(2,1)S(1)} %add_convert_fusion.2), channel_id=1, source_target_pairs={{0,2},{2,0},{4,6},{6,4},{1,3},{3,1},{5,7},{7,5},{8,10},{10,8},{12,... | collective-permute-start | bytes 196616 | tf_op jit(solution)/shard_map/ppermute | solution.py:284
  121.0 4.5 %collective-permute-start.6 = (bf16[128,256]{1,0:T(8,128)(2,1)S(1)}, bf16[128,256]{1,0:T(8,128)(2,1)S(1)}, u32[]{:S(2)}, u32[]{:S(2)}) collective-permute-start(bf16[128,256]{1,0:T(8,128)(2,1)S(1)} %add_convert_fusion.1), channel_id=1, source_target_pairs={{2,4},{4,2},{6,0},{0,6},{3,5},{5,3},{7,1},{1,7},{10,12},{12,10},{1... | collective-permute-start | bytes 196616 | tf_op jit(solution)/shard_map/ppermute | solution.py:284
  125.6 3.6 %collective-permute-start.7 = (bf16[128,256]{1,0:T(8,128)(2,1)S(1)}, bf16[128,256]{1,0:T(8,128)(2,1)S(1)}, u32[]{:S(2)}, u32[]{:S(2)}) collective-permute-start(bf16[128,256]{1,0:T(8,128)(2,1)S(1)} %add_convert_fusion), channel_id=1, source_target_pairs={{0,1},{1,0},{2,3},{3,2},{4,5},{5,4},{6,7},{7,6},{8,9},{9,8},{10,11... | collective-permute-start | bytes 196616 | tf_op jit(solution)/shard_map/ppermute | solution.py:275

commit v4 on v3

--- a/solution.py
+++ b/solution.py
@@ -67,6 +67,7 @@
         in_specs=[IN_VMEM] * 5,
         out_specs=IN_VMEM,
         compiler_params=SMALL,
+        cost_estimate=pl.CostEstimate(flops=20_000_000_000, bytes_accessed=60_000_000, transcendentals=0),
         name="input_projection",
     )(residual, norm, mix, group, step_t)
 
@@ -84,16 +85,8 @@
         arrived_ref, lengths_ref, tail_mix_ref, tail_group_ref, conv_mix_ref, conv_group_ref,
         bias_mix_ref, bias_group_ref, step_bias_ref, decay_log_ref, skip_ref, gain_ref, state_ref,
         y_ref, tail_mix_out_ref, tail_group_out_ref, u_ref, decay_ref, b_ref,
-        c_ref, columns_ref, read_ref, buffer_ref, sems,
+        c_ref, columns_ref, read_ref,
     ):
-        def fetch(r):
-            return pltpu.make_async_copy(state_ref.at[r], buffer_ref.at[r], sems.at[r])
-
-        def begin(r, carry):
-            fetch(r).start()
-            return carry
-
-        lax.fori_loop(0, rows, begin, 0)
         spread = expander(heads, mix, head_dim)
 
         def expand(v):
@@ -154,8 +147,7 @@
             right = []
             for k in range(BATCH):
                 r = i * BATCH + k
-                fetch(r).wait()
-                s = buffer_ref[r].reshape(mix, state)
+                s = state_ref[r].reshape(mix, state)
                 s_high = s.astype(bf16)
                 left += [s_high, (s - s_high.astype(f32)).astype(bf16)]
                 own = jnp.where(lane % rows == r, columns_ref[...], 0.0).astype(bf16)
@@ -188,7 +180,7 @@
     taps = conv_mix.shape[0]
     args = (
         arrived, lengths[None], jnp.transpose(tail_mix, (1, 0, 2)), tail_group, conv_mix, conv_group,
-        bias_mix[None], bias_group, step_bias[None], decay_log[None], skip_gain[None], gate_gain[None], in_hbm(ssm_state),
+        bias_mix[None], bias_group, step_bias[None], decay_log[None], skip_gain[None], gate_gain[None], ssm_state,
     )
     outs = (
         jax.ShapeDtypeStruct((pieces, rows, mix), bf16),
@@ -200,15 +192,13 @@
     )
     return pl.pallas_call(
         make_mixer_kernel(width_all, (pieces, rows, heads, head_dim, state, mix, taps)),
-        in_specs=[IN_VMEM] * (len(args) - 1) + [pl.BlockSpec(memory_space=pl.ANY)],
+        in_specs=[IN_VMEM] * len(args),
         out_specs=[IN_VMEM] * len(outs),
         out_shape=outs,
         scratch_shapes=[
             pltpu.VMEM((rows, state), f32),
             pltpu.VMEM((state, LANES), f32),
             pltpu.VMEM((mix, LANES), f32),
-            pltpu.VMEM((rows, heads, head_dim, state), f32),
-            pltpu.SemaphoreType.DMA((rows,)),
         ],
         compiler_params=SMALL,
         name="mixer_step",

time: 130 us -> 128 us (0.985)
  Pallas kernels: 13.9 us -> 12 us
    pallas_call x1, Pallas kernels: 6.4 us -> 4.54 us  [mixer_step(): pl.pallas_call(make_mixer_kernel(width_all, (pieces, rows, heads, head_di...]
    unnamed x38 -> x42, local copies, waits for them, and re-layouts: 2.63 us -> 2.65 us
where the time goes in v4:
time: 128 us
  blocking collectives  73.5 us (57%)
  starting transfers between devices  20.7 us (16%)
  waiting for transfers between devices  14.8 us (12%)
  Pallas kernels  12 us (9%)
  local copies, waits for them, and re-layouts  2.78 us (2%)
  other arithmetic  1.8 us (1%)
  matrix products  1.39 us (1%)
    all_to_all x3, blocking collectives, exchange(): return lax.all_to_all(value, axis, 0, 0, tiled=True)  73.5 us
    ppermute x4, starting transfers between devices, swap_core(): return lax.ppermute(value, 'c', [(0, 1), (1, 0)])  9.98 us
    ppermute x4, waiting for transfers between devices, ring_pairs(): return lax.ppermute(value, 'y', pairs)  8.16 us
    ppermute x4, starting transfers between devices, ring_pairs(): return lax.ppermute(value, 'y', pairs)  7.15 us
    pallas_call x1, Pallas kernels, state_update(): pl.pallas_call(make_update_kernel(rows, heads, head_dim, state), in_specs...  6.98 us
    pallas_call x1, Pallas kernels, mixer_step(): pl.pallas_call(make_mixer_kernel(width_all, (pieces, rows, heads, head_di...  4.54 us
    ppermute x4, waiting for transfers between devices, swap_core(): return lax.ppermute(value, 'c', [(0, 1), (1, 0)])  3.6 us
    all_to_all x1, starting transfers between devices, exchange(): return lax.all_to_all(value, axis, 0, 0, tiled=True)  3.57 us
  transfers between devices with their start and end apart: 9, of which 9 were waited for; matrix products, arithmetic and copies ran while one was open for 0% of the time, Pallas kernels for 5%

profile of v4, /device:TPU:1, one launch (start us, length us, event | category | flops | bytes accessed | tf_op | source)
XLA Modules:
  0.0 128.1 jit_solution(1217006440788518730)
XLA Ops:
  0.7 1.0 copy.29
  1.7 1.5 %copy.26 = bf16[32,8,2,1024]{3,1,2,0:T(8,128)(2,1)S(1)} copy(bf16[32,8,2,1024]{3,2,1,0:T(2,128)(2,1)} %bitcast.42) | data formatting | bytes 2097152
  3.3 0.5 input_projection.1
  3.9 26.9 %all_to_all.20.arrived_ref = bf16[16,16,2432]{2,1,0:T(8,128)(2,1)S(1)} all-to-all(bf16[16,16,2432]{2,1,0:T(8,128)(2,1)S(1)} %bitcast.27), channel_id=1, replica_groups=mesh['z'=4,'x'=4,'y'=4,'c'=2] {'z','x'}, dimensions={0} | all-to-all | bytes 2490368 | tf_op jit(solution)/shard_map/all_to_all | solution.py:304
  31.0 4.5 %mixer_step.1 = (bf16[16,16,1024]{2,1,0:T(8,128)(2,1)}, f32[3,16,1024]{2,1,0:T(8,128)}, f32[16,3,2,128]{3,2,1,0:T(2,128)}, f32[8,16,128]{2,1,0:T(8,128)S(1)}, f3...) custom-call(bf16[16,16,2432]{2,1,0:T(8,128)(2,1)S(1)} %all_to_all.20.arrived_ref, s32[1,16]{1,0:T(1,128)S(1)} %bitcast.33, ...), custom_call_target="tpu_custom_call" | custom-call | tf_op jit(solution)/shard_map/mixer_step/pallas_call | solution.py:193
  35.5 3.6 %all-to-all-start.1 = ((bf16[16,16,1024]{2,1,0:T(8,128)(2,1)}), bf16[16,16,1024]{2,1,0:T(8,128)(2,1)S(1)}, u32[]{:S(2)}, u32[]{:S(2)}) async-start(bf16[16,16,1024]{2,1,0:T(8,128)(2,1)} %get-tuple-element.12), calls=%async_computation.1 | async-start | bytes 1048576 | tf_op jit(solution)/shard_map/all_to_all | solution.py:304
  39.1 7.0 %state_update.1 = f32[16,16,64,128]{3,2,1,0:T(8,128)} custom-call(f32[8,16,128]{2,1,0:T(8,128)S(1)} %get-tuple-element.13.u_ref, f32[16,128]{1,0:T(8,128)S(1)} %get-tuple-element.14.decay_ref, f32[16,128]{1,0:T(8,128)S(1)} %get-tuple-element.15.b_ref, f32[16,16,64,128]{3,2,1,0:T(8,128)} %state_ref.3), custom_call_target="tpu_custom_call" | custom-call | tf_op jit(solution)/shard_map/state_update/pallas_call | solution.py:249
  46.1 3.1 %all-to-all-done.1 = bf16[16,16,1024]{2,1,0:T(8,128)(2,1)S(1)} async-done(((bf16[16,16,1024]{2,1,0:T(8,128)(2,1)}), bf16[16,16,1024]{2,1,0:T(8,128)(2,1)S(1)}, u32[]{:S(2)}, u32[]{:S(2)}) %all-to-all-start.1) | async-done | bytes 524320 | tf_op jit(solution)/shard_map/all_to_all | solution.py:304
  49.2 0.3 fusion.14
  49.5 2.5 %collective-permute-start = (bf16[128,256]{1,0:T(8,128)(2,1)S(1)}, bf16[128,256]{1,0:T(8,128)(2,1)S(1)}, u32[]{:S(2)}, u32[]{:S(2)}) collective-permute-start(bf16[128,256]{1,0:T(8,128)(2,1)S(1)} %dynamic-slice_convert_fusion.1), channel_id=1, source_target_pairs={{0,1},{1,0},{2,3},{3,2},{4,5},{5,4},{6,7},{7,6},{8,9},{9,8},{10,11... | collective-permute-start | bytes 196616 | tf_op jit(solution)/shard_map/ppermute | solution.py:265
  52.0 0.9 collective-permute-done
  52.9 1.4 %collective-permute-start.1 = (bf16[128,256]{1,0:T(8,128)(2,1)S(1)}, bf16[128,256]{1,0:T(8,128)(2,1)S(1)}, u32[]{:S(2)}, u32[]{:S(2)}) collective-permute-start(bf16[128,256]{1,0:T(8,128)(2,1)S(1)} %add_convert_fusion.5), channel_id=1, source_target_pairs={{0,2},{2,0},{4,6},{6,4},{1,3},{3,1},{5,7},{7,5},{8,10},{10,8},{12,... | collective-permute-start | bytes 196616 | tf_op jit(solution)/shard_map/ppermute | solution.py:274
  54.3 1.8 %collective-permute-done.1 = bf16[128,256]{1,0:T(8,128)(2,1)S(1)} collective-permute-done((bf16[128,256]{1,0:T(8,128)(2,1)S(1)}, bf16[128,256]{1,0:T(8,128)(2,1)S(1)}, u32[]{:S(2)}, u32[]{:S(2)}) %collective-permute-start.1) | collective-permute-done | bytes 65568 | tf_op jit(solution)/shard_map/ppermute | solution.py:274
  56.1 2.8 %collective-permute-start.2 = (bf16[128,256]{1,0:T(8,128)(2,1)S(1)}, bf16[128,256]{1,0:T(8,128)(2,1)S(1)}, u32[]{:S(2)}, u32[]{:S(2)}) collective-permute-start(bf16[128,256]{1,0:T(8,128)(2,1)S(1)} %add_convert_fusion.4), channel_id=1, source_target_pairs={{2,4},{4,2},{6,0},{0,6},{3,5},{5,3},{7,1},{1,7},{10,12},{12,10},{1... | collective-permute-start | bytes 196616 | tf_op jit(solution)/shard_map/ppermute | solution.py:274
  58.9 1.6 %collective-permute-done.2 = bf16[128,256]{1,0:T(8,128)(2,1)S(1)} collective-permute-done((bf16[128,256]{1,0:T(8,128)(2,1)S(1)}, bf16[128,256]{1,0:T(8,128)(2,1)S(1)}, u32[]{:S(2)}, u32[]{:S(2)}) %collective-permute-start.2) | collective-permute-done | bytes 65568 | tf_op jit(solution)/shard_map/ppermute | solution.py:274
  60.6 2.7 %collective-permute-start.3 = (bf16[128,256]{1,0:T(8,128)(2,1)S(1)}, bf16[128,256]{1,0:T(8,128)(2,1)S(1)}, u32[]{:S(2)}, u32[]{:S(2)}) collective-permute-start(bf16[128,256]{1,0:T(8,128)(2,1)S(1)} %add_convert_fusion.3), channel_id=1, source_target_pairs={{0,1},{1,0},{2,3},{3,2},{4,5},{5,4},{6,7},{7,6},{8,9},{9,8},{10,11... | collective-permute-start | bytes 196616 | tf_op jit(solution)/shard_map/ppermute | solution.py:265
  63.3 0.9 collective-permute-done.3
  64.4 0.6 convolution_convert_fusion
  64.9 0.2 select_convert_fusion
  65.2 23.7 %all_to_all.21 = bf16[16,16,2816]{2,1,0:T(8,128)(2,1)S(1)} all-to-all(bf16[16,16,2816]{2,1,0:T(8,128)(2,1)S(1)} %bitcast.39), channel_id=1, replica_groups=mesh['z'=4,'x'=4,'y'=4,'c'=2] {'z','x'}, dimensions={0} | all-to-all | bytes 2883584 | tf_op jit(solution)/shard_map/all_to_all | solution.py:304
  88.9 0.2 convert_reduce_fusion
  89.1 0.2 fusion.11
  89.5 22.9 %all_to_all.22 = bf16[16,16,2688]{2,1,0:T(8,128)(2,1)S(1)} all-to-all(bf16[16,16,2688]{2,1,0:T(8,128)(2,1)S(1)} %broadcast_in_dim.65), channel_id=1, replica_groups=mesh['z'=4,'x'=4,'y'=4,'c'=2] {'z','x'}, dimensions={0} | all-to-all | bytes 2752512 | tf_op jit(solution)/shard_map/all_to_all | solution.py:304
  112.4 0.5 fusion.15
  113.0 2.1 %collective-permute-start.4 = (bf16[128,256]{1,0:T(8,128)(2,1)S(1)}, bf16[128,256]{1,0:T(8,128)(2,1)S(1)}, u32[]{:S(2)}, u32[]{:S(2)}) collective-permute-start(bf16[128,256]{1,0:T(8,128)(2,1)S(1)} %dynamic-slice_convert_fusion), channel_id=1, source_target_pairs={{0,1},{1,0},{2,3},{3,2},{4,5},{5,4},{6,7},{7,6},{8,9},{9,8},{10,11... | collective-permute-start | bytes 196616 | tf_op jit(solution)/shard_map/ppermute | solution.py:265
  115.1 0.9 collective-permute-done.4
  116.2 3.0 %collective-permute-done.5 = bf16[128,256]{1,0:T(8,128)(2,1)S(1)} collective-permute-done((bf16[128,256]{1,0:T(8,128)(2,1)S(1)}, bf16[128,256]{1,0:T(8,128)(2,1)S(1)}, u32[]{:S(2)}, u32[]{:S(2)}) %collective-permute-start.5) | collective-permute-done | bytes 65568 | tf_op jit(solution)/shard_map/ppermute | solution.py:274
  119.3 2.8 %collective-permute-start.6 = (bf16[128,256]{1,0:T(8,128)(2,1)S(1)}, bf16[128,256]{1,0:T(8,128)(2,1)S(1)}, u32[]{:S(2)}, u32[]{:S(2)}) collective-permute-start(bf16[128,256]{1,0:T(8,128)(2,1)S(1)} %add_convert_fusion.1), channel_id=1, source_target_pairs={{2,4},{4,2},{6,0},{0,6},{3,5},{5,3},{7,1},{1,7},{10,12},{12,10},{1... | collective-permute-start | bytes 196616 | tf_op jit(solution)/shard_map/ppermute | solution.py:274
  122.1 1.7 %collective-permute-done.6 = bf16[128,256]{1,0:T(8,128)(2,1)S(1)} collective-permute-done((bf16[128,256]{1,0:T(8,128)(2,1)S(1)}, bf16[128,256]{1,0:T(8,128)(2,1)S(1)}, u32[]{:S(2)}, u32[]{:S(2)}) %collective-permute-start.6) | collective-permute-done | bytes 65568 | tf_op jit(solution)/shard_map/ppermute | solution.py:274
  123.9 2.7 %collective-permute-start.7 = (bf16[128,256]{1,0:T(8,128)(2,1)S(1)}, bf16[128,256]{1,0:T(8,128)(2,1)S(1)}, u32[]{:S(2)}, u32[]{:S(2)}) collective-permute-start(bf16[128,256]{1,0:T(8,128)(2,1)S(1)} %add_convert_fusion), channel_id=1, source_target_pairs={{0,1},{1,0},{2,3},{3,2},{4,5},{5,4},{6,7},{7,6},{8,9},{9,8},{10,11... | collective-permute-start | bytes 196616 | tf_op jit(solution)/shard_map/ppermute | solution.py:265
  126.5 0.9 collective-permute-done.7
  127.5 0.7 pad_maximum_fusion.2
  (59 shorter events, 1.0 us)
Async XLA Ops:
  0.6 63.7 %copy-start = (bf16[256,2688]{1,0:T(8,128)(2,1)S(1)}, bf16[256,2688]{1,0:T(8,128)(2,1)}, u32[]{:S(2)}) copy-start(bf16[256,2688]{1,0:T(8,128)(2,1)} %param.40) | copy-start | bytes 4128772
  0.6 2.6 %copy-start.3 = (bf16[256,256]{1,0:T(8,128)(2,1)S(1)}, bf16[256,256]{1,0:T(8,128)(2,1)}, u32[]{:S(2)}) copy-start(bf16[256,256]{1,0:T(8,128)(2,1)} %residual_ref.1) | copy-start | bytes 393220
  0.7 2.6 %copy-start.13 = (bf16[256,16]{0,1:T(8,128)(2,1)S(1)}, bf16[256,16]{0,1:T(8,128)(2,1)}, u32[]{:S(2)}) copy-start(bf16[256,16]{0,1:T(8,128)(2,1)} %param.29) | copy-start | bytes 24580
  0.7 2.6 %copy-start.14 = (f32[256]{0:T(256)S(1)}, f32[256]{0:T(256)}, u32[]{:S(2)}) copy-start(f32[256]{0:T(256)} %param.26) | copy-start | bytes 3076
  3.2 27.6 %slice-start = ((s8[8388608]{0:T(1024)(128)(4,1)}), s8[4194304]{0:T(1024)(128)(4,1)S(1)}, s32[]{:S(2)}) async-start(s8[8388608]{0:T(1024)(128)(4,1)} %bitcast.25), calls=%async_computation.4 | async-start | bytes 8388608
  3.3 27.6 %slice-start.1 = ((s8[8388608]{0:T(1024)(128)(4,1)}), s8[4194304]{0:T(1024)(128)(4,1)S(1)}, s32[]{:S(2)}) async-start(s8[8388608]{0:T(1024)(128)(4,1)} %bitcast.25), calls=%async_computation.5 | async-start | bytes 8388608
  3.8 27.1 %copy-start.1 = (f32[16,3,1024]{2,0,1:T(8,128)S(1)}, f32[16,3,1024]{2,0,1:T(8,128)}, u32[]{:S(2)}) copy-start(f32[16,3,1024]{2,0,1:T(8,128)} %param.24) | copy-start | bytes 589828
  3.8 27.1 %copy-start.2 = (f32[16,3,2,128]{3,2,1,0:T(2,128)S(1)}, f32[16,3,2,128]{3,2,1,0:T(2,128)}, u32[]{:S(2)}) copy-start(f32[16,3,2,128]{3,2,1,0:T(2,128)} %tail_group_ref.1) | copy-start | bytes 147460
  3.8 27.1 %copy-start.4 = (f32[4,1024]{1,0:T(4,128)S(1)}, f32[4,1024]{1,0:T(4,128)}, u32[]{:S(2)}) copy-start(f32[4,1024]{1,0:T(4,128)} %conv_mix_ref.1) | copy-start | bytes 49156
  3.8 27.1 %copy-start.5 = (f32[4,2,128]{2,1,0:T(2,128)S(1)}, f32[4,2,128]{2,1,0:T(2,128)}, u32[]{:S(2)}) copy-start(f32[4,2,128]{2,1,0:T(2,128)} %conv_group_ref.1) | copy-start | bytes 12292
  3.8 27.1 %copy-start.6 = (f32[1024]{0:T(1024)S(1)}, f32[1024]{0:T(1024)}, u32[]{:S(2)}) copy-start(f32[1024]{0:T(1024)} %param.32) | copy-start | bytes 12292
  3.8 27.1 %copy-start.7 = (f32[1024]{0:T(1024)S(1)}, f32[1024]{0:T(1024)}, u32[]{:S(2)}) copy-start(f32[1024]{0:T(1024)} %param.37) | copy-start | bytes 12292
  3.9 27.1 %copy-start.8 = (f32[2,128]{1,0:T(2,128)S(1)}, f32[2,128]{1,0:T(2,128)}, u32[]{:S(2)}) copy-start(f32[2,128]{1,0:T(2,128)} %bias_group_ref.1) | copy-start | bytes 3076
  3.9 27.0 %copy-start.9 = (s32[16]{0:T(128)S(1)}, s32[16]{0:T(128)}, u32[]{:S(2)}) copy-start(s32[16]{0:T(128)} %param.22) | copy-start | bytes 196
  3.9 27.0 %copy-start.10 = (f32[16]{0:T(128)S(1)}, f32[16]{0:T(128)}, u32[]{:S(2)}) copy-start(f32[16]{0:T(128)} %param.34) | copy-start | bytes 196
  3.9 27.0 %copy-start.11 = (f32[16]{0:T(128)S(1)}, f32[16]{0:T(128)}, u32[]{:S(2)}) copy-start(f32[16]{0:T(128)} %param.35) | copy-start | bytes 196
  3.9 27.0 %copy-start.12 = (f32[16]{0:T(128)S(1)}, f32[16]{0:T(128)}, u32[]{:S(2)}) copy-start(f32[16]{0:T(128)} %param.36) | copy-start | bytes 196
  35.5 13.7 %all-to-all-start.1 = ((bf16[16,16,1024]{2,1,0:T(8,128)(2,1)}), bf16[16,16,1024]{2,1,0:T(8,128)(2,1)S(1)}, u32[]{:S(2)}, u32[]{:S(2)}) async-start(bf16[16,16,1024]{2,1,0:T(8,128)(2,1)} %get-tuple-element.12), calls=%async_computation.1 | async-start | bytes 1048576 | tf_op jit(solution)/shard_map/all_to_all | solution.py:304
  39.1 10.1 %copy-start.16 = (bf16[1024,256]{1,0:T(8,128)(2,1)S(1)}, bf16[1024,256]{1,0:T(8,128)(2,1)}, u32[]{:S(2)}) copy-start(bf16[1024,256]{1,0:T(8,128)(2,1)} %param.38) | copy-start | bytes 1572868
  46.1 18.3 %copy-start.17 = (f32[256]{0:T(256)S(1)}, f32[256]{0:T(256)}, u32[]{:S(2)}) copy-start(f32[256]{0:T(256)} %param.39) | copy-start | bytes 3076
  49.5 3.4 %collective-permute-start = (bf16[128,256]{1,0:T(8,128)(2,1)S(1)}, bf16[128,256]{1,0:T(8,128)(2,1)S(1)}, u32[]{:S(2)}, u32[]{:S(2)}) collective-permute-start(bf16[128,256]{1,0:T(8,128)(2,1)S(1)} %dynamic-slice_convert_fusion.1), channel_id=1, source_target_pairs={{0,1},{1,0},{2,3},{3,2},{4,5},{5,4},{6,7},{7,6},{8,9},{9,8},{10,11... | collective-permute-start | bytes 196616 | tf_op jit(solution)/shard_map/ppermute | solution.py:265
  52.9 3.2 %collective-permute-start.1 = (bf16[128,256]{1,0:T(8,128)(2,1)S(1)}, bf16[128,256]{1,0:T(8,128)(2,1)S(1)}, u32[]{:S(2)}, u32[]{:S(2)}) collective-permute-start(bf16[128,256]{1,0:T(8,128)(2,1)S(1)} %add_convert_fusion.5), channel_id=1, source_target_pairs={{0,2},{2,0},{4,6},{6,4},{1,3},{3,1},{5,7},{7,5},{8,10},{10,8},{12,... | collective-permute-start | bytes 196616 | tf_op jit(solution)/shard_map/ppermute | solution.py:274
  56.1 4.5 %collective-permute-start.2 = (bf16[128,256]{1,0:T(8,128)(2,1)S(1)}, bf16[128,256]{1,0:T(8,128)(2,1)S(1)}, u32[]{:S(2)}, u32[]{:S(2)}) collective-permute-start(bf16[128,256]{1,0:T(8,128)(2,1)S(1)} %add_convert_fusion.4), channel_id=1, source_target_pairs={{2,4},{4,2},{6,0},{0,6},{3,5},{5,3},{7,1},{1,7},{10,12},{12,10},{1... | collective-permute-start | bytes 196616 | tf_op jit(solution)/shard_map/ppermute | solution.py:274
  60.6 3.6 %collective-permute-start.3 = (bf16[128,256]{1,0:T(8,128)(2,1)S(1)}, bf16[128,256]{1,0:T(8,128)(2,1)S(1)}, u32[]{:S(2)}, u32[]{:S(2)}) collective-permute-start(bf16[128,256]{1,0:T(8,128)(2,1)S(1)} %add_convert_fusion.3), channel_id=1, source_target_pairs={{0,1},{1,0},{2,3},{3,2},{4,5},{5,4},{6,7},{7,6},{8,9},{9,8},{10,11... | collective-permute-start | bytes 196616 | tf_op jit(solution)/shard_map/ppermute | solution.py:265
  89.5 22.9 %copy-start.15 = (bf16[2688,256]{1,0:T(8,128)(2,1)S(1)}, bf16[2688,256]{1,0:T(8,128)(2,1)}, u32[]{:S(2)}) copy-start(bf16[2688,256]{1,0:T(8,128)(2,1)} %param.41) | copy-start | bytes 4128772
  113.0 3.0 %collective-permute-start.4 = (bf16[128,256]{1,0:T(8,128)(2,1)S(1)}, bf16[128,256]{1,0:T(8,128)(2,1)S(1)}, u32[]{:S(2)}, u32[]{:S(2)}) collective-permute-start(bf16[128,256]{1,0:T(8,128)(2,1)S(1)} %dynamic-slice_convert_fusion), channel_id=1, source_target_pairs={{0,1},{1,0},{2,3},{3,2},{4,5},{5,4},{6,7},{7,6},{8,9},{9,8},{10,11... | collective-permute-start | bytes 196616 | tf_op jit(solution)/shard_map/ppermute | solution.py:265
  116.1 3.2 %collective-permute-start.5 = (bf16[128,256]{1,0:T(8,128)(2,1)S(1)}, bf16[128,256]{1,0:T(8,128)(2,1)S(1)}, u32[]{:S(2)}, u32[]{:S(2)}) collective-permute-start(bf16[128,256]{1,0:T(8,128)(2,1)S(1)} %add_convert_fusion.2), channel_id=1, source_target_pairs={{0,2},{2,0},{4,6},{6,4},{1,3},{3,1},{5,7},{7,5},{8,10},{10,8},{12,... | collective-permute-start | bytes 196616 | tf_op jit(solution)/shard_map/ppermute | solution.py:274
  119.3 4.5 %collective-permute-start.6 = (bf16[128,256]{1,0:T(8,128)(2,1)S(1)}, bf16[128,256]{1,0:T(8,128)(2,1)S(1)}, u32[]{:S(2)}, u32[]{:S(2)}) collective-permute-start(bf16[128,256]{1,0:T(8,128)(2,1)S(1)} %add_convert_fusion.1), channel_id=1, source_target_pairs={{2,4},{4,2},{6,0},{0,6},{3,5},{5,3},{7,1},{1,7},{10,12},{12,10},{1... | collective-permute-start | bytes 196616 | tf_op jit(solution)/shard_map/ppermute | solution.py:274
  123.9 3.6 %collective-permute-start.7 = (bf16[128,256]{1,0:T(8,128)(2,1)S(1)}, bf16[128,256]{1,0:T(8,128)(2,1)S(1)}, u32[]{:S(2)}, u32[]{:S(2)}) collective-permute-start(bf16[128,256]{1,0:T(8,128)(2,1)S(1)} %add_convert_fusion), channel_id=1, source_target_pairs={{0,1},{1,0},{2,3},{3,2},{4,5},{5,4},{6,7},{7,6},{8,9},{9,8},{10,11... | collective-permute-start | bytes 196616 | tf_op jit(solution)/shard_map/ppermute | solution.py:265

commit v5 on v4

--- a/solution.py
+++ b/solution.py
@@ -9,7 +9,8 @@
 REQ = ("z", "x")
 HEAD = ("y", "c")
 LANES = 128
-BATCH = 4
+BATCH = 8
+ON_MXU = 3
 IN_VMEM = pl.BlockSpec(memory_space=pltpu.VMEM)
 SMALL = pltpu.CompilerParams(vmem_limit_bytes=16 * 2**20)
 f32 = jnp.float32
@@ -48,10 +49,18 @@
     wide = residual_ref[...].astype(f32)
     scaled = (wide * norm_ref[...]).astype(bf16)
     mix = mix_ref.shape[1]
-    group = group_ref.shape[1]
+    depth = wide.shape[1]
+    state = group_ref.shape[2]
+    group = 2 * state
     steps = step_ref.shape[0]
     out_ref[:, :mix] = jnp.dot(scaled, mix_ref[...], preferred_element_type=f32).astype(bf16)
-    out_ref[:, mix : mix + group] = jnp.dot(scaled, group_ref[...], preferred_element_type=f32).astype(bf16)
+    row = lax.broadcasted_iota(jnp.int32, (depth, 2 * depth), 0)
+    col = lax.broadcasted_iota(jnp.int32, (depth, 2 * depth), 1)
+    pairs = group_ref[...].reshape(2 * depth, state)
+    for j in range(2):
+        spaced = jnp.dot(scaled, (col == 2 * row + j).astype(bf16), preferred_element_type=f32).astype(bf16)
+        at = mix + j * state
+        out_ref[:, at : at + state] = jnp.dot(spaced, pairs, preferred_element_type=f32).astype(bf16)
     step = lax.dot_general(scaled, step_ref[...], (((1,), (1,)), ((), ())), preferred_element_type=f32)
     tail = norm_columns(wide, steps)
     out_ref[:, mix + group :] = tail.astype(bf16)
@@ -60,7 +69,7 @@
 
 def input_projection(residual, norm, mix, group, step_t):
     rows = residual.shape[0]
-    width = mix.shape[1] + group.shape[1] + LANES
+    width = mix.shape[1] + 2 * group.shape[2] + LANES
     return pl.pallas_call(
         input_kernel,
         out_shape=jax.ShapeDtypeStruct((rows, width), bf16),
@@ -85,7 +94,7 @@
         arrived_ref, lengths_ref, tail_mix_ref, tail_group_ref, conv_mix_ref, conv_group_ref,
         bias_mix_ref, bias_group_ref, step_bias_ref, decay_log_ref, skip_ref, gain_ref, state_ref,
         y_ref, tail_mix_out_ref, tail_group_out_ref, u_ref, decay_ref, b_ref,
-        c_ref, columns_ref, read_ref,
+        c_ref, columns_ref, read_ref, summed_ref,
     ):
         spread = expander(heads, mix, head_dim)
 
@@ -140,13 +149,19 @@
         both = jnp.concatenate([c_high, c - c_high, jnp.zeros((LANES - 2 * rows, state), f32)], axis=0)
         columns_ref[...] = jnp.transpose(both)
         read_ref[...] = jnp.zeros_like(read_ref)
+        summed_ref[...] = jnp.zeros_like(summed_ref)
+        head_lane = lax.broadcasted_iota(jnp.int32, (head_dim, LANES), 1)
         lane = lax.broadcasted_iota(jnp.int32, (state, LANES), 1)
 
         def some_rows(i, carry):
             left = []
             right = []
+            others = []
             for k in range(BATCH):
                 r = i * BATCH + k
+                if k >= ON_MXU:
+                    others.append((r, c_ref[pl.ds(r, 1), :]))
+                    continue
                 s = state_ref[r].reshape(mix, state)
                 s_high = s.astype(bf16)
                 left += [s_high, (s - s_high.astype(f32)).astype(bf16)]
@@ -155,10 +170,17 @@
             read_ref[...] += jnp.dot(
                 jnp.concatenate(left, axis=1), jnp.concatenate(right, axis=0), preferred_element_type=f32
             )
+            for h in range(heads):
+                at = slice(h * head_dim, (h + 1) * head_dim)
+                block = summed_ref[at, :]
+                for r, c_row in others:
+                    part = jnp.sum(state_ref[r, h] * c_row, axis=1, keepdims=True)
+                    block = jnp.where(head_lane == r, part, block)
+                summed_ref[at, :] = block
             return carry
 
         lax.fori_loop(0, rows // BATCH, some_rows, 0)
-        across_read = jnp.transpose(read_ref[...])
+        across_read = jnp.transpose(read_ref[...] + summed_ref[...])
         read = across_read[:rows, :] + across_read[rows : 2 * rows, :]
         bc = jnp.sum(b_ref[...] * c_ref[...], axis=1, keepdims=True)
         skip = expand(jnp.broadcast_to(skip_ref[...], (rows, heads)))
@@ -199,6 +221,7 @@
             pltpu.VMEM((rows, state), f32),
             pltpu.VMEM((state, LANES), f32),
             pltpu.VMEM((mix, LANES), f32),
+            pltpu.VMEM((mix, LANES), f32),
         ],
         compiler_params=SMALL,
         name="mixer_step",
@@ -261,6 +284,25 @@
     )(u, decay, b, in_hbm(ssm_state))
 
 
+def up_kernel(middle_ref, norm_ref, up_ref, out_ref):
+    wide = middle_ref[...].astype(f32)
+    scaled = (wide * norm_ref[...]).astype(bf16)
+    width = up_ref.shape[1]
+    out_ref[:, width:] = norm_columns(wide, 0).astype(bf16)
+    out_ref[:, :width] = jnp.dot(scaled, up_ref[...], preferred_element_type=f32).astype(bf16)
+
+
+def up_projection(middle, norm, up):
+    return pl.pallas_call(
+        up_kernel,
+        out_shape=jax.ShapeDtypeStruct((middle.shape[0], up.shape[1] + LANES), bf16),
+        in_specs=[IN_VMEM] * 3,
+        out_specs=IN_VMEM,
+        compiler_params=SMALL,
+        name="up_projection",
+    )(middle, norm, up)
+
+
 def swap_core(value):
     return lax.ppermute(value, "c", [(0, 1), (1, 0)])
 
@@ -320,8 +362,7 @@
     rows, width_dev = residual.shape
     width_all = width_dev * peers
     mix_flat = mix_weight.reshape(width_dev, -1)
-    group_flat = group_weight.reshape(width_dev, -1)
-    pieces = input_projection(residual, norm_first[None], mix_flat, group_flat, step_weight.T)
+    pieces = input_projection(residual, norm_first[None], mix_flat, group_weight, step_weight.T)
     arrived = exchange(pieces.reshape(peers, rows_dev, -1), REQ)
     copies, tail_mix_out, tail_group_out, u, decay, b = mixer_step(
         arrived, lengths, tail_mix, tail_group, conv_mix, conv_group, bias_mix, bias_group, step_bias,
@@ -331,17 +372,8 @@
     state_out = state_update(ssm_state, u, decay, b)
     every_y, state_out = lax.optimization_barrier((every_y, state_out))
     middle = add_over_heads(residual, jnp.dot(every_y, out_weight, preferred_element_type=f32))
-    wide = middle.astype(f32)
-    scaled_two = (wide * norm_second).astype(bf16)
-    activation = jnp.dot(scaled_two, up_weight, preferred_element_type=f32).astype(bf16)
     hidden_dev = up_weight.shape[1]
-    total = jnp.sum(wide * wide, axis=1, keepdims=True)
-    high = lax.reduce_precision(total, 8, 7)
-    mid = lax.reduce_precision(total - high, 8, 7)
-    low = total - high - mid
-    lane = lax.broadcasted_iota(jnp.int32, (rows, LANES), 1)
-    columns = jnp.where(lane == 0, high, jnp.where(lane == 1, mid, jnp.where(lane == 2, low, 0.0))).astype(bf16)
-    sent = jnp.concatenate([activation, columns], axis=1).reshape(peers, rows_dev, hidden_dev + LANES)
+    sent = up_projection(middle, norm_second[None], up_weight).reshape(peers, rows_dev, -1)
     sums = exchange(sent, REQ).astype(f32).sum(axis=0)
     squares = sums[:, hidden_dev : hidden_dev + 1] + sums[:, hidden_dev + 1 : hidden_dev + 2] + sums[:, hidden_dev + 2 : hidden_dev + 3]
     inverse = lax.rsqrt(squares / width_all + eps)

time: 128 us -> 129 us (level)
    unnamed x42 -> x43, local copies, waits for them, and re-layouts: 2.65 us -> 2.42 us
where the time goes in v5:
time: 129 us
  blocking collectives  73.4 us (57%)
  starting transfers between devices  20.7 us (16%)
  waiting for transfers between devices  14.9 us (12%)
  Pallas kernels  11.8 us (9%)
  local copies, waits for them, and re-layouts  2.54 us (2%)
  other arithmetic  2.32 us (2%)
  matrix products  1.9 us (1%)
    all_to_all x3, blocking collectives, exchange(): return lax.all_to_all(value, axis, 0, 0, tiled=True)  73.4 us
    ppermute x4, starting transfers between devices, swap_core(): return lax.ppermute(value, 'c', [(0, 1), (1, 0)])  9.96 us
    ppermute x4, waiting for transfers between devices, ring_pairs(): return lax.ppermute(value, 'y', pairs)  8.18 us
    ppermute x4, starting transfers between devices, ring_pairs(): return lax.ppermute(value, 'y', pairs)  7.16 us
    pallas_call x1, Pallas kernels, state_update(): pl.pallas_call(make_update_kernel(rows, heads, head_dim, state), in_specs...  6.93 us
    ppermute x4, waiting for transfers between devices, swap_core(): return lax.ppermute(value, 'c', [(0, 1), (1, 0)])  3.61 us
    all_to_all x1, starting transfers between devices, exchange(): return lax.all_to_all(value, axis, 0, 0, tiled=True)  3.57 us
    pallas_call x1, Pallas kernels, mixer_step(): pl.pallas_call(make_mixer_kernel(width_all, (pieces, rows, heads, head_di...  3.42 us
  transfers between devices with their start and end apart: 9, of which 9 were waited for; matrix products, arithmetic and copies ran while one was open for 0% of the time, Pallas kernels for 5%

profile of v5, /device:TPU:1, one launch (start us, length us, event | category | flops | bytes accessed | tf_op | source)
XLA Modules:
  0.0 128.6 jit_solution(14388510878616402181)
XLA Ops:
  0.7 1.6 %copy.26 = bf16[32,8,2,1024]{3,1,2,0:T(8,128)(2,1)S(1)} copy(bf16[32,8,2,1024]{3,2,1,0:T(2,128)(2,1)} %bitcast.38) | data formatting | bytes 2097152
  2.4 0.9 input_projection.1
  3.4 26.9 %all_to_all.20.arrived_ref = bf16[16,16,2432]{2,1,0:T(8,128)(2,1)S(1)} all-to-all(bf16[16,16,2432]{2,1,0:T(8,128)(2,1)S(1)} %bitcast.24), channel_id=1, replica_groups=mesh['z'=4,'x'=4,'y'=4,'c'=2] {'z','x'}, dimensions={0} | all-to-all | bytes 2490368 | tf_op jit(solution)/shard_map/all_to_all | solution.py:346
  30.4 3.4 %mixer_step.1 = (bf16[16,16,1024]{2,1,0:T(8,128)(2,1)}, f32[3,16,1024]{2,1,0:T(8,128)}, f32[16,3,2,128]{3,2,1,0:T(2,128)}, f32[8,16,128]{2,1,0:T(8,128)S(1)}, f3...) custom-call(bf16[16,16,2432]{2,1,0:T(8,128)(2,1)S(1)} %all_to_all.20.arrived_ref, s32[1,16]{1,0:T(1,128)S(1)} %bitcast.30, ...), custom_call_target="tpu_custom_call" | custom-call | tf_op jit(solution)/shard_map/mixer_step/pallas_call | solution.py:215
  33.8 3.6 %all-to-all-start.1 = ((bf16[16,16,1024]{2,1,0:T(8,128)(2,1)}), bf16[16,16,1024]{2,1,0:T(8,128)(2,1)S(1)}, u32[]{:S(2)}, u32[]{:S(2)}) async-start(bf16[16,16,1024]{2,1,0:T(8,128)(2,1)} %get-tuple-element.12), calls=%async_computation.1 | async-start | bytes 1048576 | tf_op jit(solution)/shard_map/all_to_all | solution.py:346
  37.4 6.9 %state_update.1 = f32[16,16,64,128]{3,2,1,0:T(8,128)} custom-call(f32[8,16,128]{2,1,0:T(8,128)S(1)} %get-tuple-element.13.u_ref, f32[16,128]{1,0:T(8,128)S(1)} %get-tuple-element.14.decay_ref, f32[16,128]{1,0:T(8,128)S(1)} %get-tuple-element.15.b_ref, f32[16,16,64,128]{3,2,1,0:T(8,128)} %state_ref.3), custom_call_target="tpu_custom_call" | custom-call | tf_op jit(solution)/shard_map/state_update/pallas_call | solution.py:272
  44.4 3.1 %all-to-all-done.1 = bf16[16,16,1024]{2,1,0:T(8,128)(2,1)S(1)} async-done(((bf16[16,16,1024]{2,1,0:T(8,128)(2,1)}), bf16[16,16,1024]{2,1,0:T(8,128)(2,1)S(1)}, u32[]{:S(2)}, u32[]{:S(2)}) %all-to-all-start.1) | async-done | bytes 524320 | tf_op jit(solution)/shard_map/all_to_all | solution.py:346
  47.5 1.3 %fusion.8 = f32[256,256]{1,0:T(8,128)S(1)} fusion(bf16[256,1024]{1,0:T(8,128)(2,1)S(1)} %bitcast.37, bf16[1024,256]{1,0:T(8,128)(2,1)} %param.38), kind=kOutput, calls=%fused_computation.28 | convolution fusion | flops 134217728 | bytes 1310720 | tf_op jit(solution)/shard_map/dot_general | solution.py:374
  48.9 0.7 copy-done.18
  49.6 2.5 %collective-permute-start = (bf16[128,256]{1,0:T(8,128)(2,1)S(1)}, bf16[128,256]{1,0:T(8,128)(2,1)S(1)}, u32[]{:S(2)}, u32[]{:S(2)}) collective-permute-start(bf16[128,256]{1,0:T(8,128)(2,1)S(1)} %dynamic-slice_convert_fusion.1), channel_id=1, source_target_pairs={{0,1},{1,0},{2,3},{3,2},{4,5},{5,4},{6,7},{7,6},{8,9},{9,8},{10,11... | collective-permute-start | bytes 196616 | tf_op jit(solution)/shard_map/ppermute | solution.py:307
  52.1 0.9 collective-permute-done
  53.0 0.9 add_convert_fusion.5
  53.9 1.4 %collective-permute-start.1 = (bf16[128,256]{1,0:T(8,128)(2,1)S(1)}, bf16[128,256]{1,0:T(8,128)(2,1)S(1)}, u32[]{:S(2)}, u32[]{:S(2)}) collective-permute-start(bf16[128,256]{1,0:T(8,128)(2,1)S(1)} %add_convert_fusion.5), channel_id=1, source_target_pairs={{0,2},{2,0},{4,6},{6,4},{1,3},{3,1},{5,7},{7,5},{8,10},{10,8},{12,... | collective-permute-start | bytes 196616 | tf_op jit(solution)/shard_map/ppermute | solution.py:316
  55.2 1.8 %collective-permute-done.1 = bf16[128,256]{1,0:T(8,128)(2,1)S(1)} collective-permute-done((bf16[128,256]{1,0:T(8,128)(2,1)S(1)}, bf16[128,256]{1,0:T(8,128)(2,1)S(1)}, u32[]{:S(2)}, u32[]{:S(2)}) %collective-permute-start.1) | collective-permute-done | bytes 65568 | tf_op jit(solution)/shard_map/ppermute | solution.py:316
  57.1 2.8 %collective-permute-start.2 = (bf16[128,256]{1,0:T(8,128)(2,1)S(1)}, bf16[128,256]{1,0:T(8,128)(2,1)S(1)}, u32[]{:S(2)}, u32[]{:S(2)}) collective-permute-start(bf16[128,256]{1,0:T(8,128)(2,1)S(1)} %add_convert_fusion.4), channel_id=1, source_target_pairs={{2,4},{4,2},{6,0},{0,6},{3,5},{5,3},{7,1},{1,7},{10,12},{12,10},{1... | collective-permute-start | bytes 196616 | tf_op jit(solution)/shard_map/ppermute | solution.py:316
  59.9 1.7 %collective-permute-done.2 = bf16[128,256]{1,0:T(8,128)(2,1)S(1)} collective-permute-done((bf16[128,256]{1,0:T(8,128)(2,1)S(1)}, bf16[128,256]{1,0:T(8,128)(2,1)S(1)}, u32[]{:S(2)}, u32[]{:S(2)}) %collective-permute-start.2) | collective-permute-done | bytes 65568 | tf_op jit(solution)/shard_map/ppermute | solution.py:316
  61.6 2.7 %collective-permute-start.3 = (bf16[128,256]{1,0:T(8,128)(2,1)S(1)}, bf16[128,256]{1,0:T(8,128)(2,1)S(1)}, u32[]{:S(2)}, u32[]{:S(2)}) collective-permute-start(bf16[128,256]{1,0:T(8,128)(2,1)S(1)} %add_convert_fusion.3), channel_id=1, source_target_pairs={{0,1},{1,0},{2,3},{3,2},{4,5},{5,4},{6,7},{7,6},{8,9},{9,8},{10,11... | collective-permute-start | bytes 196616 | tf_op jit(solution)/shard_map/ppermute | solution.py:307
  64.3 0.9 collective-permute-done.3
  65.2 0.5 up_projection.1
  65.8 23.7 %all_to_all.21 = bf16[16,16,2816]{2,1,0:T(8,128)(2,1)S(1)} all-to-all(bf16[16,16,2816]{2,1,0:T(8,128)(2,1)S(1)} %bitcast.23), channel_id=1, replica_groups=mesh['z'=4,'x'=4,'y'=4,'c'=2] {'z','x'}, dimensions={0} | all-to-all | bytes 2883584 | tf_op jit(solution)/shard_map/all_to_all | solution.py:346
  89.5 0.2 convert_reduce_fusion
  89.7 0.2 fusion.7
  90.1 22.8 %all_to_all.22 = bf16[16,16,2688]{2,1,0:T(8,128)(2,1)S(1)} all-to-all(bf16[16,16,2688]{2,1,0:T(8,128)(2,1)S(1)} %broadcast_in_dim.38), channel_id=1, replica_groups=mesh['z'=4,'x'=4,'y'=4,'c'=2] {'z','x'}, dimensions={0} | all-to-all | bytes 2752512 | tf_op jit(solution)/shard_map/all_to_all | solution.py:346
  112.9 0.6 fusion.9
  113.5 2.1 %collective-permute-start.4 = (bf16[128,256]{1,0:T(8,128)(2,1)S(1)}, bf16[128,256]{1,0:T(8,128)(2,1)S(1)}, u32[]{:S(2)}, u32[]{:S(2)}) collective-permute-start(bf16[128,256]{1,0:T(8,128)(2,1)S(1)} %dynamic-slice_convert_fusion), channel_id=1, source_target_pairs={{0,1},{1,0},{2,3},{3,2},{4,5},{5,4},{6,7},{7,6},{8,9},{9,8},{10,11... | collective-permute-start | bytes 196616 | tf_op jit(solution)/shard_map/ppermute | solution.py:307
  115.6 0.9 collective-permute-done.4
  116.7 3.0 %collective-permute-done.5 = bf16[128,256]{1,0:T(8,128)(2,1)S(1)} collective-permute-done((bf16[128,256]{1,0:T(8,128)(2,1)S(1)}, bf16[128,256]{1,0:T(8,128)(2,1)S(1)}, u32[]{:S(2)}, u32[]{:S(2)}) %collective-permute-start.5) | collective-permute-done | bytes 65568 | tf_op jit(solution)/shard_map/ppermute | solution.py:316
  119.7 2.8 %collective-permute-start.6 = (bf16[128,256]{1,0:T(8,128)(2,1)S(1)}, bf16[128,256]{1,0:T(8,128)(2,1)S(1)}, u32[]{:S(2)}, u32[]{:S(2)}) collective-permute-start(bf16[128,256]{1,0:T(8,128)(2,1)S(1)} %add_convert_fusion.1), channel_id=1, source_target_pairs={{2,4},{4,2},{6,0},{0,6},{3,5},{5,3},{7,1},{1,7},{10,12},{12,10},{1... | collective-permute-start | bytes 196616 | tf_op jit(solution)/shard_map/ppermute | solution.py:316
  122.6 1.7 %collective-permute-done.6 = bf16[128,256]{1,0:T(8,128)(2,1)S(1)} collective-permute-done((bf16[128,256]{1,0:T(8,128)(2,1)S(1)}, bf16[128,256]{1,0:T(8,128)(2,1)S(1)}, u32[]{:S(2)}, u32[]{:S(2)}) %collective-permute-start.6) | collective-permute-done | bytes 65568 | tf_op jit(solution)/shard_map/ppermute | solution.py:316
  124.4 2.7 %collective-permute-start.7 = (bf16[128,256]{1,0:T(8,128)(2,1)S(1)}, bf16[128,256]{1,0:T(8,128)(2,1)S(1)}, u32[]{:S(2)}, u32[]{:S(2)}) collective-permute-start(bf16[128,256]{1,0:T(8,128)(2,1)S(1)} %add_convert_fusion), channel_id=1, source_target_pairs={{0,1},{1,0},{2,3},{3,2},{4,5},{5,4},{6,7},{7,6},{8,9},{9,8},{10,11... | collective-permute-start | bytes 196616 | tf_op jit(solution)/shard_map/ppermute | solution.py:307
  127.0 0.9 collective-permute-done.7
  127.9 0.7 pad_maximum_fusion.1
  (55 shorter events, 0.8 us)
Async XLA Ops:
  0.6 112.3 %copy-start = (bf16[2688,256]{1,0:T(8,128)(2,1)S(1)}, bf16[2688,256]{1,0:T(8,128)(2,1)}, u32[]{:S(2)}) copy-start(bf16[2688,256]{1,0:T(8,128)(2,1)} %param.41) | copy-start | bytes 4128772
  0.6 1.7 %copy-start.4 = (bf16[256,256]{1,0:T(8,128)(2,1)S(1)}, bf16[256,256]{1,0:T(8,128)(2,1)}, u32[]{:S(2)}) copy-start(bf16[256,256]{1,0:T(8,128)(2,1)} %residual_ref.1) | copy-start | bytes 393220
  0.7 1.7 %copy-start.16 = (bf16[256,16]{0,1:T(8,128)(2,1)S(1)}, bf16[256,16]{0,1:T(8,128)(2,1)}, u32[]{:S(2)}) copy-start(bf16[256,16]{0,1:T(8,128)(2,1)} %param.29) | copy-start | bytes 24580
  0.7 1.7 %copy-start.15 = (bf16[256,2,128]{2,1,0:T(2,128)(2,1)S(1)}, bf16[256,2,128]{2,1,0:T(2,128)(2,1)}, u32[]{:S(2)}) copy-start(bf16[256,2,128]{2,1,0:T(2,128)(2,1)} %group_ref.1) | copy-start | bytes 393220
  0.7 1.7 %copy-start.17 = (f32[256]{0:T(256)S(1)}, f32[256]{0:T(256)}, u32[]{:S(2)}) copy-start(f32[256]{0:T(256)} %param.26) | copy-start | bytes 3076
  2.3 28.0 %slice-start = ((s8[8388608]{0:T(1024)(128)(4,1)}), s8[4194304]{0:T(1024)(128)(4,1)S(1)}, s32[]{:S(2)}) async-start(s8[8388608]{0:T(1024)(128)(4,1)} %bitcast.21), calls=%async_computation.4 | async-start | bytes 8388608
  2.4 28.0 %slice-start.1 = ((s8[8388608]{0:T(1024)(128)(4,1)}), s8[4194304]{0:T(1024)(128)(4,1)S(1)}, s32[]{:S(2)}) async-start(s8[8388608]{0:T(1024)(128)(4,1)} %bitcast.21), calls=%async_computation.5 | async-start | bytes 8388608
  3.2 27.1 %copy-start.2 = (f32[16,3,1024]{2,0,1:T(8,128)S(1)}, f32[16,3,1024]{2,0,1:T(8,128)}, u32[]{:S(2)}) copy-start(f32[16,3,1024]{2,0,1:T(8,128)} %param.24) | copy-start | bytes 589828
  3.2 27.1 %copy-start.3 = (f32[16,3,2,128]{3,2,1,0:T(2,128)S(1)}, f32[16,3,2,128]{3,2,1,0:T(2,128)}, u32[]{:S(2)}) copy-start(f32[16,3,2,128]{3,2,1,0:T(2,128)} %tail_group_ref.1) | copy-start | bytes 147460
  3.3 27.1 %copy-start.5 = (f32[4,1024]{1,0:T(4,128)S(1)}, f32[4,1024]{1,0:T(4,128)}, u32[]{:S(2)}) copy-start(f32[4,1024]{1,0:T(4,128)} %conv_mix_ref.1) | copy-start | bytes 49156
  3.3 27.1 %copy-start.6 = (f32[4,2,128]{2,1,0:T(2,128)S(1)}, f32[4,2,128]{2,1,0:T(2,128)}, u32[]{:S(2)}) copy-start(f32[4,2,128]{2,1,0:T(2,128)} %conv_group_ref.1) | copy-start | bytes 12292
  3.3 27.1 %copy-start.7 = (f32[1024]{0:T(1024)S(1)}, f32[1024]{0:T(1024)}, u32[]{:S(2)}) copy-start(f32[1024]{0:T(1024)} %param.32) | copy-start | bytes 12292
  3.3 27.1 %copy-start.8 = (f32[1024]{0:T(1024)S(1)}, f32[1024]{0:T(1024)}, u32[]{:S(2)}) copy-start(f32[1024]{0:T(1024)} %param.37) | copy-start | bytes 12292
  3.3 27.1 %copy-start.9 = (f32[2,128]{1,0:T(2,128)S(1)}, f32[2,128]{1,0:T(2,128)}, u32[]{:S(2)}) copy-start(f32[2,128]{1,0:T(2,128)} %bias_group_ref.1) | copy-start | bytes 3076
  3.3 27.0 %copy-start.11 = (s32[16]{0:T(128)S(1)}, s32[16]{0:T(128)}, u32[]{:S(2)}) copy-start(s32[16]{0:T(128)} %param.22) | copy-start | bytes 196
  3.3 27.0 %copy-start.12 = (f32[16]{0:T(128)S(1)}, f32[16]{0:T(128)}, u32[]{:S(2)}) copy-start(f32[16]{0:T(128)} %param.34) | copy-start | bytes 196
  3.3 27.0 %copy-start.13 = (f32[16]{0:T(128)S(1)}, f32[16]{0:T(128)}, u32[]{:S(2)}) copy-start(f32[16]{0:T(128)} %param.35) | copy-start | bytes 196
  3.4 27.0 %copy-start.14 = (f32[16]{0:T(128)S(1)}, f32[16]{0:T(128)}, u32[]{:S(2)}) copy-start(f32[16]{0:T(128)} %param.36) | copy-start | bytes 196
  33.8 13.7 %all-to-all-start.1 = ((bf16[16,16,1024]{2,1,0:T(8,128)(2,1)}), bf16[16,16,1024]{2,1,0:T(8,128)(2,1)S(1)}, u32[]{:S(2)}, u32[]{:S(2)}) async-start(bf16[16,16,1024]{2,1,0:T(8,128)(2,1)} %get-tuple-element.12), calls=%async_computation.1 | async-start | bytes 1048576 | tf_op jit(solution)/shard_map/all_to_all | solution.py:346
  44.4 20.9 %copy-start.1 = (bf16[256,2688]{1,0:T(8,128)(2,1)S(1)}, bf16[256,2688]{1,0:T(8,128)(2,1)}, u32[]{:S(2)}) copy-start(bf16[256,2688]{1,0:T(8,128)(2,1)} %up_ref.1) | copy-start | bytes 4128772
  44.4 20.9 %copy-start.10 = (f32[256]{0:T(256)S(1)}, f32[256]{0:T(256)}, u32[]{:S(2)}) copy-start(f32[256]{0:T(256)} %param.39) | copy-start | bytes 3076
  48.8 0.7 copy-start.18
  49.6 3.4 %collective-permute-start = (bf16[128,256]{1,0:T(8,128)(2,1)S(1)}, bf16[128,256]{1,0:T(8,128)(2,1)S(1)}, u32[]{:S(2)}, u32[]{:S(2)}) collective-permute-start(bf16[128,256]{1,0:T(8,128)(2,1)S(1)} %dynamic-slice_convert_fusion.1), channel_id=1, source_target_pairs={{0,1},{1,0},{2,3},{3,2},{4,5},{5,4},{6,7},{7,6},{8,9},{9,8},{10,11... | collective-permute-start | bytes 196616 | tf_op jit(solution)/shard_map/ppermute | solution.py:307
  53.9 3.2 %collective-permute-start.1 = (bf16[128,256]{1,0:T(8,128)(2,1)S(1)}, bf16[128,256]{1,0:T(8,128)(2,1)S(1)}, u32[]{:S(2)}, u32[]{:S(2)}) collective-permute-start(bf16[128,256]{1,0:T(8,128)(2,1)S(1)} %add_convert_fusion.5), channel_id=1, source_target_pairs={{0,2},{2,0},{4,6},{6,4},{1,3},{3,1},{5,7},{7,5},{8,10},{10,8},{12,... | collective-permute-start | bytes 196616 | tf_op jit(solution)/shard_map/ppermute | solution.py:316
  57.1 4.5 %collective-permute-start.2 = (bf16[128,256]{1,0:T(8,128)(2,1)S(1)}, bf16[128,256]{1,0:T(8,128)(2,1)S(1)}, u32[]{:S(2)}, u32[]{:S(2)}) collective-permute-start(bf16[128,256]{1,0:T(8,128)(2,1)S(1)} %add_convert_fusion.4), channel_id=1, source_target_pairs={{2,4},{4,2},{6,0},{0,6},{3,5},{5,3},{7,1},{1,7},{10,12},{12,10},{1... | collective-permute-start | bytes 196616 | tf_op jit(solution)/shard_map/ppermute | solution.py:316
  61.6 3.6 %collective-permute-start.3 = (bf16[128,256]{1,0:T(8,128)(2,1)S(1)}, bf16[128,256]{1,0:T(8,128)(2,1)S(1)}, u32[]{:S(2)}, u32[]{:S(2)}) collective-permute-start(bf16[128,256]{1,0:T(8,128)(2,1)S(1)} %add_convert_fusion.3), channel_id=1, source_target_pairs={{0,1},{1,0},{2,3},{3,2},{4,5},{5,4},{6,7},{7,6},{8,9},{9,8},{10,11... | collective-permute-start | bytes 196616 | tf_op jit(solution)/shard_map/ppermute | solution.py:307
  113.5 3.0 %collective-permute-start.4 = (bf16[128,256]{1,0:T(8,128)(2,1)S(1)}, bf16[128,256]{1,0:T(8,128)(2,1)S(1)}, u32[]{:S(2)}, u32[]{:S(2)}) collective-permute-start(bf16[128,256]{1,0:T(8,128)(2,1)S(1)} %dynamic-slice_convert_fusion), channel_id=1, source_target_pairs={{0,1},{1,0},{2,3},{3,2},{4,5},{5,4},{6,7},{7,6},{8,9},{9,8},{10,11... | collective-permute-start | bytes 196616 | tf_op jit(solution)/shard_map/ppermute | solution.py:307
  116.5 3.2 %collective-permute-start.5 = (bf16[128,256]{1,0:T(8,128)(2,1)S(1)}, bf16[128,256]{1,0:T(8,128)(2,1)S(1)}, u32[]{:S(2)}, u32[]{:S(2)}) collective-permute-start(bf16[128,256]{1,0:T(8,128)(2,1)S(1)} %add_convert_fusion.2), channel_id=1, source_target_pairs={{0,2},{2,0},{4,6},{6,4},{1,3},{3,1},{5,7},{7,5},{8,10},{10,8},{12,... | collective-permute-start | bytes 196616 | tf_op jit(solution)/shard_map/ppermute | solution.py:316
  119.7 4.5 %collective-permute-start.6 = (bf16[128,256]{1,0:T(8,128)(2,1)S(1)}, bf16[128,256]{1,0:T(8,128)(2,1)S(1)}, u32[]{:S(2)}, u32[]{:S(2)}) collective-permute-start(bf16[128,256]{1,0:T(8,128)(2,1)S(1)} %add_convert_fusion.1), channel_id=1, source_target_pairs={{2,4},{4,2},{6,0},{0,6},{3,5},{5,3},{7,1},{1,7},{10,12},{12,10},{1... | collective-permute-start | bytes 196616 | tf_op jit(solution)/shard_map/ppermute | solution.py:316
  124.4 3.6 %collective-permute-start.7 = (bf16[128,256]{1,0:T(8,128)(2,1)S(1)}, bf16[128,256]{1,0:T(8,128)(2,1)S(1)}, u32[]{:S(2)}, u32[]{:S(2)}) collective-permute-start(bf16[128,256]{1,0:T(8,128)(2,1)S(1)} %add_convert_fusion), channel_id=1, source_target_pairs={{0,1},{1,0},{2,3},{3,2},{4,5},{5,4},{6,7},{7,6},{8,9},{9,8},{10,11... | collective-permute-start | bytes 196616 | tf_op jit(solution)/shard_map/ppermute | solution.py:307

commit v6 on v5

--- a/solution.py
+++ b/solution.py
@@ -284,25 +284,6 @@
     )(u, decay, b, in_hbm(ssm_state))
 
 
-def up_kernel(middle_ref, norm_ref, up_ref, out_ref):
-    wide = middle_ref[...].astype(f32)
-    scaled = (wide * norm_ref[...]).astype(bf16)
-    width = up_ref.shape[1]
-    out_ref[:, width:] = norm_columns(wide, 0).astype(bf16)
-    out_ref[:, :width] = jnp.dot(scaled, up_ref[...], preferred_element_type=f32).astype(bf16)
-
-
-def up_projection(middle, norm, up):
-    return pl.pallas_call(
-        up_kernel,
-        out_shape=jax.ShapeDtypeStruct((middle.shape[0], up.shape[1] + LANES), bf16),
-        in_specs=[IN_VMEM] * 3,
-        out_specs=IN_VMEM,
-        compiler_params=SMALL,
-        name="up_projection",
-    )(middle, norm, up)
-
-
 def swap_core(value):
     return lax.ppermute(value, "c", [(0, 1), (1, 0)])
 
@@ -372,8 +353,17 @@
     state_out = state_update(ssm_state, u, decay, b)
     every_y, state_out = lax.optimization_barrier((every_y, state_out))
     middle = add_over_heads(residual, jnp.dot(every_y, out_weight, preferred_element_type=f32))
+    wide = middle.astype(f32)
+    scaled_two = (wide * norm_second).astype(bf16)
+    activation = jnp.dot(scaled_two, up_weight, preferred_element_type=f32).astype(bf16)
     hidden_dev = up_weight.shape[1]
-    sent = up_projection(middle, norm_second[None], up_weight).reshape(peers, rows_dev, -1)
+    total = jnp.sum(wide * wide, axis=1, keepdims=True)
+    high = lax.reduce_precision(total, 8, 7)
+    mid = lax.reduce_precision(total - high, 8, 7)
+    low = total - high - mid
+    lane = lax.broadcasted_iota(jnp.int32, (rows, LANES), 1)
+    columns = jnp.where(lane == 0, high, jnp.where(lane == 1, mid, jnp.where(lane == 2, low, 0.0))).astype(bf16)
+    sent = jnp.concatenate([activation, columns], axis=1).reshape(peers, rows_dev, hidden_dev + LANES)
     sums = exchange(sent, REQ).astype(f32).sum(axis=0)
     squares = sums[:, hidden_dev : hidden_dev + 1] + sums[:, hidden_dev + 1 : hidden_dev + 2] + sums[:, hidden_dev + 2 : hidden_dev + 3]
     inverse = lax.rsqrt(squares / width_all + eps)

time: 129 us -> 127 us (0.984)
  transfers between devices with their start and end apart: 9 -> 9, of which waited for: 9 -> 9; matrix products, arithmetic and copies ran while one was open for 0% -> 0% of each run, Pallas kernels for 5% -> 6%
where the time goes in v6:
time: 127 us; the launch traced here: 126 us
  blocking collectives  73.5 us (58%)
  starting transfers between devices  20.7 us (16%)
  waiting for transfers between devices  14.8 us (12%)
  Pallas kernels  11.1 us (9%)
  local copies, waits for them, and re-layouts  1.86 us (1%)
  other arithmetic  1.8 us (1%)
  matrix products  1.39 us (1%)
    all_to_all x3, blocking collectives, exchange(): return lax.all_to_all(value, axis, 0, 0, tiled=True)  73.5 us
    ppermute x4, starting transfers between devices, swap_core(): return lax.ppermute(value, 'c', [(0, 1), (1, 0)])  9.97 us
    ppermute x4, waiting for transfers between devices, ring_pairs(): return lax.ppermute(value, 'y', pairs)  8.16 us
    ppermute x4, starting transfers between devices, ring_pairs(): return lax.ppermute(value, 'y', pairs)  7.16 us
    pallas_call x1, Pallas kernels, state_update(): pl.pallas_call(make_update_kernel(rows, heads, head_dim, state), in_specs...  6.98 us
    ppermute x4, waiting for transfers between devices, swap_core(): return lax.ppermute(value, 'c', [(0, 1), (1, 0)])  3.6 us
    all_to_all x1, starting transfers between devices, exchange(): return lax.all_to_all(value, axis, 0, 0, tiled=True)  3.57 us
    pallas_call x1, Pallas kernels, mixer_step(): pl.pallas_call(make_mixer_kernel(width_all, (pieces, rows, heads, head_di...  3.29 us
  transfers between devices with their start and end apart: 9, of which 9 were waited for; matrix products, arithmetic and copies ran while one was open for 0% of the time, Pallas kernels for 6%

profile of v6, /device:TPU:1, one launch (start us, length us, event | category | flops | bytes accessed | tf_op | source)
XLA Modules:
  0.0 126.3 jit_solution(14096968032600676928)
XLA Ops:
  0.7 1.6 %copy.26 = bf16[32,8,2,1024]{3,1,2,0:T(8,128)(2,1)S(1)} copy(bf16[32,8,2,1024]{3,2,1,0:T(2,128)(2,1)} %bitcast.37) | data formatting | bytes 2097152
  2.4 0.9 input_projection.1
  3.4 26.9 %all_to_all.20.arrived_ref = bf16[16,16,2432]{2,1,0:T(8,128)(2,1)S(1)} all-to-all(bf16[16,16,2432]{2,1,0:T(8,128)(2,1)S(1)} %bitcast.23), channel_id=1, replica_groups=mesh['z'=4,'x'=4,'y'=4,'c'=2] {'z','x'}, dimensions={0} | all-to-all | bytes 2490368 | tf_op jit(solution)/shard_map/all_to_all | solution.py:327
  30.4 3.3 %mixer_step.1 = (bf16[16,16,1024]{2,1,0:T(8,128)(2,1)}, f32[3,16,1024]{2,1,0:T(8,128)}, f32[16,3,2,128]{3,2,1,0:T(2,128)}, f32[8,16,128]{2,1,0:T(8,128)S(1)}, f3...) custom-call(bf16[16,16,2432]{2,1,0:T(8,128)(2,1)S(1)} %all_to_all.20.arrived_ref, s32[1,16]{1,0:T(1,128)S(1)} %bitcast.28, ...), custom_call_target="tpu_custom_call" | custom-call | tf_op jit(solution)/shard_map/mixer_step/pallas_call | solution.py:215
  33.7 3.6 %all-to-all-start.1 = ((bf16[16,16,1024]{2,1,0:T(8,128)(2,1)}), bf16[16,16,1024]{2,1,0:T(8,128)(2,1)S(1)}, u32[]{:S(2)}, u32[]{:S(2)}) async-start(bf16[16,16,1024]{2,1,0:T(8,128)(2,1)} %get-tuple-element.12), calls=%async_computation.1 | async-start | bytes 1048576 | tf_op jit(solution)/shard_map/all_to_all | solution.py:327
  37.3 7.0 %state_update.1 = f32[16,16,64,128]{3,2,1,0:T(8,128)} custom-call(f32[8,16,128]{2,1,0:T(8,128)S(1)} %get-tuple-element.13.u_ref, f32[16,128]{1,0:T(8,128)S(1)} %get-tuple-element.14.decay_ref, f32[16,128]{1,0:T(8,128)S(1)} %get-tuple-element.15.b_ref, f32[16,16,64,128]{3,2,1,0:T(8,128)} %state_ref.3), custom_call_target="tpu_custom_call" | custom-call | tf_op jit(solution)/shard_map/state_update/pallas_call | solution.py:272
  44.3 3.1 %all-to-all-done.1 = bf16[16,16,1024]{2,1,0:T(8,128)(2,1)S(1)} async-done(((bf16[16,16,1024]{2,1,0:T(8,128)(2,1)}), bf16[16,16,1024]{2,1,0:T(8,128)(2,1)S(1)}, u32[]{:S(2)}, u32[]{:S(2)}) %all-to-all-start.1) | async-done | bytes 524320 | tf_op jit(solution)/shard_map/all_to_all | solution.py:327
  47.4 0.3 fusion.14
  47.7 2.5 %collective-permute-start = (bf16[128,256]{1,0:T(8,128)(2,1)S(1)}, bf16[128,256]{1,0:T(8,128)(2,1)S(1)}, u32[]{:S(2)}, u32[]{:S(2)}) collective-permute-start(bf16[128,256]{1,0:T(8,128)(2,1)S(1)} %dynamic-slice_convert_fusion.1), channel_id=1, source_target_pairs={{0,1},{1,0},{2,3},{3,2},{4,5},{5,4},{6,7},{7,6},{8,9},{9,8},{10,11... | collective-permute-start | bytes 196616 | tf_op jit(solution)/shard_map/ppermute | solution.py:288
  50.2 0.9 collective-permute-done
  51.1 1.4 %collective-permute-start.1 = (bf16[128,256]{1,0:T(8,128)(2,1)S(1)}, bf16[128,256]{1,0:T(8,128)(2,1)S(1)}, u32[]{:S(2)}, u32[]{:S(2)}) collective-permute-start(bf16[128,256]{1,0:T(8,128)(2,1)S(1)} %add_convert_fusion.5), channel_id=1, source_target_pairs={{0,2},{2,0},{4,6},{6,4},{1,3},{3,1},{5,7},{7,5},{8,10},{10,8},{12,... | collective-permute-start | bytes 196616 | tf_op jit(solution)/shard_map/ppermute | solution.py:297
  52.5 1.8 %collective-permute-done.1 = bf16[128,256]{1,0:T(8,128)(2,1)S(1)} collective-permute-done((bf16[128,256]{1,0:T(8,128)(2,1)S(1)}, bf16[128,256]{1,0:T(8,128)(2,1)S(1)}, u32[]{:S(2)}, u32[]{:S(2)}) %collective-permute-start.1) | collective-permute-done | bytes 65568 | tf_op jit(solution)/shard_map/ppermute | solution.py:297
  54.3 2.8 %collective-permute-start.2 = (bf16[128,256]{1,0:T(8,128)(2,1)S(1)}, bf16[128,256]{1,0:T(8,128)(2,1)S(1)}, u32[]{:S(2)}, u32[]{:S(2)}) collective-permute-start(bf16[128,256]{1,0:T(8,128)(2,1)S(1)} %add_convert_fusion.4), channel_id=1, source_target_pairs={{2,4},{4,2},{6,0},{0,6},{3,5},{5,3},{7,1},{1,7},{10,12},{12,10},{1... | collective-permute-start | bytes 196616 | tf_op jit(solution)/shard_map/ppermute | solution.py:297
  57.1 1.6 %collective-permute-done.2 = bf16[128,256]{1,0:T(8,128)(2,1)S(1)} collective-permute-done((bf16[128,256]{1,0:T(8,128)(2,1)S(1)}, bf16[128,256]{1,0:T(8,128)(2,1)S(1)}, u32[]{:S(2)}, u32[]{:S(2)}) %collective-permute-start.2) | collective-permute-done | bytes 65568 | tf_op jit(solution)/shard_map/ppermute | solution.py:297
  58.8 2.7 %collective-permute-start.3 = (bf16[128,256]{1,0:T(8,128)(2,1)S(1)}, bf16[128,256]{1,0:T(8,128)(2,1)S(1)}, u32[]{:S(2)}, u32[]{:S(2)}) collective-permute-start(bf16[128,256]{1,0:T(8,128)(2,1)S(1)} %add_convert_fusion.3), channel_id=1, source_target_pairs={{0,1},{1,0},{2,3},{3,2},{4,5},{5,4},{6,7},{7,6},{8,9},{9,8},{10,11... | collective-permute-start | bytes 196616 | tf_op jit(solution)/shard_map/ppermute | solution.py:288
  61.5 0.9 collective-permute-done.3
  62.6 0.6 convolution_convert_fusion
  63.1 0.2 select_convert_fusion
  63.4 23.7 %all_to_all.21 = bf16[16,16,2816]{2,1,0:T(8,128)(2,1)S(1)} all-to-all(bf16[16,16,2816]{2,1,0:T(8,128)(2,1)S(1)} %bitcast.34), channel_id=1, replica_groups=mesh['z'=4,'x'=4,'y'=4,'c'=2] {'z','x'}, dimensions={0} | all-to-all | bytes 2883584 | tf_op jit(solution)/shard_map/all_to_all | solution.py:327
  87.1 0.2 convert_reduce_fusion
  87.3 0.2 fusion.11
  87.7 22.9 %all_to_all.22 = bf16[16,16,2688]{2,1,0:T(8,128)(2,1)S(1)} all-to-all(bf16[16,16,2688]{2,1,0:T(8,128)(2,1)S(1)} %broadcast_in_dim.65), channel_id=1, replica_groups=mesh['z'=4,'x'=4,'y'=4,'c'=2] {'z','x'}, dimensions={0} | all-to-all | bytes 2752512 | tf_op jit(solution)/shard_map/all_to_all | solution.py:327
  110.6 0.5 fusion.15
  111.2 2.1 %collective-permute-start.4 = (bf16[128,256]{1,0:T(8,128)(2,1)S(1)}, bf16[128,256]{1,0:T(8,128)(2,1)S(1)}, u32[]{:S(2)}, u32[]{:S(2)}) collective-permute-start(bf16[128,256]{1,0:T(8,128)(2,1)S(1)} %dynamic-slice_convert_fusion), channel_id=1, source_target_pairs={{0,1},{1,0},{2,3},{3,2},{4,5},{5,4},{6,7},{7,6},{8,9},{9,8},{10,11... | collective-permute-start | bytes 196616 | tf_op jit(solution)/shard_map/ppermute | solution.py:288
  113.3 0.9 collective-permute-done.4
  114.3 0.2 collective-permute-start.5
  114.4 3.0 %collective-permute-done.5 = bf16[128,256]{1,0:T(8,128)(2,1)S(1)} collective-permute-done((bf16[128,256]{1,0:T(8,128)(2,1)S(1)}, bf16[128,256]{1,0:T(8,128)(2,1)S(1)}, u32[]{:S(2)}, u32[]{:S(2)}) %collective-permute-start.5) | collective-permute-done | bytes 65568 | tf_op jit(solution)/shard_map/ppermute | solution.py:297
  117.5 2.8 %collective-permute-start.6 = (bf16[128,256]{1,0:T(8,128)(2,1)S(1)}, bf16[128,256]{1,0:T(8,128)(2,1)S(1)}, u32[]{:S(2)}, u32[]{:S(2)}) collective-permute-start(bf16[128,256]{1,0:T(8,128)(2,1)S(1)} %add_convert_fusion.1), channel_id=1, source_target_pairs={{2,4},{4,2},{6,0},{0,6},{3,5},{5,3},{7,1},{1,7},{10,12},{12,10},{1... | collective-permute-start | bytes 196616 | tf_op jit(solution)/shard_map/ppermute | solution.py:297
  120.3 1.7 %collective-permute-done.6 = bf16[128,256]{1,0:T(8,128)(2,1)S(1)} collective-permute-done((bf16[128,256]{1,0:T(8,128)(2,1)S(1)}, bf16[128,256]{1,0:T(8,128)(2,1)S(1)}, u32[]{:S(2)}, u32[]{:S(2)}) %collective-permute-start.6) | collective-permute-done | bytes 65568 | tf_op jit(solution)/shard_map/ppermute | solution.py:297
  122.1 2.7 %collective-permute-start.7 = (bf16[128,256]{1,0:T(8,128)(2,1)S(1)}, bf16[128,256]{1,0:T(8,128)(2,1)S(1)}, u32[]{:S(2)}, u32[]{:S(2)}) collective-permute-start(bf16[128,256]{1,0:T(8,128)(2,1)S(1)} %add_convert_fusion), channel_id=1, source_target_pairs={{0,1},{1,0},{2,3},{3,2},{4,5},{5,4},{6,7},{7,6},{8,9},{9,8},{10,11... | collective-permute-start | bytes 196616 | tf_op jit(solution)/shard_map/ppermute | solution.py:288
  124.7 0.9 collective-permute-done.7
  125.7 0.7 pad_maximum_fusion.2
  (60 shorter events, 0.8 us)
Async XLA Ops:
  0.6 61.9 %copy-start = (bf16[256,2688]{1,0:T(8,128)(2,1)S(1)}, bf16[256,2688]{1,0:T(8,128)(2,1)}, u32[]{:S(2)}) copy-start(bf16[256,2688]{1,0:T(8,128)(2,1)} %param.40) | copy-start | bytes 4128772
  0.6 1.7 %copy-start.3 = (bf16[256,256]{1,0:T(8,128)(2,1)S(1)}, bf16[256,256]{1,0:T(8,128)(2,1)}, u32[]{:S(2)}) copy-start(bf16[256,256]{1,0:T(8,128)(2,1)} %residual_ref.1) | copy-start | bytes 393220
  0.7 1.7 %copy-start.14 = (bf16[256,16]{0,1:T(8,128)(2,1)S(1)}, bf16[256,16]{0,1:T(8,128)(2,1)}, u32[]{:S(2)}) copy-start(bf16[256,16]{0,1:T(8,128)(2,1)} %param.29) | copy-start | bytes 24580
  0.7 1.7 %copy-start.13 = (bf16[256,2,128]{2,1,0:T(2,128)(2,1)S(1)}, bf16[256,2,128]{2,1,0:T(2,128)(2,1)}, u32[]{:S(2)}) copy-start(bf16[256,2,128]{2,1,0:T(2,128)(2,1)} %group_ref.1) | copy-start | bytes 393220
  0.7 1.7 %copy-start.15 = (f32[256]{0:T(256)S(1)}, f32[256]{0:T(256)}, u32[]{:S(2)}) copy-start(f32[256]{0:T(256)} %param.26) | copy-start | bytes 3076
  2.3 28.0 %slice-start = ((s8[8388608]{0:T(1024)(128)(4,1)}), s8[4194304]{0:T(1024)(128)(4,1)S(1)}, s32[]{:S(2)}) async-start(s8[8388608]{0:T(1024)(128)(4,1)} %bitcast.21), calls=%async_computation.4 | async-start | bytes 8388608
  2.4 28.0 %slice-start.1 = ((s8[8388608]{0:T(1024)(128)(4,1)}), s8[4194304]{0:T(1024)(128)(4,1)S(1)}, s32[]{:S(2)}) async-start(s8[8388608]{0:T(1024)(128)(4,1)} %bitcast.21), calls=%async_computation.5 | async-start | bytes 8388608
  3.2 27.1 %copy-start.1 = (f32[16,3,1024]{2,0,1:T(8,128)S(1)}, f32[16,3,1024]{2,0,1:T(8,128)}, u32[]{:S(2)}) copy-start(f32[16,3,1024]{2,0,1:T(8,128)} %param.24) | copy-start | bytes 589828
  3.3 27.1 %copy-start.2 = (f32[16,3,2,128]{3,2,1,0:T(2,128)S(1)}, f32[16,3,2,128]{3,2,1,0:T(2,128)}, u32[]{:S(2)}) copy-start(f32[16,3,2,128]{3,2,1,0:T(2,128)} %tail_group_ref.1) | copy-start | bytes 147460
  3.3 27.1 %copy-start.4 = (f32[4,1024]{1,0:T(4,128)S(1)}, f32[4,1024]{1,0:T(4,128)}, u32[]{:S(2)}) copy-start(f32[4,1024]{1,0:T(4,128)} %conv_mix_ref.1) | copy-start | bytes 49156
  3.3 27.1 %copy-start.5 = (f32[4,2,128]{2,1,0:T(2,128)S(1)}, f32[4,2,128]{2,1,0:T(2,128)}, u32[]{:S(2)}) copy-start(f32[4,2,128]{2,1,0:T(2,128)} %conv_group_ref.1) | copy-start | bytes 12292
  3.3 27.1 %copy-start.6 = (f32[1024]{0:T(1024)S(1)}, f32[1024]{0:T(1024)}, u32[]{:S(2)}) copy-start(f32[1024]{0:T(1024)} %param.32) | copy-start | bytes 12292
  3.3 27.1 %copy-start.7 = (f32[1024]{0:T(1024)S(1)}, f32[1024]{0:T(1024)}, u32[]{:S(2)}) copy-start(f32[1024]{0:T(1024)} %param.37) | copy-start | bytes 12292
  3.3 27.1 %copy-start.8 = (f32[2,128]{1,0:T(2,128)S(1)}, f32[2,128]{1,0:T(2,128)}, u32[]{:S(2)}) copy-start(f32[2,128]{1,0:T(2,128)} %bias_group_ref.1) | copy-start | bytes 3076
  3.3 27.0 %copy-start.9 = (s32[16]{0:T(128)S(1)}, s32[16]{0:T(128)}, u32[]{:S(2)}) copy-start(s32[16]{0:T(128)} %param.22) | copy-start | bytes 196
  3.3 27.0 %copy-start.10 = (f32[16]{0:T(128)S(1)}, f32[16]{0:T(128)}, u32[]{:S(2)}) copy-start(f32[16]{0:T(128)} %param.34) | copy-start | bytes 196
  3.3 27.0 %copy-start.11 = (f32[16]{0:T(128)S(1)}, f32[16]{0:T(128)}, u32[]{:S(2)}) copy-start(f32[16]{0:T(128)} %param.35) | copy-start | bytes 196
  3.4 27.0 %copy-start.12 = (f32[16]{0:T(128)S(1)}, f32[16]{0:T(128)}, u32[]{:S(2)}) copy-start(f32[16]{0:T(128)} %param.36) | copy-start | bytes 196
  33.7 13.7 %all-to-all-start.1 = ((bf16[16,16,1024]{2,1,0:T(8,128)(2,1)}), bf16[16,16,1024]{2,1,0:T(8,128)(2,1)S(1)}, u32[]{:S(2)}, u32[]{:S(2)}) async-start(bf16[16,16,1024]{2,1,0:T(8,128)(2,1)} %get-tuple-element.12), calls=%async_computation.1 | async-start | bytes 1048576 | tf_op jit(solution)/shard_map/all_to_all | solution.py:327
  37.3 10.1 %copy-start.17 = (bf16[1024,256]{1,0:T(8,128)(2,1)S(1)}, bf16[1024,256]{1,0:T(8,128)(2,1)}, u32[]{:S(2)}) copy-start(bf16[1024,256]{1,0:T(8,128)(2,1)} %param.38) | copy-start | bytes 1572868
  44.3 18.3 %copy-start.18 = (f32[256]{0:T(256)S(1)}, f32[256]{0:T(256)}, u32[]{:S(2)}) copy-start(f32[256]{0:T(256)} %param.39) | copy-start | bytes 3076
  47.7 3.4 %collective-permute-start = (bf16[128,256]{1,0:T(8,128)(2,1)S(1)}, bf16[128,256]{1,0:T(8,128)(2,1)S(1)}, u32[]{:S(2)}, u32[]{:S(2)}) collective-permute-start(bf16[128,256]{1,0:T(8,128)(2,1)S(1)} %dynamic-slice_convert_fusion.1), channel_id=1, source_target_pairs={{0,1},{1,0},{2,3},{3,2},{4,5},{5,4},{6,7},{7,6},{8,9},{9,8},{10,11... | collective-permute-start | bytes 196616 | tf_op jit(solution)/shard_map/ppermute | solution.py:288
  51.1 3.2 %collective-permute-start.1 = (bf16[128,256]{1,0:T(8,128)(2,1)S(1)}, bf16[128,256]{1,0:T(8,128)(2,1)S(1)}, u32[]{:S(2)}, u32[]{:S(2)}) collective-permute-start(bf16[128,256]{1,0:T(8,128)(2,1)S(1)} %add_convert_fusion.5), channel_id=1, source_target_pairs={{0,2},{2,0},{4,6},{6,4},{1,3},{3,1},{5,7},{7,5},{8,10},{10,8},{12,... | collective-permute-start | bytes 196616 | tf_op jit(solution)/shard_map/ppermute | solution.py:297
  54.3 4.5 %collective-permute-start.2 = (bf16[128,256]{1,0:T(8,128)(2,1)S(1)}, bf16[128,256]{1,0:T(8,128)(2,1)S(1)}, u32[]{:S(2)}, u32[]{:S(2)}) collective-permute-start(bf16[128,256]{1,0:T(8,128)(2,1)S(1)} %add_convert_fusion.4), channel_id=1, source_target_pairs={{2,4},{4,2},{6,0},{0,6},{3,5},{5,3},{7,1},{1,7},{10,12},{12,10},{1... | collective-permute-start | bytes 196616 | tf_op jit(solution)/shard_map/ppermute | solution.py:297
  58.8 3.6 %collective-permute-start.3 = (bf16[128,256]{1,0:T(8,128)(2,1)S(1)}, bf16[128,256]{1,0:T(8,128)(2,1)S(1)}, u32[]{:S(2)}, u32[]{:S(2)}) collective-permute-start(bf16[128,256]{1,0:T(8,128)(2,1)S(1)} %add_convert_fusion.3), channel_id=1, source_target_pairs={{0,1},{1,0},{2,3},{3,2},{4,5},{5,4},{6,7},{7,6},{8,9},{9,8},{10,11... | collective-permute-start | bytes 196616 | tf_op jit(solution)/shard_map/ppermute | solution.py:288
  87.7 22.9 %copy-start.16 = (bf16[2688,256]{1,0:T(8,128)(2,1)S(1)}, bf16[2688,256]{1,0:T(8,128)(2,1)}, u32[]{:S(2)}) copy-start(bf16[2688,256]{1,0:T(8,128)(2,1)} %param.41) | copy-start | bytes 4128772
  111.2 3.0 %collective-permute-start.4 = (bf16[128,256]{1,0:T(8,128)(2,1)S(1)}, bf16[128,256]{1,0:T(8,128)(2,1)S(1)}, u32[]{:S(2)}, u32[]{:S(2)}) collective-permute-start(bf16[128,256]{1,0:T(8,128)(2,1)S(1)} %dynamic-slice_convert_fusion), channel_id=1, source_target_pairs={{0,1},{1,0},{2,3},{3,2},{4,5},{5,4},{6,7},{7,6},{8,9},{9,8},{10,11... | collective-permute-start | bytes 196616 | tf_op jit(solution)/shard_map/ppermute | solution.py:288
  114.3 3.2 %collective-permute-start.5 = (bf16[128,256]{1,0:T(8,128)(2,1)S(1)}, bf16[128,256]{1,0:T(8,128)(2,1)S(1)}, u32[]{:S(2)}, u32[]{:S(2)}) collective-permute-start(bf16[128,256]{1,0:T(8,128)(2,1)S(1)} %add_convert_fusion.2), channel_id=1, source_target_pairs={{0,2},{2,0},{4,6},{6,4},{1,3},{3,1},{5,7},{7,5},{8,10},{10,8},{12,... | collective-permute-start | bytes 196616 | tf_op jit(solution)/shard_map/ppermute | solution.py:297
  117.5 4.5 %collective-permute-start.6 = (bf16[128,256]{1,0:T(8,128)(2,1)S(1)}, bf16[128,256]{1,0:T(8,128)(2,1)S(1)}, u32[]{:S(2)}, u32[]{:S(2)}) collective-permute-start(bf16[128,256]{1,0:T(8,128)(2,1)S(1)} %add_convert_fusion.1), channel_id=1, source_target_pairs={{2,4},{4,2},{6,0},{0,6},{3,5},{5,3},{7,1},{1,7},{10,12},{12,10},{1... | collective-permute-start | bytes 196616 | tf_op jit(solution)/shard_map/ppermute | solution.py:297
  122.1 3.6 %collective-permute-start.7 = (bf16[128,256]{1,0:T(8,128)(2,1)S(1)}, bf16[128,256]{1,0:T(8,128)(2,1)S(1)}, u32[]{:S(2)}, u32[]{:S(2)}) collective-permute-start(bf16[128,256]{1,0:T(8,128)(2,1)S(1)} %add_convert_fusion), channel_id=1, source_target_pairs={{0,1},{1,0},{2,3},{3,2},{4,5},{5,4},{6,7},{7,6},{8,9},{9,8},{10,11... | collective-permute-start | bytes 196616 | tf_op jit(solution)/shard_map/ppermute | solution.py:288

commit v7 on v6

--- a/solution.py
+++ b/solution.py
@@ -297,30 +297,50 @@
     return lax.ppermute(value, "y", pairs)
 
 
-def head_sum_half(partial):
-    half = partial.shape[0] // 2
-    core = lax.axis_index("c")
-    mine = lax.dynamic_slice_in_dim(partial, core * half, half, 0)
-    theirs = lax.dynamic_slice_in_dim(partial, (1 - core) * half, half, 0).astype(bf16)
-    total = mine + swap_core(theirs).astype(f32)
+def ring_sum(total):
     for first in (0, 1):
         sent = total.astype(bf16)
         total = sent.astype(f32) + ring_pairs(sent, first).astype(f32)
-    return total, core
-
-
-def both_halves(half, core):
+    return total
+
+
+def rows_from(value, start, count):
+    return lax.dynamic_slice(value, (start, jnp.uint32(0)), (count, value.shape[1]))
+
+
+def head_sum_half(partial, starts):
+    half = partial.shape[0] // 2
+    mine = rows_from(partial, starts[0], half)
+    theirs = rows_from(partial, starts[1], half).astype(bf16)
+    return ring_sum(mine + swap_core(theirs).astype(f32))
+
+
+def both_halves(half, core, axis=0):
     other = swap_core(half)
     first = jnp.where(core == 0, half, other)
     second = jnp.where(core == 0, other, half)
-    return jnp.concatenate([first, second], axis=0)
-
-
-def add_over_heads(base, partial):
-    total, core = head_sum_half(partial)
-    half = total.shape[0]
-    mine = lax.dynamic_slice_in_dim(base, core * half, half, 0).astype(f32)
+    return jnp.concatenate([first, second], axis=axis)
+
+
+def add_over_heads(base, partial, core, starts):
+    total = head_sum_half(partial, starts)
+    mine = rows_from(base, starts[0], total.shape[0]).astype(f32)
     return both_halves((mine + total).astype(bf16), core)
+
+
+def of_core(value, core):
+    return lax.dynamic_index_in_dim(value, core, 1, keepdims=False)
+
+
+def add_mixer(residual, arrived, own_weight, other_weight, core):
+    peers, _, rows, channels = arrived.shape
+    own = of_core(arrived, core).reshape(peers * rows, channels)
+    other = of_core(arrived, 1 - core).reshape(peers * rows, channels)
+    partial = jnp.dot(own, own_weight, preferred_element_type=f32)
+    total = ring_sum(partial + jnp.dot(other, other_weight, preferred_element_type=f32))
+    mine = of_core(residual.reshape(peers, 2, rows, -1), core).reshape(peers * rows, -1).astype(f32)
+    half = (mine + total).astype(bf16).reshape(peers, 1, rows, -1)
+    return both_halves(half, core, 1).reshape(residual.shape)
 
 
 def exchange(value, axis):
@@ -344,15 +364,20 @@
     width_all = width_dev * peers
     mix_flat = mix_weight.reshape(width_dev, -1)
     pieces = input_projection(residual, norm_first[None], mix_flat, group_weight, step_weight.T)
+    other_weight = swap_core(out_weight)
     arrived = exchange(pieces.reshape(peers, rows_dev, -1), REQ)
     copies, tail_mix_out, tail_group_out, u, decay, b = mixer_step(
         arrived, lengths, tail_mix, tail_group, conv_mix, conv_group, bias_mix, bias_group, step_bias,
         decay_log, skip_gain, gate_gain, ssm_state, width_all,
     )
-    every_y = exchange(copies, REQ).reshape(rows, -1)
+    every_y = exchange(copies.reshape(2 * peers, rows_dev // 2, -1), REQ + ("c",))
     state_out = state_update(ssm_state, u, decay, b)
-    every_y, state_out = lax.optimization_barrier((every_y, state_out))
-    middle = add_over_heads(residual, jnp.dot(every_y, out_weight, preferred_element_type=f32))
+    core = lax.axis_index("c")
+    place = core.astype(jnp.uint32)
+    starts = (place * jnp.uint32(rows // 2), (jnp.uint32(1) - place) * jnp.uint32(rows // 2))
+    every_y, state_out, core, starts = lax.optimization_barrier((every_y, state_out, core, starts))
+    every_y = every_y.reshape(peers, 2, rows_dev // 2, -1)
+    middle = add_mixer(residual, every_y, out_weight, other_weight, core)
     wide = middle.astype(f32)
     scaled_two = (wide * norm_second).astype(bf16)
     activation = jnp.dot(scaled_two, up_weight, preferred_element_type=f32).astype(bf16)
@@ -369,7 +394,8 @@
     inverse = lax.rsqrt(squares / width_all + eps)
     hidden = jnp.square(jax.nn.relu(sums[:, :hidden_dev] * inverse)).astype(bf16)
     every_hidden = to_everyone(hidden, REQ)
-    residual_out = add_over_heads(middle, jnp.dot(every_hidden, down_weight, preferred_element_type=f32))
+    projected = jnp.dot(every_hidden, down_weight, preferred_element_type=f32)
+    residual_out = add_over_heads(middle, projected, core, starts)
     return residual_out, state_out, jnp.transpose(tail_mix_out, (1, 0, 2)), tail_group_out
 
 

time: 127 us -> 127 us (level)
    ppermute x4, starting transfers between devices: 9.97 us -> 7.96 us  [swap_core(): return lax.ppermute(value, 'c', [(0, 1), (1, 0)])]
    all_to_all x1, starting transfers between devices: 3.57 us -> 5.32 us  [exchange(): return lax.all_to_all(value, axis, 0, 0, tiled=True)]
  transfers between devices with their start and end apart: 9 -> 9, of which waited for: 9 -> 8; matrix products, arithmetic and copies ran while one was open for 0% -> 0% of each run, Pallas kernels for 6% -> 5%
where the time goes in v7:
time: 127 us; the launch traced here: 126 us
  blocking collectives  73.5 us (58%)
  starting transfers between devices  20.4 us (16%)
  waiting for transfers between devices  15.1 us (12%)
  Pallas kernels  11.1 us (9%)
  local copies, waits for them, and re-layouts  1.96 us (2%)
  other arithmetic  1.75 us (1%)
  matrix products  1.57 us (1%)
    all_to_all x3, blocking collectives, exchange(): return lax.all_to_all(value, axis, 0, 0, tiled=True)  73.5 us
    ppermute x4, waiting for transfers between devices, ring_pairs(): return lax.ppermute(value, 'y', pairs)  8.17 us
    ppermute x4, starting transfers between devices, swap_core(): return lax.ppermute(value, 'c', [(0, 1), (1, 0)])  7.96 us
    ppermute x4, starting transfers between devices, ring_pairs(): return lax.ppermute(value, 'y', pairs)  7.13 us
    pallas_call x1, Pallas kernels, state_update(): pl.pallas_call(make_update_kernel(rows, heads, head_dim, state), in_specs...  6.91 us
    all_to_all x1, starting transfers between devices, exchange(): return lax.all_to_all(value, axis, 0, 0, tiled=True)  5.32 us
    all_to_all x1, waiting for transfers between devices, exchange(): return lax.all_to_all(value, axis, 0, 0, tiled=True)  4.19 us
    pallas_call x1, Pallas kernels, mixer_step(): pl.pallas_call(make_mixer_kernel(width_all, (pieces, rows, heads, head_di...  3.29 us
  transfers between devices with their start and end apart: 9, of which 8 were waited for; matrix products, arithmetic and copies ran while one was open for 0% of the time, Pallas kernels for 5%

profile of v7, /device:TPU:1, one launch (start us, length us, event | category | flops | bytes accessed | tf_op | source)
XLA Modules:
  0.0 126.4 jit_solution(11041209989730460061)
XLA Ops:
  0.7 1.6 %copy.38 = bf16[32,8,2,1024]{3,1,2,0:T(8,128)(2,1)S(1)} copy(bf16[32,8,2,1024]{3,2,1,0:T(2,128)(2,1)} %bitcast.60) | data formatting | bytes 2097152
  2.4 0.9 input_projection.1
  3.4 26.9 %all_to_all.20.arrived_ref = bf16[16,16,2432]{2,1,0:T(8,128)(2,1)S(1)} all-to-all(bf16[16,16,2432]{2,1,0:T(8,128)(2,1)S(1)} %bitcast.43), channel_id=1, replica_groups=mesh['z'=4,'x'=4,'y'=4,'c'=2] {'z','x'}, dimensions={0} | all-to-all | bytes 2490368 | tf_op jit(solution)/shard_map/all_to_all | solution.py:347
  30.4 3.3 %mixer_step.1 = (bf16[16,16,1024]{2,1,0:T(8,128)(2,1)}, f32[3,16,1024]{2,1,0:T(8,128)}, f32[16,3,2,128]{3,2,1,0:T(2,128)}, f32[8,16,128]{2,1,0:T(8,128)S(1)}, f3...) custom-call(bf16[16,16,2432]{2,1,0:T(8,128)(2,1)S(1)} %all_to_all.20.arrived_ref, s32[1,16]{1,0:T(1,128)S(1)} %bitcast.50, ...), custom_call_target="tpu_custom_call" | custom-call | tf_op jit(solution)/shard_map/mixer_step/pallas_call | solution.py:215
  33.7 5.3 %all-to-all-start.1 = ((bf16[32,8,1024]{2,1,0:T(8,128)(2,1)}), bf16[32,8,1024]{2,1,0:T(8,128)(2,1)S(1)}, u32[]{:S(2)}, u32[]{:S(2)}) async-start(bf16[32,8,1024]{2,1,0:T(8,128)(2,1)} %bitcast.10), calls=%async_computation.1 | async-start | bytes 1048576 | tf_op jit(solution)/shard_map/all_to_all | solution.py:347
  39.1 0.4 collective-permute-start
  39.5 6.9 %state_update.1 = f32[16,16,64,128]{3,2,1,0:T(8,128)} custom-call(f32[8,16,128]{2,1,0:T(8,128)S(1)} %get-tuple-element.16.u_ref, f32[16,128]{1,0:T(8,128)S(1)} %get-tuple-element.17.decay_ref, f32[16,128]{1,0:T(8,128)S(1)} %get-tuple-element.18.b_ref, f32[16,16,64,128]{3,2,1,0:T(8,128)} %state_ref.3), custom_call_target="tpu_custom_call" | custom-call | tf_op jit(solution)/shard_map/state_update/pallas_call | solution.py:272
  46.4 4.2 %all-to-all-done.1 = bf16[32,8,1024]{2,1,0:T(8,128)(2,1)S(1)} async-done(((bf16[32,8,1024]{2,1,0:T(8,128)(2,1)}), bf16[32,8,1024]{2,1,0:T(8,128)(2,1)S(1)}, u32[]{:S(2)}, u32[]{:S(2)}) %all-to-all-start.1) | async-done | bytes 524320 | tf_op jit(solution)/shard_map/all_to_all | solution.py:347
  50.6 0.2 fusion.2
  50.8 0.2 fusion
  51.1 1.4 %collective-permute-start.1 = (bf16[128,256]{1,0:T(8,128)(2,1)S(1)}, bf16[128,256]{1,0:T(8,128)(2,1)S(1)}, u32[]{:S(2)}, u32[]{:S(2)}) collective-permute-start(bf16[128,256]{1,0:T(8,128)(2,1)S(1)} %fusion), channel_id=1, source_target_pairs={{0,2},{2,0},{4,6},{6,4},{1,3},{3,1},{5,7},{7,5},{8,10},{10,8},{12,... | collective-permute-start | bytes 196616 | tf_op jit(solution)/shard_map/ppermute | solution.py:297
  52.5 1.8 %collective-permute-done.1 = bf16[128,256]{1,0:T(8,128)(2,1)S(1)} collective-permute-done((bf16[128,256]{1,0:T(8,128)(2,1)S(1)}, bf16[128,256]{1,0:T(8,128)(2,1)S(1)}, u32[]{:S(2)}, u32[]{:S(2)}) %collective-permute-start.1) | collective-permute-done | bytes 65568 | tf_op jit(solution)/shard_map/ppermute | solution.py:297
  54.3 2.8 %collective-permute-start.2 = (bf16[128,256]{1,0:T(8,128)(2,1)S(1)}, bf16[128,256]{1,0:T(8,128)(2,1)S(1)}, u32[]{:S(2)}, u32[]{:S(2)}) collective-permute-start(bf16[128,256]{1,0:T(8,128)(2,1)S(1)} %add_convert_fusion.3), channel_id=1, source_target_pairs={{2,4},{4,2},{6,0},{0,6},{3,5},{5,3},{7,1},{1,7},{10,12},{12,10},{1... | collective-permute-start | bytes 196616 | tf_op jit(solution)/shard_map/ppermute | solution.py:297
  57.1 1.6 %collective-permute-done.2 = bf16[128,256]{1,0:T(8,128)(2,1)S(1)} collective-permute-done((bf16[128,256]{1,0:T(8,128)(2,1)S(1)}, bf16[128,256]{1,0:T(8,128)(2,1)S(1)}, u32[]{:S(2)}, u32[]{:S(2)}) %collective-permute-start.2) | collective-permute-done | bytes 65568 | tf_op jit(solution)/shard_map/ppermute | solution.py:297
  58.8 2.7 %collective-permute-start.3 = (bf16[16,1,8,256]{3,2,0,1:T(8,128)(2,1)S(1)}, bf16[16,1,8,256]{3,2,0,1:T(8,128)(2,1)S(1)}, u32[]{:S(2)}, u32[]{:S(2)}) collective-permute-start(bf16[16,1,8,256]{3,2,0,1:T(8,128)(2,1)S(1)} %fusion.11), channel_id=1, source_target_pairs={{0,1},{1,0},{2,3},{3,2},{4,5},{5,4},{6,7},{7,6},{8,9},{9,8},{10,11... | collective-permute-start | bytes 196616 | tf_op jit(solution)/shard_map/ppermute | solution.py:288
  61.5 0.9 collective-permute-done.3
  62.8 0.5 convolution_convert_fusion
  63.3 0.2 select_convert_fusion
  63.6 23.6 %all_to_all.21 = bf16[16,16,2816]{2,1,0:T(8,128)(2,1)S(1)} all-to-all(bf16[16,16,2816]{2,1,0:T(8,128)(2,1)S(1)} %bitcast.56), channel_id=1, replica_groups=mesh['z'=4,'x'=4,'y'=4,'c'=2] {'z','x'}, dimensions={0} | all-to-all | bytes 2883584 | tf_op jit(solution)/shard_map/all_to_all | solution.py:347
  87.3 0.2 convert_reduce_fusion
  87.5 0.2 fusion.15
  87.9 22.9 %all_to_all.22 = bf16[16,16,2688]{2,1,0:T(8,128)(2,1)S(1)} all-to-all(bf16[16,16,2688]{2,1,0:T(8,128)(2,1)S(1)} %broadcast_in_dim.65), channel_id=1, replica_groups=mesh['z'=4,'x'=4,'y'=4,'c'=2] {'z','x'}, dimensions={0} | all-to-all | bytes 2752512 | tf_op jit(solution)/shard_map/all_to_all | solution.py:347
  110.8 0.5 fusion.19
  111.4 2.1 %collective-permute-start.4 = (bf16[128,256]{1,0:T(8,128)(2,1)S(1)}, bf16[128,256]{1,0:T(8,128)(2,1)S(1)}, u32[]{:S(2)}, u32[]{:S(2)}) collective-permute-start(bf16[128,256]{1,0:T(8,128)(2,1)S(1)} %dynamic-slice_convert_fusion), channel_id=1, source_target_pairs={{0,1},{1,0},{2,3},{3,2},{4,5},{5,4},{6,7},{7,6},{8,9},{9,8},{10,11... | collective-permute-start | bytes 196616 | tf_op jit(solution)/shard_map/ppermute | solution.py:288
  113.5 0.9 collective-permute-done.4
  114.4 0.2 collective-permute-start.5
  114.6 3.0 %collective-permute-done.5 = bf16[128,256]{1,0:T(8,128)(2,1)S(1)} collective-permute-done((bf16[128,256]{1,0:T(8,128)(2,1)S(1)}, bf16[128,256]{1,0:T(8,128)(2,1)S(1)}, u32[]{:S(2)}, u32[]{:S(2)}) %collective-permute-start.5) | collective-permute-done | bytes 65568 | tf_op jit(solution)/shard_map/ppermute | solution.py:297
  117.6 2.8 %collective-permute-start.6 = (bf16[128,256]{1,0:T(8,128)(2,1)S(1)}, bf16[128,256]{1,0:T(8,128)(2,1)S(1)}, u32[]{:S(2)}, u32[]{:S(2)}) collective-permute-start(bf16[128,256]{1,0:T(8,128)(2,1)S(1)} %add_convert_fusion.1), channel_id=1, source_target_pairs={{2,4},{4,2},{6,0},{0,6},{3,5},{5,3},{7,1},{1,7},{10,12},{12,10},{1... | collective-permute-start | bytes 196616 | tf_op jit(solution)/shard_map/ppermute | solution.py:297
  120.4 1.7 %collective-permute-done.6 = bf16[128,256]{1,0:T(8,128)(2,1)S(1)} collective-permute-done((bf16[128,256]{1,0:T(8,128)(2,1)S(1)}, bf16[128,256]{1,0:T(8,128)(2,1)S(1)}, u32[]{:S(2)}, u32[]{:S(2)}) %collective-permute-start.6) | collective-permute-done | bytes 65568 | tf_op jit(solution)/shard_map/ppermute | solution.py:297
  122.1 2.7 %collective-permute-start.7 = (bf16[128,256]{1,0:T(8,128)(2,1)S(1)}, bf16[128,256]{1,0:T(8,128)(2,1)S(1)}, u32[]{:S(2)}, u32[]{:S(2)}) collective-permute-start(bf16[128,256]{1,0:T(8,128)(2,1)S(1)} %add_convert_fusion), channel_id=1, source_target_pairs={{0,1},{1,0},{2,3},{3,2},{4,5},{5,4},{6,7},{7,6},{8,9},{9,8},{10,11... | collective-permute-start | bytes 196616 | tf_op jit(solution)/shard_map/ppermute | solution.py:288
  124.8 0.9 collective-permute-done.7
  125.7 0.7 pad_maximum_fusion.2
  (63 shorter events, 0.9 us)
Async XLA Ops:
  0.6 62.1 %copy-start = (bf16[256,2688]{1,0:T(8,128)(2,1)S(1)}, bf16[256,2688]{1,0:T(8,128)(2,1)}, u32[]{:S(2)}) copy-start(bf16[256,2688]{1,0:T(8,128)(2,1)} %param.40) | copy-start | bytes 4128772
  0.6 1.7 %copy-start.2 = (bf16[256,256]{1,0:T(8,128)(2,1)S(1)}, bf16[256,256]{1,0:T(8,128)(2,1)}, u32[]{:S(2)}) copy-start(bf16[256,256]{1,0:T(8,128)(2,1)} %residual_ref.1) | copy-start | bytes 393220
  0.7 1.7 %copy-start.14 = (bf16[256,16]{0,1:T(8,128)(2,1)S(1)}, bf16[256,16]{0,1:T(8,128)(2,1)}, u32[]{:S(2)}) copy-start(bf16[256,16]{0,1:T(8,128)(2,1)} %param.29) | copy-start | bytes 24580
  0.7 1.7 %copy-start.13 = (bf16[256,2,128]{2,1,0:T(2,128)(2,1)S(1)}, bf16[256,2,128]{2,1,0:T(2,128)(2,1)}, u32[]{:S(2)}) copy-start(bf16[256,2,128]{2,1,0:T(2,128)(2,1)} %group_ref.1) | copy-start | bytes 393220
  0.7 1.7 %copy-start.15 = (f32[256]{0:T(256)S(1)}, f32[256]{0:T(256)}, u32[]{:S(2)}) copy-start(f32[256]{0:T(256)} %param.26) | copy-start | bytes 3076
  2.3 28.0 %slice-start = ((s8[8388608]{0:T(1024)(128)(4,1)}), s8[4194304]{0:T(1024)(128)(4,1)S(1)}, s32[]{:S(2)}) async-start(s8[8388608]{0:T(1024)(128)(4,1)} %bitcast.41), calls=%async_computation.4 | async-start | bytes 8388608
  2.4 28.0 %slice-start.1 = ((s8[8388608]{0:T(1024)(128)(4,1)}), s8[4194304]{0:T(1024)(128)(4,1)S(1)}, s32[]{:S(2)}) async-start(s8[8388608]{0:T(1024)(128)(4,1)} %bitcast.41), calls=%async_computation.5 | async-start | bytes 8388608
  3.2 27.1 %copy-start.1 = (f32[16,3,1024]{2,0,1:T(8,128)S(1)}, f32[16,3,1024]{2,0,1:T(8,128)}, u32[]{:S(2)}) copy-start(f32[16,3,1024]{2,0,1:T(8,128)} %param.24) | copy-start | bytes 589828
  3.3 27.1 %copy-start.3 = (f32[16,3,2,128]{3,2,1,0:T(2,128)S(1)}, f32[16,3,2,128]{3,2,1,0:T(2,128)}, u32[]{:S(2)}) copy-start(f32[16,3,2,128]{3,2,1,0:T(2,128)} %tail_group_ref.1) | copy-start | bytes 147460
  3.3 27.1 %copy-start.4 = (f32[4,1024]{1,0:T(4,128)S(1)}, f32[4,1024]{1,0:T(4,128)}, u32[]{:S(2)}) copy-start(f32[4,1024]{1,0:T(4,128)} %conv_mix_ref.1) | copy-start | bytes 49156
  3.3 27.1 %copy-start.5 = (f32[4,2,128]{2,1,0:T(2,128)S(1)}, f32[4,2,128]{2,1,0:T(2,128)}, u32[]{:S(2)}) copy-start(f32[4,2,128]{2,1,0:T(2,128)} %conv_group_ref.1) | copy-start | bytes 12292
  3.3 27.1 %copy-start.6 = (f32[1024]{0:T(1024)S(1)}, f32[1024]{0:T(1024)}, u32[]{:S(2)}) copy-start(f32[1024]{0:T(1024)} %param.32) | copy-start | bytes 12292
  3.3 27.1 %copy-start.7 = (f32[1024]{0:T(1024)S(1)}, f32[1024]{0:T(1024)}, u32[]{:S(2)}) copy-start(f32[1024]{0:T(1024)} %param.37) | copy-start | bytes 12292
  3.3 27.1 %copy-start.8 = (f32[2,128]{1,0:T(2,128)S(1)}, f32[2,128]{1,0:T(2,128)}, u32[]{:S(2)}) copy-start(f32[2,128]{1,0:T(2,128)} %bias_group_ref.1) | copy-start | bytes 3076
  3.3 27.0 %copy-start.9 = (s32[16]{0:T(128)S(1)}, s32[16]{0:T(128)}, u32[]{:S(2)}) copy-start(s32[16]{0:T(128)} %param.22) | copy-start | bytes 196
  3.3 27.0 %copy-start.10 = (f32[16]{0:T(128)S(1)}, f32[16]{0:T(128)}, u32[]{:S(2)}) copy-start(f32[16]{0:T(128)} %param.34) | copy-start | bytes 196
  3.3 27.0 %copy-start.11 = (f32[16]{0:T(128)S(1)}, f32[16]{0:T(128)}, u32[]{:S(2)}) copy-start(f32[16]{0:T(128)} %param.35) | copy-start | bytes 196
  3.4 27.0 %copy-start.12 = (f32[16]{0:T(128)S(1)}, f32[16]{0:T(128)}, u32[]{:S(2)}) copy-start(f32[16]{0:T(128)} %param.36) | copy-start | bytes 196
  30.4 8.6 %copy-start.17 = (bf16[1024,256]{1,0:T(8,128)(2,1)S(1)}, bf16[1024,256]{1,0:T(8,128)(2,1)}, u32[]{:S(2)}) copy-start(bf16[1024,256]{1,0:T(8,128)(2,1)} %param.38) | copy-start | bytes 1572868
  33.7 16.9 %all-to-all-start.1 = ((bf16[32,8,1024]{2,1,0:T(8,128)(2,1)}), bf16[32,8,1024]{2,1,0:T(8,128)(2,1)S(1)}, u32[]{:S(2)}, u32[]{:S(2)}) async-start(bf16[32,8,1024]{2,1,0:T(8,128)(2,1)} %bitcast.10), calls=%async_computation.1 | async-start | bytes 1048576 | tf_op jit(solution)/shard_map/all_to_all | solution.py:347
  39.1 11.8 %collective-permute-start = (bf16[1024,256]{1,0:T(8,128)(2,1)S(1)}, bf16[1024,256]{1,0:T(8,128)(2,1)S(1)}, u32[]{:S(2)}, u32[]{:S(2)}) collective-permute-start(bf16[1024,256]{1,0:T(8,128)(2,1)S(1)} %copy-done.17), channel_id=1, source_target_pairs={{0,1},{1,0},{2,3},{3,2},{4,5},{5,4},{6,7},{7,6},{8,9},{9,8},{10,11... | collective-permute-start | bytes 1572872 | tf_op jit(solution)/shard_map/ppermute | solution.py:288
  50.8 12.0 %copy-start.18 = (f32[256]{0:T(256)S(1)}, f32[256]{0:T(256)}, u32[]{:S(2)}) copy-start(f32[256]{0:T(256)} %param.39) | copy-start | bytes 3076
  51.1 3.2 %collective-permute-start.1 = (bf16[128,256]{1,0:T(8,128)(2,1)S(1)}, bf16[128,256]{1,0:T(8,128)(2,1)S(1)}, u32[]{:S(2)}, u32[]{:S(2)}) collective-permute-start(bf16[128,256]{1,0:T(8,128)(2,1)S(1)} %fusion), channel_id=1, source_target_pairs={{0,2},{2,0},{4,6},{6,4},{1,3},{3,1},{5,7},{7,5},{8,10},{10,8},{12,... | collective-permute-start | bytes 196616 | tf_op jit(solution)/shard_map/ppermute | solution.py:297
  54.3 4.5 %collective-permute-start.2 = (bf16[128,256]{1,0:T(8,128)(2,1)S(1)}, bf16[128,256]{1,0:T(8,128)(2,1)S(1)}, u32[]{:S(2)}, u32[]{:S(2)}) collective-permute-start(bf16[128,256]{1,0:T(8,128)(2,1)S(1)} %add_convert_fusion.3), channel_id=1, source_target_pairs={{2,4},{4,2},{6,0},{0,6},{3,5},{5,3},{7,1},{1,7},{10,12},{12,10},{1... | collective-permute-start | bytes 196616 | tf_op jit(solution)/shard_map/ppermute | solution.py:297
  58.8 3.6 %collective-permute-start.3 = (bf16[16,1,8,256]{3,2,0,1:T(8,128)(2,1)S(1)}, bf16[16,1,8,256]{3,2,0,1:T(8,128)(2,1)S(1)}, u32[]{:S(2)}, u32[]{:S(2)}) collective-permute-start(bf16[16,1,8,256]{3,2,0,1:T(8,128)(2,1)S(1)} %fusion.11), channel_id=1, source_target_pairs={{0,1},{1,0},{2,3},{3,2},{4,5},{5,4},{6,7},{7,6},{8,9},{9,8},{10,11... | collective-permute-start | bytes 196616 | tf_op jit(solution)/shard_map/ppermute | solution.py:288
  87.9 22.9 %copy-start.16 = (bf16[2688,256]{1,0:T(8,128)(2,1)S(1)}, bf16[2688,256]{1,0:T(8,128)(2,1)}, u32[]{:S(2)}) copy-start(bf16[2688,256]{1,0:T(8,128)(2,1)} %param.41) | copy-start | bytes 4128772
  111.4 3.0 %collective-permute-start.4 = (bf16[128,256]{1,0:T(8,128)(2,1)S(1)}, bf16[128,256]{1,0:T(8,128)(2,1)S(1)}, u32[]{:S(2)}, u32[]{:S(2)}) collective-permute-start(bf16[128,256]{1,0:T(8,128)(2,1)S(1)} %dynamic-slice_convert_fusion), channel_id=1, source_target_pairs={{0,1},{1,0},{2,3},{3,2},{4,5},{5,4},{6,7},{7,6},{8,9},{9,8},{10,11... | collective-permute-start | bytes 196616 | tf_op jit(solution)/shard_map/ppermute | solution.py:288
  114.4 3.2 %collective-permute-start.5 = (bf16[128,256]{1,0:T(8,128)(2,1)S(1)}, bf16[128,256]{1,0:T(8,128)(2,1)S(1)}, u32[]{:S(2)}, u32[]{:S(2)}) collective-permute-start(bf16[128,256]{1,0:T(8,128)(2,1)S(1)} %add_convert_fusion.2), channel_id=1, source_target_pairs={{0,2},{2,0},{4,6},{6,4},{1,3},{3,1},{5,7},{7,5},{8,10},{10,8},{12,... | collective-permute-start | bytes 196616 | tf_op jit(solution)/shard_map/ppermute | solution.py:297
  117.6 4.5 %collective-permute-start.6 = (bf16[128,256]{1,0:T(8,128)(2,1)S(1)}, bf16[128,256]{1,0:T(8,128)(2,1)S(1)}, u32[]{:S(2)}, u32[]{:S(2)}) collective-permute-start(bf16[128,256]{1,0:T(8,128)(2,1)S(1)} %add_convert_fusion.1), channel_id=1, source_target_pairs={{2,4},{4,2},{6,0},{0,6},{3,5},{5,3},{7,1},{1,7},{10,12},{12,10},{1... | collective-permute-start | bytes 196616 | tf_op jit(solution)/shard_map/ppermute | solution.py:297
  122.1 3.6 %collective-permute-start.7 = (bf16[128,256]{1,0:T(8,128)(2,1)S(1)}, bf16[128,256]{1,0:T(8,128)(2,1)S(1)}, u32[]{:S(2)}, u32[]{:S(2)}) collective-permute-start(bf16[128,256]{1,0:T(8,128)(2,1)S(1)} %add_convert_fusion), channel_id=1, source_target_pairs={{0,1},{1,0},{2,3},{3,2},{4,5},{5,4},{6,7},{7,6},{8,9},{9,8},{10,11... | collective-permute-start | bytes 196616 | tf_op jit(solution)/shard_map/ppermute | solution.py:288

commit v8 on v7

--- a/solution.py
+++ b/solution.py
@@ -10,7 +10,7 @@
 HEAD = ("y", "c")
 LANES = 128
 BATCH = 8
-ON_MXU = 3
+ON_MXU = 5
 IN_VMEM = pl.BlockSpec(memory_space=pltpu.VMEM)
 SMALL = pltpu.CompilerParams(vmem_limit_bytes=16 * 2**20)
 f32 = jnp.float32
@@ -162,11 +162,8 @@
                 if k >= ON_MXU:
                     others.append((r, c_ref[pl.ds(r, 1), :]))
                     continue
-                s = state_ref[r].reshape(mix, state)
-                s_high = s.astype(bf16)
-                left += [s_high, (s - s_high.astype(f32)).astype(bf16)]
-                own = jnp.where(lane % rows == r, columns_ref[...], 0.0).astype(bf16)
-                right += [own, own]
+                left.append(state_ref[r].reshape(mix, state).astype(bf16))
+                right.append(jnp.where(lane % rows == r, columns_ref[...], 0.0).astype(bf16))
             read_ref[...] += jnp.dot(
                 jnp.concatenate(left, axis=1), jnp.concatenate(right, axis=0), preferred_element_type=f32
             )

time: 127 us -> 126 us (level)
  no operation moved by 1% of the time
where the time goes in v8:
time: 126 us
  blocking collectives  73.5 us (58%)
  starting transfers between devices  20.4 us (16%)
  waiting for transfers between devices  15.1 us (12%)
  Pallas kernels  10.5 us (8%)
  local copies, waits for them, and re-layouts  1.96 us (2%)
  other arithmetic  1.75 us (1%)
  matrix products  1.56 us (1%)
    all_to_all x3, blocking collectives, exchange(): return lax.all_to_all(value, axis, 0, 0, tiled=True)  73.5 us
    ppermute x4, waiting for transfers between devices, ring_pairs(): return lax.ppermute(value, 'y', pairs)  8.17 us
    ppermute x4, starting transfers between devices, swap_core(): return lax.ppermute(value, 'c', [(0, 1), (1, 0)])  7.94 us
    ppermute x4, starting transfers between devices, ring_pairs(): return lax.ppermute(value, 'y', pairs)  7.17 us
    pallas_call x1, Pallas kernels, state_update(): pl.pallas_call(make_update_kernel(rows, heads, head_dim, state), in_specs...  6.91 us
    all_to_all x1, starting transfers between devices, exchange(): return lax.all_to_all(value, axis, 0, 0, tiled=True)  5.31 us
    all_to_all x1, waiting for transfers between devices, exchange(): return lax.all_to_all(value, axis, 0, 0, tiled=True)  4.19 us
    pallas_call x1, Pallas kernels, mixer_step(): pl.pallas_call(make_mixer_kernel(width_all, (pieces, rows, heads, head_di...  2.72 us
  transfers between devices with their start and end apart: 9, of which 8 were waited for; matrix products, arithmetic and copies ran while one was open for 0% of the time, Pallas kernels for 5%

profile of v8, /device:TPU:1, one launch (start us, length us, event | category | flops | bytes accessed | tf_op | source)
XLA Modules:
  0.0 125.8 jit_solution(5295290207007790976)
XLA Ops:
  0.7 1.6 %copy.38 = bf16[32,8,2,1024]{3,1,2,0:T(8,128)(2,1)S(1)} copy(bf16[32,8,2,1024]{3,2,1,0:T(2,128)(2,1)} %bitcast.60) | data formatting | bytes 2097152
  2.4 0.9 input_projection.1
  3.4 26.9 %all_to_all.20.arrived_ref = bf16[16,16,2432]{2,1,0:T(8,128)(2,1)S(1)} all-to-all(bf16[16,16,2432]{2,1,0:T(8,128)(2,1)S(1)} %bitcast.43), channel_id=1, replica_groups=mesh['z'=4,'x'=4,'y'=4,'c'=2] {'z','x'}, dimensions={0} | all-to-all | bytes 2490368 | tf_op jit(solution)/shard_map/all_to_all | solution.py:344
  30.4 2.7 %mixer_step.1 = (bf16[16,16,1024]{2,1,0:T(8,128)(2,1)}, f32[3,16,1024]{2,1,0:T(8,128)}, f32[16,3,2,128]{3,2,1,0:T(2,128)}, f32[8,16,128]{2,1,0:T(8,128)S(1)}, f3...) custom-call(bf16[16,16,2432]{2,1,0:T(8,128)(2,1)S(1)} %all_to_all.20.arrived_ref, s32[1,16]{1,0:T(1,128)S(1)} %bitcast.50, ...), custom_call_target="tpu_custom_call" | custom-call | tf_op jit(solution)/shard_map/mixer_step/pallas_call | solution.py:212
  33.1 5.3 %all-to-all-start.1 = ((bf16[32,8,1024]{2,1,0:T(8,128)(2,1)}), bf16[32,8,1024]{2,1,0:T(8,128)(2,1)S(1)}, u32[]{:S(2)}, u32[]{:S(2)}) async-start(bf16[32,8,1024]{2,1,0:T(8,128)(2,1)} %bitcast.10), calls=%async_computation.1 | async-start | bytes 1048576 | tf_op jit(solution)/shard_map/all_to_all | solution.py:344
  38.5 0.4 collective-permute-start
  38.9 6.9 %state_update.1 = f32[16,16,64,128]{3,2,1,0:T(8,128)} custom-call(f32[8,16,128]{2,1,0:T(8,128)S(1)} %get-tuple-element.16.u_ref, f32[16,128]{1,0:T(8,128)S(1)} %get-tuple-element.17.decay_ref, f32[16,128]{1,0:T(8,128)S(1)} %get-tuple-element.18.b_ref, f32[16,16,64,128]{3,2,1,0:T(8,128)} %state_ref.3), custom_call_target="tpu_custom_call" | custom-call | tf_op jit(solution)/shard_map/state_update/pallas_call | solution.py:269
  45.8 4.2 %all-to-all-done.1 = bf16[32,8,1024]{2,1,0:T(8,128)(2,1)S(1)} async-done(((bf16[32,8,1024]{2,1,0:T(8,128)(2,1)}), bf16[32,8,1024]{2,1,0:T(8,128)(2,1)S(1)}, u32[]{:S(2)}, u32[]{:S(2)}) %all-to-all-start.1) | async-done | bytes 524320 | tf_op jit(solution)/shard_map/all_to_all | solution.py:344
  50.0 0.2 fusion.2
  50.3 0.2 fusion
  50.5 1.4 %collective-permute-start.1 = (bf16[128,256]{1,0:T(8,128)(2,1)S(1)}, bf16[128,256]{1,0:T(8,128)(2,1)S(1)}, u32[]{:S(2)}, u32[]{:S(2)}) collective-permute-start(bf16[128,256]{1,0:T(8,128)(2,1)S(1)} %fusion), channel_id=1, source_target_pairs={{0,2},{2,0},{4,6},{6,4},{1,3},{3,1},{5,7},{7,5},{8,10},{10,8},{12,... | collective-permute-start | bytes 196616 | tf_op jit(solution)/shard_map/ppermute | solution.py:294
  51.9 1.8 %collective-permute-done.1 = bf16[128,256]{1,0:T(8,128)(2,1)S(1)} collective-permute-done((bf16[128,256]{1,0:T(8,128)(2,1)S(1)}, bf16[128,256]{1,0:T(8,128)(2,1)S(1)}, u32[]{:S(2)}, u32[]{:S(2)}) %collective-permute-start.1) | collective-permute-done | bytes 65568 | tf_op jit(solution)/shard_map/ppermute | solution.py:294
  53.7 2.8 %collective-permute-start.2 = (bf16[128,256]{1,0:T(8,128)(2,1)S(1)}, bf16[128,256]{1,0:T(8,128)(2,1)S(1)}, u32[]{:S(2)}, u32[]{:S(2)}) collective-permute-start(bf16[128,256]{1,0:T(8,128)(2,1)S(1)} %add_convert_fusion.3), channel_id=1, source_target_pairs={{2,4},{4,2},{6,0},{0,6},{3,5},{5,3},{7,1},{1,7},{10,12},{12,10},{1... | collective-permute-start | bytes 196616 | tf_op jit(solution)/shard_map/ppermute | solution.py:294
  56.6 1.6 %collective-permute-done.2 = bf16[128,256]{1,0:T(8,128)(2,1)S(1)} collective-permute-done((bf16[128,256]{1,0:T(8,128)(2,1)S(1)}, bf16[128,256]{1,0:T(8,128)(2,1)S(1)}, u32[]{:S(2)}, u32[]{:S(2)}) %collective-permute-start.2) | collective-permute-done | bytes 65568 | tf_op jit(solution)/shard_map/ppermute | solution.py:294
  58.2 2.7 %collective-permute-start.3 = (bf16[16,1,8,256]{3,2,0,1:T(8,128)(2,1)S(1)}, bf16[16,1,8,256]{3,2,0,1:T(8,128)(2,1)S(1)}, u32[]{:S(2)}, u32[]{:S(2)}) collective-permute-start(bf16[16,1,8,256]{3,2,0,1:T(8,128)(2,1)S(1)} %fusion.11), channel_id=1, source_target_pairs={{0,1},{1,0},{2,3},{3,2},{4,5},{5,4},{6,7},{7,6},{8,9},{9,8},{10,11... | collective-permute-start | bytes 196616 | tf_op jit(solution)/shard_map/ppermute | solution.py:285
  61.0 0.9 collective-permute-done.3
  62.2 0.5 convolution_convert_fusion
  62.8 0.2 select_convert_fusion
  63.1 23.6 %all_to_all.21 = bf16[16,16,2816]{2,1,0:T(8,128)(2,1)S(1)} all-to-all(bf16[16,16,2816]{2,1,0:T(8,128)(2,1)S(1)} %bitcast.56), channel_id=1, replica_groups=mesh['z'=4,'x'=4,'y'=4,'c'=2] {'z','x'}, dimensions={0} | all-to-all | bytes 2883584 | tf_op jit(solution)/shard_map/all_to_all | solution.py:344
  86.7 0.2 convert_reduce_fusion
  86.9 0.2 fusion.15
  87.3 22.9 %all_to_all.22 = bf16[16,16,2688]{2,1,0:T(8,128)(2,1)S(1)} all-to-all(bf16[16,16,2688]{2,1,0:T(8,128)(2,1)S(1)} %broadcast_in_dim.65), channel_id=1, replica_groups=mesh['z'=4,'x'=4,'y'=4,'c'=2] {'z','x'}, dimensions={0} | all-to-all | bytes 2752512 | tf_op jit(solution)/shard_map/all_to_all | solution.py:344
  110.2 0.5 fusion.19
  110.8 2.1 %collective-permute-start.4 = (bf16[128,256]{1,0:T(8,128)(2,1)S(1)}, bf16[128,256]{1,0:T(8,128)(2,1)S(1)}, u32[]{:S(2)}, u32[]{:S(2)}) collective-permute-start(bf16[128,256]{1,0:T(8,128)(2,1)S(1)} %dynamic-slice_convert_fusion), channel_id=1, source_target_pairs={{0,1},{1,0},{2,3},{3,2},{4,5},{5,4},{6,7},{7,6},{8,9},{9,8},{10,11... | collective-permute-start | bytes 196616 | tf_op jit(solution)/shard_map/ppermute | solution.py:285
  112.9 0.9 collective-permute-done.4
  113.8 0.2 collective-permute-start.5
  114.0 3.0 %collective-permute-done.5 = bf16[128,256]{1,0:T(8,128)(2,1)S(1)} collective-permute-done((bf16[128,256]{1,0:T(8,128)(2,1)S(1)}, bf16[128,256]{1,0:T(8,128)(2,1)S(1)}, u32[]{:S(2)}, u32[]{:S(2)}) %collective-permute-start.5) | collective-permute-done | bytes 65568 | tf_op jit(solution)/shard_map/ppermute | solution.py:294
  117.1 2.8 %collective-permute-start.6 = (bf16[128,256]{1,0:T(8,128)(2,1)S(1)}, bf16[128,256]{1,0:T(8,128)(2,1)S(1)}, u32[]{:S(2)}, u32[]{:S(2)}) collective-permute-start(bf16[128,256]{1,0:T(8,128)(2,1)S(1)} %add_convert_fusion.1), channel_id=1, source_target_pairs={{2,4},{4,2},{6,0},{0,6},{3,5},{5,3},{7,1},{1,7},{10,12},{12,10},{1... | collective-permute-start | bytes 196616 | tf_op jit(solution)/shard_map/ppermute | solution.py:294
  119.9 1.7 %collective-permute-done.6 = bf16[128,256]{1,0:T(8,128)(2,1)S(1)} collective-permute-done((bf16[128,256]{1,0:T(8,128)(2,1)S(1)}, bf16[128,256]{1,0:T(8,128)(2,1)S(1)}, u32[]{:S(2)}, u32[]{:S(2)}) %collective-permute-start.6) | collective-permute-done | bytes 65568 | tf_op jit(solution)/shard_map/ppermute | solution.py:294
  121.6 2.7 %collective-permute-start.7 = (bf16[128,256]{1,0:T(8,128)(2,1)S(1)}, bf16[128,256]{1,0:T(8,128)(2,1)S(1)}, u32[]{:S(2)}, u32[]{:S(2)}) collective-permute-start(bf16[128,256]{1,0:T(8,128)(2,1)S(1)} %add_convert_fusion), channel_id=1, source_target_pairs={{0,1},{1,0},{2,3},{3,2},{4,5},{5,4},{6,7},{7,6},{8,9},{9,8},{10,11... | collective-permute-start | bytes 196616 | tf_op jit(solution)/shard_map/ppermute | solution.py:285
  124.2 0.9 collective-permute-done.7
  125.2 0.7 pad_maximum_fusion.2
  (63 shorter events, 0.9 us)
Async XLA Ops:
  0.6 61.6 %copy-start = (bf16[256,2688]{1,0:T(8,128)(2,1)S(1)}, bf16[256,2688]{1,0:T(8,128)(2,1)}, u32[]{:S(2)}) copy-start(bf16[256,2688]{1,0:T(8,128)(2,1)} %param.40) | copy-start | bytes 4128772
  0.6 1.7 %copy-start.2 = (bf16[256,256]{1,0:T(8,128)(2,1)S(1)}, bf16[256,256]{1,0:T(8,128)(2,1)}, u32[]{:S(2)}) copy-start(bf16[256,256]{1,0:T(8,128)(2,1)} %residual_ref.1) | copy-start | bytes 393220
  0.7 1.7 %copy-start.14 = (bf16[256,16]{0,1:T(8,128)(2,1)S(1)}, bf16[256,16]{0,1:T(8,128)(2,1)}, u32[]{:S(2)}) copy-start(bf16[256,16]{0,1:T(8,128)(2,1)} %param.29) | copy-start | bytes 24580
  0.7 1.7 %copy-start.13 = (bf16[256,2,128]{2,1,0:T(2,128)(2,1)S(1)}, bf16[256,2,128]{2,1,0:T(2,128)(2,1)}, u32[]{:S(2)}) copy-start(bf16[256,2,128]{2,1,0:T(2,128)(2,1)} %group_ref.1) | copy-start | bytes 393220
  0.7 1.7 %copy-start.15 = (f32[256]{0:T(256)S(1)}, f32[256]{0:T(256)}, u32[]{:S(2)}) copy-start(f32[256]{0:T(256)} %param.26) | copy-start | bytes 3076
  2.3 28.0 %slice-start = ((s8[8388608]{0:T(1024)(128)(4,1)}), s8[4194304]{0:T(1024)(128)(4,1)S(1)}, s32[]{:S(2)}) async-start(s8[8388608]{0:T(1024)(128)(4,1)} %bitcast.41), calls=%async_computation.4 | async-start | bytes 8388608
  2.4 28.0 %slice-start.1 = ((s8[8388608]{0:T(1024)(128)(4,1)}), s8[4194304]{0:T(1024)(128)(4,1)S(1)}, s32[]{:S(2)}) async-start(s8[8388608]{0:T(1024)(128)(4,1)} %bitcast.41), calls=%async_computation.5 | async-start | bytes 8388608
  3.2 27.1 %copy-start.1 = (f32[16,3,1024]{2,0,1:T(8,128)S(1)}, f32[16,3,1024]{2,0,1:T(8,128)}, u32[]{:S(2)}) copy-start(f32[16,3,1024]{2,0,1:T(8,128)} %param.24) | copy-start | bytes 589828
  3.3 27.1 %copy-start.3 = (f32[16,3,2,128]{3,2,1,0:T(2,128)S(1)}, f32[16,3,2,128]{3,2,1,0:T(2,128)}, u32[]{:S(2)}) copy-start(f32[16,3,2,128]{3,2,1,0:T(2,128)} %tail_group_ref.1) | copy-start | bytes 147460
  3.3 27.1 %copy-start.4 = (f32[4,1024]{1,0:T(4,128)S(1)}, f32[4,1024]{1,0:T(4,128)}, u32[]{:S(2)}) copy-start(f32[4,1024]{1,0:T(4,128)} %conv_mix_ref.1) | copy-start | bytes 49156
  3.3 27.1 %copy-start.5 = (f32[4,2,128]{2,1,0:T(2,128)S(1)}, f32[4,2,128]{2,1,0:T(2,128)}, u32[]{:S(2)}) copy-start(f32[4,2,128]{2,1,0:T(2,128)} %conv_group_ref.1) | copy-start | bytes 12292
  3.3 27.1 %copy-start.6 = (f32[1024]{0:T(1024)S(1)}, f32[1024]{0:T(1024)}, u32[]{:S(2)}) copy-start(f32[1024]{0:T(1024)} %param.32) | copy-start | bytes 12292
  3.3 27.1 %copy-start.7 = (f32[1024]{0:T(1024)S(1)}, f32[1024]{0:T(1024)}, u32[]{:S(2)}) copy-start(f32[1024]{0:T(1024)} %param.37) | copy-start | bytes 12292
  3.3 27.1 %copy-start.8 = (f32[2,128]{1,0:T(2,128)S(1)}, f32[2,128]{1,0:T(2,128)}, u32[]{:S(2)}) copy-start(f32[2,128]{1,0:T(2,128)} %bias_group_ref.1) | copy-start | bytes 3076
  3.3 27.0 %copy-start.9 = (s32[16]{0:T(128)S(1)}, s32[16]{0:T(128)}, u32[]{:S(2)}) copy-start(s32[16]{0:T(128)} %param.22) | copy-start | bytes 196
  3.3 27.0 %copy-start.10 = (f32[16]{0:T(128)S(1)}, f32[16]{0:T(128)}, u32[]{:S(2)}) copy-start(f32[16]{0:T(128)} %param.34) | copy-start | bytes 196
  3.3 27.0 %copy-start.11 = (f32[16]{0:T(128)S(1)}, f32[16]{0:T(128)}, u32[]{:S(2)}) copy-start(f32[16]{0:T(128)} %param.35) | copy-start | bytes 196
  3.4 27.0 %copy-start.12 = (f32[16]{0:T(128)S(1)}, f32[16]{0:T(128)}, u32[]{:S(2)}) copy-start(f32[16]{0:T(128)} %param.36) | copy-start | bytes 196
  30.4 8.1 %copy-start.17 = (bf16[1024,256]{1,0:T(8,128)(2,1)S(1)}, bf16[1024,256]{1,0:T(8,128)(2,1)}, u32[]{:S(2)}) copy-start(bf16[1024,256]{1,0:T(8,128)(2,1)} %param.38) | copy-start | bytes 1572868
  33.1 16.9 %all-to-all-start.1 = ((bf16[32,8,1024]{2,1,0:T(8,128)(2,1)}), bf16[32,8,1024]{2,1,0:T(8,128)(2,1)S(1)}, u32[]{:S(2)}, u32[]{:S(2)}) async-start(bf16[32,8,1024]{2,1,0:T(8,128)(2,1)} %bitcast.10), calls=%async_computation.1 | async-start | bytes 1048576 | tf_op jit(solution)/shard_map/all_to_all | solution.py:344
  38.5 11.8 %collective-permute-start = (bf16[1024,256]{1,0:T(8,128)(2,1)S(1)}, bf16[1024,256]{1,0:T(8,128)(2,1)S(1)}, u32[]{:S(2)}, u32[]{:S(2)}) collective-permute-start(bf16[1024,256]{1,0:T(8,128)(2,1)S(1)} %copy-done.17), channel_id=1, source_target_pairs={{0,1},{1,0},{2,3},{3,2},{4,5},{5,4},{6,7},{7,6},{8,9},{9,8},{10,11... | collective-permute-start | bytes 1572872 | tf_op jit(solution)/shard_map/ppermute | solution.py:285
  50.3 12.0 %copy-start.18 = (f32[256]{0:T(256)S(1)}, f32[256]{0:T(256)}, u32[]{:S(2)}) copy-start(f32[256]{0:T(256)} %param.39) | copy-start | bytes 3076
  50.5 3.2 %collective-permute-start.1 = (bf16[128,256]{1,0:T(8,128)(2,1)S(1)}, bf16[128,256]{1,0:T(8,128)(2,1)S(1)}, u32[]{:S(2)}, u32[]{:S(2)}) collective-permute-start(bf16[128,256]{1,0:T(8,128)(2,1)S(1)} %fusion), channel_id=1, source_target_pairs={{0,2},{2,0},{4,6},{6,4},{1,3},{3,1},{5,7},{7,5},{8,10},{10,8},{12,... | collective-permute-start | bytes 196616 | tf_op jit(solution)/shard_map/ppermute | solution.py:294
  53.7 4.5 %collective-permute-start.2 = (bf16[128,256]{1,0:T(8,128)(2,1)S(1)}, bf16[128,256]{1,0:T(8,128)(2,1)S(1)}, u32[]{:S(2)}, u32[]{:S(2)}) collective-permute-start(bf16[128,256]{1,0:T(8,128)(2,1)S(1)} %add_convert_fusion.3), channel_id=1, source_target_pairs={{2,4},{4,2},{6,0},{0,6},{3,5},{5,3},{7,1},{1,7},{10,12},{12,10},{1... | collective-permute-start | bytes 196616 | tf_op jit(solution)/shard_map/ppermute | solution.py:294
  58.2 3.6 %collective-permute-start.3 = (bf16[16,1,8,256]{3,2,0,1:T(8,128)(2,1)S(1)}, bf16[16,1,8,256]{3,2,0,1:T(8,128)(2,1)S(1)}, u32[]{:S(2)}, u32[]{:S(2)}) collective-permute-start(bf16[16,1,8,256]{3,2,0,1:T(8,128)(2,1)S(1)} %fusion.11), channel_id=1, source_target_pairs={{0,1},{1,0},{2,3},{3,2},{4,5},{5,4},{6,7},{7,6},{8,9},{9,8},{10,11... | collective-permute-start | bytes 196616 | tf_op jit(solution)/shard_map/ppermute | solution.py:285
  87.3 22.9 %copy-start.16 = (bf16[2688,256]{1,0:T(8,128)(2,1)S(1)}, bf16[2688,256]{1,0:T(8,128)(2,1)}, u32[]{:S(2)}) copy-start(bf16[2688,256]{1,0:T(8,128)(2,1)} %param.41) | copy-start | bytes 4128772
  110.8 3.0 %collective-permute-start.4 = (bf16[128,256]{1,0:T(8,128)(2,1)S(1)}, bf16[128,256]{1,0:T(8,128)(2,1)S(1)}, u32[]{:S(2)}, u32[]{:S(2)}) collective-permute-start(bf16[128,256]{1,0:T(8,128)(2,1)S(1)} %dynamic-slice_convert_fusion), channel_id=1, source_target_pairs={{0,1},{1,0},{2,3},{3,2},{4,5},{5,4},{6,7},{7,6},{8,9},{9,8},{10,11... | collective-permute-start | bytes 196616 | tf_op jit(solution)/shard_map/ppermute | solution.py:285
  113.8 3.2 %collective-permute-start.5 = (bf16[128,256]{1,0:T(8,128)(2,1)S(1)}, bf16[128,256]{1,0:T(8,128)(2,1)S(1)}, u32[]{:S(2)}, u32[]{:S(2)}) collective-permute-start(bf16[128,256]{1,0:T(8,128)(2,1)S(1)} %add_convert_fusion.2), channel_id=1, source_target_pairs={{0,2},{2,0},{4,6},{6,4},{1,3},{3,1},{5,7},{7,5},{8,10},{10,8},{12,... | collective-permute-start | bytes 196616 | tf_op jit(solution)/shard_map/ppermute | solution.py:294
  117.1 4.5 %collective-permute-start.6 = (bf16[128,256]{1,0:T(8,128)(2,1)S(1)}, bf16[128,256]{1,0:T(8,128)(2,1)S(1)}, u32[]{:S(2)}, u32[]{:S(2)}) collective-permute-start(bf16[128,256]{1,0:T(8,128)(2,1)S(1)} %add_convert_fusion.1), channel_id=1, source_target_pairs={{2,4},{4,2},{6,0},{0,6},{3,5},{5,3},{7,1},{1,7},{10,12},{12,10},{1... | collective-permute-start | bytes 196616 | tf_op jit(solution)/shard_map/ppermute | solution.py:294
  121.6 3.6 %collective-permute-start.7 = (bf16[128,256]{1,0:T(8,128)(2,1)S(1)}, bf16[128,256]{1,0:T(8,128)(2,1)S(1)}, u32[]{:S(2)}, u32[]{:S(2)}) collective-permute-start(bf16[128,256]{1,0:T(8,128)(2,1)S(1)} %add_convert_fusion), channel_id=1, source_target_pairs={{0,1},{1,0},{2,3},{3,2},{4,5},{5,4},{6,7},{7,6},{8,9},{9,8},{10,11... | collective-permute-start | bytes 196616 | tf_op jit(solution)/shard_map/ppermute | solution.py:285
